TPU v7x, 32 devices: a whole 2x2x4 slice. The times are simulated.
32 devices in a mesh: grp: 2 (over y), res: 4 (over z), seq: 2 (over x), head: 2 (over core).
Axes of the slice: x: 2, y: 2, z: 4, core: 2. Of those that a mesh axis runs over, the one named last changes fastest.
Arguments:
- tokens: bfloat16 [24, 512, 768], P(('grp', 'seq'), 'res'), parts along dimension 0, may hold values from -20 to 20
- weights: int32 [24], P(('grp', 'seq')), parts along dimension 0, may hold values from 3 to 17
- key_mask: int32 [1024], P(('grp', 'res')), parts along dimension 0, may hold values 0 or 1
- w_query: bfloat16 [768, 768], P(None, 'head'), may hold values from -0.21875 to 0.21875
- w_key: bfloat16 [768, 768], P(None, 'head'), may hold values from -0.21875 to 0.21875
- w_value: bfloat16 [768, 768], P(None, 'head'), may hold values from -0.21875 to 0.21875
- w_out: bfloat16 [768, 768], P('head'), may hold values from -0.21875 to 0.21875
Outputs:
- attention_out: bfloat16 [24, 512, 768], P(('grp', 'seq'), 'res', 'head'), parts along dimension 0
There are 2 independent parts, one for each index of `grp`. A program takes and returns all parts, laid end to end along the dimension named above; an argument that names none is the same for every part. Nothing has to cross between parts.
All inputs are finite; a program needn't handle non-finite values. No bound on the sum of `key_mask` on one device may be relied on, other than what follows from the above.
Results may differ from a plain program's by a relative error of at most 0.011.
The roundings to bfloat16 on the way count: a program that leaves them out, or rounds other values in their place, can miss the bound.
Values may be sent and summed in bfloat16 or wider, within the bound.
No kernel may reach another device: no remote copies, remote signals or barrier semaphores. Data moves between devices by JAX's collectives and lax.ppermute only.
A program may use at most 64 MiB of HBM per device.

v0:
```python
import math

import jax
import jax.numpy as jnp
from jax import lax
from jax.sharding import PartitionSpec as P

HEAD_DIM = 64


def from_behind(value, axis, by):
    length = lax.axis_size(axis)
    return lax.ppermute(value, axis, [(i, (i + by) % length) for i in range(length)])


def shards(tokens, weights, key_mask, w_query, w_key, w_value, w_out):
    rows, cells, width = tokens.shape
    head_count = w_query.shape[1] // HEAD_DIM
    flat = tokens.reshape(rows * cells, width)
    total = lax.psum(jnp.sum(weights).astype(jnp.float32), "seq")
    factor = weights.astype(jnp.float32) * lax.rsqrt(total) / math.sqrt(HEAD_DIM)
    query = jnp.dot(flat, w_query, preferred_element_type=jnp.float32).reshape(
        rows, cells, head_count, HEAD_DIM
    )
    query = (query * factor[:, None, None, None]).astype(jnp.bfloat16)
    keys = (
        jnp.dot(flat, w_key, preferred_element_type=jnp.float32)
        .astype(jnp.bfloat16)
        .reshape(rows, cells, head_count, HEAD_DIM)
    )
    values = (
        jnp.dot(flat, w_value, preferred_element_type=jnp.float32)
        .astype(jnp.bfloat16)
        .reshape(rows, cells, head_count, HEAD_DIM)
    )
    kv_pair = jnp.stack([keys, values])
    mask_all = lax.all_gather(key_mask, "res", axis=0, tiled=True)
    cycle_size = lax.axis_size("res")
    position = lax.axis_index("res")
    seq_size = lax.axis_size("seq")

    def block_mask(offset, count):
        source = (position - offset) % cycle_size
        live = lax.dynamic_slice_in_dim(mask_all, source * cells, cells) > 0
        return jnp.broadcast_to(live[None, :], (count, cells))

    def scores(q_part, k_part):
        return jnp.einsum("rihe,rjhe->hij", q_part, k_part, preferred_element_type=jnp.float32)

    def mixes(p_part, v_part):
        return jnp.einsum("hij,rjhe->rihe", p_part, v_part, preferred_element_type=jnp.float32)

    def partial_tiles(streams, step):
        tiles = scores(query, streams[0][0])
        masks = block_mask(step, head_count)
        return (tiles, masks)

    def weighted(probs, streams):
        return mixes(probs, streams[0][1])

    def consume(carry, step):
        streams, top, denom, accum = carry
        tiles, masks = partial_tiles(streams, step)
        summed = lax.psum_scatter(tiles, "seq", scatter_dimension=1, tiled=True)
        summed = jnp.where(masks[:, None, :], summed, -1000000000.0)
        new_top = jnp.maximum(top, jnp.max(summed, axis=-1))
        rescale = jnp.exp(top - new_top)
        expo = jnp.exp(summed - new_top[:, :, None])
        denom = denom * rescale + jnp.sum(expo, axis=-1)
        probs = expo.astype(jnp.bfloat16)
        probs = lax.all_gather(probs, "seq", axis=1, tiled=True)
        rescale = lax.all_gather(rescale, "seq", axis=1, tiled=True)
        accum = accum * jnp.transpose(rescale)[None, :, :, None] + weighted(probs, streams)
        return (streams, new_top, denom, accum)

    streams = (kv_pair,)
    query_rows = cells // seq_size
    top = jnp.full((head_count, query_rows), -1e30, jnp.float32)
    denom = jnp.zeros((head_count, query_rows), jnp.float32)
    accum = jnp.zeros((rows, cells, head_count, HEAD_DIM), jnp.float32)
    carry = consume((streams, top, denom, accum), 0)

    def cycle_step(step, carry):
        streams, top, denom, accum = carry
        streams = (from_behind(streams[0], "res", 1),)
        return consume((streams, top, denom, accum), step)

    carry = lax.fori_loop(1, cycle_size, cycle_step, carry)
    streams, top, denom, accum = carry
    denom = lax.all_gather(denom, "seq", axis=1, tiled=True)
    attended = (accum / jnp.transpose(denom)[None, :, :, None]).astype(jnp.bfloat16)
    attended = attended.reshape(rows * cells, head_count * HEAD_DIM)
    projected = jnp.dot(attended, w_out, preferred_element_type=jnp.float32)
    result = lax.psum_scatter(
        projected.astype(jnp.bfloat16), "head", scatter_dimension=1, tiled=True
    ).astype(jnp.float32)
    return result.astype(jnp.bfloat16).reshape(rows, cells, result.shape[1])


def solution(mesh):
    in_specs = (
        P(("grp", "seq"), "res", None),
        P(("grp", "seq")),
        P(("grp", "res")),
        P(None, "head"),
        P(None, "head"),
        P(None, "head"),
        P("head", None),
    )
    out_specs = P(("grp", "seq"), "res", "head")
    return jax.shard_map(shards, mesh=mesh, in_specs=in_specs, out_specs=out_specs, check_vma=False)
```

profile of v0, /device:TPU:0, one launch (start us, length us, event | category | flops | bytes accessed | tf_op | source)
XLA Modules:
  0.0 243.3 jit_solution(7062445969776256166)
XLA Ops:
  6.5 1.4 reduce_sum.34
  8.6 6.4 %psum.7 = f32[]{:T(128)} all-reduce(f32[]{:T(128)S(6)} %convert_element_type.39), channel_id=1, replica_groups=mesh['grp'=2,'res'=4,'seq'=2,'head'=2] {'seq'}, use_global_device_ids=true, to_apply=%region_1.0 | all-reduce | flops 1 | bytes 8 | tf_op jit(solution)/shard_map/psum | solution.py:20
  15.7 0.7 multiply_multiply_fusion
  16.3 2.1 copy.32
  18.5 0.8 convolution_convert_fusion.2
  19.2 0.9 reshape.41
  20.1 1.7 fusion.4
  21.9 0.8 copy-done.2
  22.7 1.3 convolution_bitcast_fusion.2
  24.0 1.1 copy.30
  25.1 0.9 copy.39
  26.0 0.8 convolution_convert_fusion.1
  27.0 1.8 reshape.42
  28.8 0.7 stack_reshape.7
  29.5 0.4 copy-done.4
  29.9 0.7 stack_reshape.6
  30.6 0.4 pad_maximum_fusion
  30.9 1.3 copy.38
  32.3 11.7 %all-gather.1 = s32[4,1,128]{2,1,0:T(1,128)S(1)} all-gather(s32[1,1,128]{2,1,0:T(1,128)S(1)} %bitcast.106), channel_id=1, replica_groups=mesh['grp'=2,'res'=4,'seq'=2,'head'=2] {'res'}, dimensions={0}, use_global_device_ids=true | all-gather | bytes 2560 | tf_op jit(solution)/shard_map/all_gather | solution.py:37
  44.0 1.0 select_reduce_fusion.1
  45.1 1.2 fusion.11
  46.3 4.4 %all-gather.2 = f32[2,64,6]{1,2,0:T(8,128)S(1)} all-gather(f32[1,64,6]{1,2,0:T(8,128)S(1)} %get-tuple-element.253), channel_id=1, replica_groups=mesh['grp'=2,'res'=4,'seq'=2,'head'=2] {'seq'}, dimensions={0}, use_global_device_ids=true | all-gather | bytes 4608 | tf_op jit(solution)/shard_map/all_gather | solution.py:72
  50.8 5.3 %all_gather.34 = bf16[6,128,128]{2,1,0:T(8,128)(2,1)S(1)} all-gather(bf16[6,64,128]{2,1,0:T(8,128)(2,1)S(1)} %get-tuple-element.251), channel_id=1, replica_groups=mesh['grp'=2,'res'=4,'seq'=2,'head'=2] {'seq'}, dimensions={1}, use_global_device_ids=true | all-gather | bytes 294912 | tf_op jit(solution)/shard_map/all_gather | solution.py:71
  56.0 1.9 fusion.3
  57.9 160.1 %while.21 = (s32[]{:T(128)}, bf16[2,6,128,6,64]{2,4,1,3,0:T(8,128)(2,1)}, f32[6,64]{1,0:T(8,128)S(1)}, f32[6,64]{1,0:T(8,128)S(1)}, f32[6,128,6,64]{1,3,0,2:T(8,...) while((s32[]{:T(128)}, ...), condition=%wide.region_9.10_spmd, body=%wide.region_5.9_spmd.sunk | while | flops 151880960 | bytes 23242548 | solution.py:88
  58.1 24.5 %collective-permute-done = bf16[2,6,128,6,64]{2,4,1,3,0:T(8,128)(2,1)S(1)} collective-permute-done((bf16[2,6,128,6,64]{2,4,1,3,0:T(8,128)(2,1)}, bf16[2,6,128,6,64]{2,4,1,3,0:T(8,128)(2,1)S(1)}, u32[]{:S(2)}, u32[]{:S(2)}) %collective-permute-start) | collective-permute-done | bytes 1179680 | tf_op jit(solution)/shard_map/while/body/eval_jaxpr/ppermute | solution.py:13
  82.6 2.6 %convolution_bitcast_fusion.4 = f32[6,128,128]{2,1,0:T(8,128)} fusion(bf16[6,128,6,64]{1,3,0,2:T(8,128)(2,1)} %get-tuple-element.347, bf16[2,6,128,6,64]{2,4,1,3,0:T(8,128)(2,1)S(1)} %collective-permute-done), kind=kOutput, calls=%fused_computation.clone.1 | convolution fusion | flops 75497472 | bytes 1572864 | tf_op jit(solution)/shard_map/while/body/eval_jaxpr/rihe,rjhe->hij/dot_general | solution.py:48
  85.3 1.0 copy.73
  86.3 10.4 %reduce-scatter.10.cloned.1.call-done = f32[6,64,128]{2,1,0:T(8,128)} async-done(((f32[6,128,128]{2,1,0:T(8,128)}), f32[6,64,128]{2,1,0:T(8,128)}) %reduce-scatter.10.cloned.1.call-update) | async-done | bytes 196624 | tf_op jit(solution)/shard_map/while/body/eval_jaxpr/reduce_scatter | solution.py:64
  96.8 1.0 select_reduce_fusion.3
  97.8 1.2 fusion.35
  99.0 4.4 %all-gather.5 = f32[2,64,6]{1,2,0:T(8,128)S(1)} all-gather(f32[1,64,6]{1,2,0:T(8,128)S(1)} %get-tuple-element.311), channel_id=1, replica_groups=mesh['grp'=2,'res'=4,'seq'=2,'head'=2] {'seq'}, dimensions={0}, use_global_device_ids=true | all-gather | bytes 4608 | tf_op jit(solution)/shard_map/while/body/eval_jaxpr/all_gather | solution.py:72
  103.5 5.3 %all_gather.37 = bf16[6,128,128]{2,1,0:T(8,128)(2,1)S(1)} all-gather(bf16[6,64,128]{2,1,0:T(8,128)(2,1)S(1)} %get-tuple-element.310), channel_id=1, replica_groups=mesh['grp'=2,'res'=4,'seq'=2,'head'=2] {'seq'}, dimensions={1}, use_global_device_ids=true | all-gather | bytes 294912 | tf_op jit(solution)/shard_map/while/body/eval_jaxpr/all_gather | solution.py:71
  108.7 0.3 fusion.36
  109.1 0.5 multiply_add_fusion.6
  109.6 1.5 collective-permute-start
  111.1 25.8 %collective-permute-done = bf16[2,6,128,6,64]{2,4,1,3,0:T(8,128)(2,1)S(1)} collective-permute-done((bf16[2,6,128,6,64]{2,4,1,3,0:T(8,128)(2,1)}, bf16[2,6,128,6,64]{2,4,1,3,0:T(8,128)(2,1)S(1)}, u32[]{:S(2)}, u32[]{:S(2)}) %collective-permute-start) | collective-permute-done | bytes 1179680 | tf_op jit(solution)/shard_map/while/body/eval_jaxpr/ppermute | solution.py:13
  136.9 2.6 %convolution_bitcast_fusion.4 = f32[6,128,128]{2,1,0:T(8,128)} fusion(bf16[6,128,6,64]{1,3,0,2:T(8,128)(2,1)} %get-tuple-element.347, bf16[2,6,128,6,64]{2,4,1,3,0:T(8,128)(2,1)S(1)} %collective-permute-done), kind=kOutput, calls=%fused_computation.clone.1 | convolution fusion | flops 75497472 | bytes 1572864 | tf_op jit(solution)/shard_map/while/body/eval_jaxpr/rihe,rjhe->hij/dot_general | solution.py:48
  139.6 1.0 copy.73
  140.6 10.4 %reduce-scatter.10.cloned.1.call-done = f32[6,64,128]{2,1,0:T(8,128)} async-done(((f32[6,128,128]{2,1,0:T(8,128)}), f32[6,64,128]{2,1,0:T(8,128)}) %reduce-scatter.10.cloned.1.call-update) | async-done | bytes 196624 | tf_op jit(solution)/shard_map/while/body/eval_jaxpr/reduce_scatter | solution.py:64
  151.0 1.0 select_reduce_fusion.3
  152.1 1.2 fusion.35
  153.3 4.4 %all-gather.5 = f32[2,64,6]{1,2,0:T(8,128)S(1)} all-gather(f32[1,64,6]{1,2,0:T(8,128)S(1)} %get-tuple-element.311), channel_id=1, replica_groups=mesh['grp'=2,'res'=4,'seq'=2,'head'=2] {'seq'}, dimensions={0}, use_global_device_ids=true | all-gather | bytes 4608 | tf_op jit(solution)/shard_map/while/body/eval_jaxpr/all_gather | solution.py:72
  157.7 5.3 %all_gather.37 = bf16[6,128,128]{2,1,0:T(8,128)(2,1)S(1)} all-gather(bf16[6,64,128]{2,1,0:T(8,128)(2,1)S(1)} %get-tuple-element.310), channel_id=1, replica_groups=mesh['grp'=2,'res'=4,'seq'=2,'head'=2] {'seq'}, dimensions={1}, use_global_device_ids=true | all-gather | bytes 294912 | tf_op jit(solution)/shard_map/while/body/eval_jaxpr/all_gather | solution.py:71
  163.0 0.3 fusion.36
  163.3 0.5 multiply_add_fusion.6
  163.9 1.6 collective-permute-start
  165.4 25.8 %collective-permute-done = bf16[2,6,128,6,64]{2,4,1,3,0:T(8,128)(2,1)S(1)} collective-permute-done((bf16[2,6,128,6,64]{2,4,1,3,0:T(8,128)(2,1)}, bf16[2,6,128,6,64]{2,4,1,3,0:T(8,128)(2,1)S(1)}, u32[]{:S(2)}, u32[]{:S(2)}) %collective-permute-start) | collective-permute-done | bytes 1179680 | tf_op jit(solution)/shard_map/while/body/eval_jaxpr/ppermute | solution.py:13
  191.2 2.6 %convolution_bitcast_fusion.4 = f32[6,128,128]{2,1,0:T(8,128)} fusion(bf16[6,128,6,64]{1,3,0,2:T(8,128)(2,1)} %get-tuple-element.347, bf16[2,6,128,6,64]{2,4,1,3,0:T(8,128)(2,1)S(1)} %collective-permute-done), kind=kOutput, calls=%fused_computation.clone.1 | convolution fusion | flops 75497472 | bytes 1572864 | tf_op jit(solution)/shard_map/while/body/eval_jaxpr/rihe,rjhe->hij/dot_general | solution.py:48
  193.9 1.0 copy.73
  194.9 10.4 %reduce-scatter.10.cloned.1.call-done = f32[6,64,128]{2,1,0:T(8,128)} async-done(((f32[6,128,128]{2,1,0:T(8,128)}), f32[6,64,128]{2,1,0:T(8,128)}) %reduce-scatter.10.cloned.1.call-update) | async-done | bytes 196624 | tf_op jit(solution)/shard_map/while/body/eval_jaxpr/reduce_scatter | solution.py:64
  205.3 1.0 select_reduce_fusion.3
  206.4 1.2 fusion.35
  207.6 4.4 %all-gather.5 = f32[2,64,6]{1,2,0:T(8,128)S(1)} all-gather(f32[1,64,6]{1,2,0:T(8,128)S(1)} %get-tuple-element.311), channel_id=1, replica_groups=mesh['grp'=2,'res'=4,'seq'=2,'head'=2] {'seq'}, dimensions={0}, use_global_device_ids=true | all-gather | bytes 4608 | tf_op jit(solution)/shard_map/while/body/eval_jaxpr/all_gather | solution.py:72
  212.0 5.3 %all_gather.37 = bf16[6,128,128]{2,1,0:T(8,128)(2,1)S(1)} all-gather(bf16[6,64,128]{2,1,0:T(8,128)(2,1)S(1)} %get-tuple-element.310), channel_id=1, replica_groups=mesh['grp'=2,'res'=4,'seq'=2,'head'=2] {'seq'}, dimensions={1}, use_global_device_ids=true | all-gather | bytes 294912 | tf_op jit(solution)/shard_map/while/body/eval_jaxpr/all_gather | solution.py:71
  217.3 0.3 fusion.36
  217.6 0.5 multiply_add_fusion.6
  218.1 4.4 %all-gather.3 = f32[2,64,6]{1,2,0:T(8,128)S(1)} all-gather(f32[1,64,6]{1,2,0:T(8,128)S(1)} %bitcast.103), channel_id=1, replica_groups=mesh['grp'=2,'res'=4,'seq'=2,'head'=2] {'seq'}, dimensions={0}, use_global_device_ids=true | all-gather | bytes 4608 | tf_op jit(solution)/shard_map/all_gather | solution.py:90
  222.8 0.4 copy.41
  223.2 0.5 copy-done.8
  223.7 0.8 convolution_convert_fusion
  224.5 1.4 copy.49
  225.9 8.7 %reduce-scatter.8.cloned.1.call-done = bf16[384,768]{1,0:T(8,128)(2,1)} async-done(((bf16[768,768]{1,0:T(8,128)(2,1)}), bf16[384,768]{1,0:T(8,128)(2,1)}) %reduce-scatter.8.cloned.1.call-update) | async-done | bytes 589840
  234.6 2.1 copy.50
  (65 shorter events, 1.6 us)
Async XLA Ops:
  6.5 11.9 %copy-start = (bf16[6,128,768]{2,1,0:T(8,128)(2,1)S(1)}, bf16[6,128,768]{2,1,0:T(8,128)(2,1)}, u32[]{:S(2)}) copy-start(bf16[6,128,768]{2,1,0:T(8,128)(2,1)} %param.9) | copy-start | bytes 3538948
  6.5 11.9 %copy-start.6 = (bf16[768,384]{1,0:T(8,128)(2,1)S(1)}, bf16[768,384]{1,0:T(8,128)(2,1)}, u32[]{:S(2)}) copy-start(bf16[768,384]{1,0:T(8,128)(2,1)} %param.13) | copy-start | bytes 1769476
  6.5 37.5 %reduce-scatter.6.cloned.1.call-start = ((), (), s32[]{:S(2)}) async-start(), calls=%async_computation.3 | async-start | bytes 589824 | tf_op jit(solution)/shard_map/reduce_scatter | solution.py:64
  21.9 0.8 copy-start.2
  24.0 1.1 copy-start.3
  24.0 2.0 copy-start.7
  28.8 1.1 copy-start.4
  30.9 1.3 copy-start.5
  58.0 38.8 %reduce-scatter.10.cloned.1.call-start = ((), (), s32[]{:S(2)}) async-start(), calls=%async_computation.5 | async-start | bytes 589824 | tf_op jit(solution)/shard_map/while/body/eval_jaxpr/reduce_scatter | solution.py:64
  58.0 24.6 %collective-permute-start = (bf16[2,6,128,6,64]{2,4,1,3,0:T(8,128)(2,1)}, bf16[2,6,128,6,64]{2,4,1,3,0:T(8,128)(2,1)S(1)}, u32[]{:S(2)}, u32[]{:S(2)}) collective-permute-start(bf16[2,6,128,6,64]{2,4,1,3,0:T(8,128)(2,1)} %get-tuple-element.327), channel_id=1, source_target_pairs={{0,4},{4,8},{8,12},{12,0},{1,5},{5,9},{9,13},{13,1},{2,6},{6,10},{... | collective-permute-start | bytes 3538952 | tf_op jit(solution)/shard_map/while/body/eval_jaxpr/ppermute | solution.py:13
  82.6 2.7 %copy-start.1 = (bf16[2,6,128,6,64]{2,4,1,3,0:T(8,128)(2,1)}, bf16[2,6,128,6,64]{2,4,1,3,0:T(8,128)(2,1)S(1)}, u32[]{:S(2)}) copy-start(bf16[2,6,128,6,64]{2,4,1,3,0:T(8,128)(2,1)S(1)} %collective-permute-done) | copy-start | bytes 3538948 | tf_op jit(solution)/shard_map/while
  86.3 22.4 %slice-start = ((bf16[2,6,128,6,64]{2,4,1,3,0:T(8,128)(2,1)}), bf16[1,6,128,6,64]{2,4,1,3,0:T(8,128)(2,1)S(1)}, s32[]{:S(2)}) async-start(bf16[2,6,128,6,64]{2,4,1,3,0:T(8,128)(2,1)} %copy-done.1), calls=%async_computation.6 | async-start | bytes 1179648 | tf_op jit(solution)/shard_map/while/body/eval_jaxpr/slice | solution.py:59
  109.5 41.5 %reduce-scatter.10.cloned.1.call-start = ((), (), s32[]{:S(2)}) async-start(), calls=%async_computation.5 | async-start | bytes 589824 | tf_op jit(solution)/shard_map/while/body/eval_jaxpr/reduce_scatter | solution.py:64
  109.6 27.3 %collective-permute-start = (bf16[2,6,128,6,64]{2,4,1,3,0:T(8,128)(2,1)}, bf16[2,6,128,6,64]{2,4,1,3,0:T(8,128)(2,1)S(1)}, u32[]{:S(2)}, u32[]{:S(2)}) collective-permute-start(bf16[2,6,128,6,64]{2,4,1,3,0:T(8,128)(2,1)} %get-tuple-element.327), channel_id=1, source_target_pairs={{0,4},{4,8},{8,12},{12,0},{1,5},{5,9},{9,13},{13,1},{2,6},{6,10},{... | collective-permute-start | bytes 3538952 | tf_op jit(solution)/shard_map/while/body/eval_jaxpr/ppermute | solution.py:13
  136.9 2.7 %copy-start.1 = (bf16[2,6,128,6,64]{2,4,1,3,0:T(8,128)(2,1)}, bf16[2,6,128,6,64]{2,4,1,3,0:T(8,128)(2,1)S(1)}, u32[]{:S(2)}) copy-start(bf16[2,6,128,6,64]{2,4,1,3,0:T(8,128)(2,1)S(1)} %collective-permute-done) | copy-start | bytes 3538948 | tf_op jit(solution)/shard_map/while
  140.6 22.4 %slice-start = ((bf16[2,6,128,6,64]{2,4,1,3,0:T(8,128)(2,1)}), bf16[1,6,128,6,64]{2,4,1,3,0:T(8,128)(2,1)S(1)}, s32[]{:S(2)}) async-start(bf16[2,6,128,6,64]{2,4,1,3,0:T(8,128)(2,1)} %copy-done.1), calls=%async_computation.6 | async-start | bytes 1179648 | tf_op jit(solution)/shard_map/while/body/eval_jaxpr/slice | solution.py:59
  163.8 41.5 %reduce-scatter.10.cloned.1.call-start = ((), (), s32[]{:S(2)}) async-start(), calls=%async_computation.5 | async-start | bytes 589824 | tf_op jit(solution)/shard_map/while/body/eval_jaxpr/reduce_scatter | solution.py:64
  163.9 27.3 %collective-permute-start = (bf16[2,6,128,6,64]{2,4,1,3,0:T(8,128)(2,1)}, bf16[2,6,128,6,64]{2,4,1,3,0:T(8,128)(2,1)S(1)}, u32[]{:S(2)}, u32[]{:S(2)}) collective-permute-start(bf16[2,6,128,6,64]{2,4,1,3,0:T(8,128)(2,1)} %get-tuple-element.327), channel_id=1, source_target_pairs={{0,4},{4,8},{8,12},{12,0},{1,5},{5,9},{9,13},{13,1},{2,6},{6,10},{... | collective-permute-start | bytes 3538952 | tf_op jit(solution)/shard_map/while/body/eval_jaxpr/ppermute | solution.py:13
  191.2 2.7 %copy-start.1 = (bf16[2,6,128,6,64]{2,4,1,3,0:T(8,128)(2,1)}, bf16[2,6,128,6,64]{2,4,1,3,0:T(8,128)(2,1)S(1)}, u32[]{:S(2)}) copy-start(bf16[2,6,128,6,64]{2,4,1,3,0:T(8,128)(2,1)S(1)} %collective-permute-done) | copy-start | bytes 3538948 | tf_op jit(solution)/shard_map/while
  194.9 22.4 %slice-start = ((bf16[2,6,128,6,64]{2,4,1,3,0:T(8,128)(2,1)}), bf16[1,6,128,6,64]{2,4,1,3,0:T(8,128)(2,1)S(1)}, s32[]{:S(2)}) async-start(bf16[2,6,128,6,64]{2,4,1,3,0:T(8,128)(2,1)} %copy-done.1), calls=%async_computation.6 | async-start | bytes 1179648 | tf_op jit(solution)/shard_map/while/body/eval_jaxpr/slice | solution.py:59
  218.1 16.5 %reduce-scatter.8.cloned.1.call-start = ((), (), s32[]{:S(2)}) async-start(), calls=%async_computation.4 | async-start | bytes 1769472
  222.6 1.1 copy-start.8
Sparse Core Ops, SparseCore 0:
  24.1 14.9 reduce-scatter.5
  85.3 11.4 reduce-scatter.9
  139.6 11.3 reduce-scatter.9
  193.9 11.3 reduce-scatter.9
  226.1 8.5 reduce-scatter.7
where the time goes:
time: 244 us; the launch traced here: 243 us
  waiting for transfers between devices  116 us (48%)
  blocking collectives  61 us (25%)
  local copies, waits for them, and re-layouts  18.9 us (8%)
  matrix products  15.9 us (7%)
  between operations  14.6 us (6%)
  other arithmetic  13.2 us (5%)
  starting transfers between devices  3.32 us (1%)
    ppermute x3, waiting for transfers between devices, from_behind(): lax.ppermute(value, axis, [(i, (i + by) % length) for i in range(length)])  76 us
    reduce_scatter x4, waiting for transfers between devices, consume(): summed = lax.psum_scatter(tiles, 'seq', scatter_dimension=1, tiled=True)  31.3 us
    all_gather x4, blocking collectives, consume(): probs = lax.all_gather(probs, 'seq', axis=1, tiled=True)  21.1 us
    all_gather x4, blocking collectives, consume(): rescale = lax.all_gather(rescale, 'seq', axis=1, tiled=True)  17.5 us
    all_gather x1, blocking collectives, shards(): mask_all = lax.all_gather(key_mask, 'res', axis=0, tiled=True)  11.7 us
    dot_general x4, matrix products, scores(): jnp.einsum('rihe,rjhe->hij', q_part, k_part, preferred_element_type=jnp.f...  9.02 us
    unnamed x3, waiting for transfers between devices  8.7 us
    unnamed x19, local copies, waits for them, and re-layouts  7.38 us
  transfers between devices with their start and end apart: 8, of which 7 were waited for; matrix products, arithmetic and copies ran while one was open for 5% of the time, Pallas kernels for 0%

commit v1 on v0

v1 whole, which is shorter than its diff:
```python
import functools
import math

import jax
import jax.numpy as jnp
from jax import lax
from jax.experimental import pallas as pl
from jax.experimental.pallas import tpu as pltpu
from jax.sharding import PartitionSpec as P

HEAD_DIM = 64
LANES = 128
PER_TILE = LANES // HEAD_DIM
MASKED = -1000000000.0
VMEM_LIMIT = 24 * 1024 * 1024


def ring(value, axis, by=1):
    length = lax.axis_size(axis)
    return lax.ppermute(value, axis, [(i, (i + by) % length) for i in range(length)])


def whole(count):
    return [pl.BlockSpec(memory_space=pltpu.VMEM) for _ in range(count)]


def call(kernel, out_shape, args, flops, scalars=0, scratch=()):
    specs = [pl.BlockSpec(memory_space=pltpu.SMEM)] * scalars + whole(len(args) - scalars)
    multiple = isinstance(out_shape, (list, tuple))
    size = sum(a.size * a.dtype.itemsize for a in args)
    return pl.pallas_call(
        kernel,
        out_shape=out_shape,
        in_specs=specs,
        out_specs=whole(len(out_shape)) if multiple else whole(1)[0],
        scratch_shapes=list(scratch),
        cost_estimate=pl.CostEstimate(flops=int(flops), transcendentals=0, bytes_accessed=int(size)),
        compiler_params=pltpu.CompilerParams(vmem_limit_bytes=VMEM_LIMIT),
    )(*args)


def lane_head(shape):
    return lax.broadcasted_iota(jnp.int32, shape, len(shape) - 1) // HEAD_DIM


def dot(a, b):
    return jnp.dot(a, b, preferred_element_type=jnp.float32)


def dot_nt(a, b):
    return lax.dot_general(a, b, (((1,), (1,)), ((), ())), preferred_element_type=jnp.float32)


def per_head(value, pick):
    heads = lane_head(value.shape)
    parts = [pick(value, heads == h) for h in range(PER_TILE)]
    out = parts[-1]
    for h in range(PER_TILE - 2, -1, -1):
        out = jnp.where(heads == h, parts[h], out)
    return jnp.broadcast_to(out, value.shape)


def max_over(value, keep):
    return jnp.max(jnp.where(keep, value, -jnp.inf), axis=-1, keepdims=True)


def sum_over(value, keep):
    return jnp.sum(jnp.where(keep, value, 0.0), axis=-1, keepdims=True)


def spread(target, chunk, flat, first_row, cells):
    rows = flat.shape[0] // cells
    tiles = flat.shape[1] // LANES
    heads = lane_head((cells, LANES))
    for tile in range(tiles):
        for row in range(rows):
            part = flat[row * cells : (row + 1) * cells, tile * LANES : (tile + 1) * LANES]
            at = slice((first_row + row) * LANES, (first_row + row + 1) * LANES)
            for h in range(PER_TILE):
                kept = jnp.where(heads == h, part, jnp.zeros_like(part))
                target[chunk, tile, h * cells : (h + 1) * cells, at] = kept


def project_kernel(*refs, chunks, pieces):
    query, w_key, w_value = refs[:3]
    tokens = refs[3 : 3 + chunks * pieces]
    logits, values, keys = refs[3 + chunks * pieces :]
    rows, cells, width = tokens[0].shape
    for chunk in range(chunks):
        for piece in range(pieces):
            flat = tokens[chunk * pieces + piece][...].reshape(rows * cells, width)
            spread(keys, 0, dot(flat, w_key[...]).astype(jnp.bfloat16), piece * rows, cells)
            spread(values, chunk, dot(flat, w_value[...]).astype(jnp.bfloat16), piece * rows, cells)
        for tile in range(query.shape[0]):
            logits[chunk, tile] = dot_nt(query[tile], keys[0, tile])


def own_kernel(order, factor, tokens, w_query, w_key, w_value, query, logits, values, keys):
    rows, cells, width = tokens.shape
    chunks = logits.shape[0]
    part = cells // chunks
    for row in range(rows):
        source = order[row]
        block = tokens[source]
        scaled = (dot(block, w_query[...]) * factor[source]).astype(jnp.bfloat16)
        for tile in range(query.shape[0]):
            query[tile, :, row * LANES : (row + 1) * LANES] = scaled[:, tile * LANES : (tile + 1) * LANES]
        key = dot(block, w_key[...]).astype(jnp.bfloat16)
        value = dot(block, w_value[...]).astype(jnp.bfloat16)
        for chunk in range(chunks):
            spread(keys, chunk, key[chunk * part : (chunk + 1) * part], row, part)
            spread(values, chunk, value[chunk * part : (chunk + 1) * part], row, part)
    for chunk in range(chunks):
        for tile in range(query.shape[0]):
            logits[chunk, tile] = dot_nt(query[tile], keys[chunk, tile])


def absorb(units, state, tile, rows):
    scores, mixed = [], []
    for tiles, mask, values in units:
        for chunk in range(tiles[0].shape[0]):
            total = tiles[0][chunk, tile]
            for other in tiles[1:]:
                total = total + other[chunk, tile]
            scores.append(jnp.where(mask[chunk : chunk + 1] > 0, total, MASKED))
            mixed.append(values[chunk, tile])
    top = functools.reduce(jnp.maximum, scores)
    top = per_head(top, max_over)
    if state is not None:
        before = state[0][tile]
        top = jnp.maximum(top, before)
        rescale = jnp.exp(before - top)
    expo = [jnp.exp(score - top) for score in scores]
    denom = functools.reduce(jnp.add, expo)
    probs = jnp.concatenate([e.astype(jnp.bfloat16) for e in expo], axis=1)
    accum = dot(probs, jnp.concatenate(mixed, axis=0))
    if state is not None:
        denom = denom + state[1][tile] * rescale
        accum = accum + state[2][tile] * jnp.concatenate([rescale] * rows, axis=1)
    return top, denom, accum


def read_units(refs, sizes):
    units, at = [], 0
    for size in sizes:
        units.append((refs[at : at + size], refs[at + size], refs[at + size + 1]))
        at += size + 2
    return units, refs[at:]


def absorb_kernel(*refs, sizes, carried):
    units, refs = read_units(refs, sizes)
    state = refs[:3] if carried else None
    top, denom, accum = refs[-3:]
    rows = accum.shape[2] // LANES
    for tile in range(accum.shape[0]):
        top[tile], denom[tile], accum[tile] = absorb(units, state, tile, rows)


def finish_kernel(order, *refs, sizes, carried):
    units, refs = read_units(refs, sizes)
    state = refs[:3] if carried else None
    w_send, attended, sent = refs[-3:]
    rows, cells, _ = attended.shape
    for tile in range(attended.shape[2] // LANES):
        top, denom, accum = absorb(units, state, tile, rows)
        denom = per_head(denom, sum_over)
        for row in range(rows):
            part = accum[:, row * LANES : (row + 1) * LANES] / denom
            attended[row, :, tile * LANES : (tile + 1) * LANES] = part.astype(jnp.bfloat16)
    for row in range(rows):
        sent[order[row]] = dot(attended[row], w_send[...]).astype(jnp.bfloat16)


def output_kernel(order, attended, w_own, kept):
    for row in range(attended.shape[0]):
        kept[order[row]] = dot(attended[row], w_own[...])


def shards(tokens, weights, key_mask, w_query, w_key, w_value, w_out):
    rows, cells, width = tokens.shape
    inner = w_query.shape[1]
    tiles = inner // LANES
    blocks = lax.axis_size("res")
    holders = lax.axis_size("seq")
    cores = lax.axis_size("head")
    core = lax.axis_index("head")
    part = HEAD_DIM
    chunks = cells // part
    share = rows // cores
    assert share * cores == rows and chunks * part == cells and tiles * LANES == inner
    f32, bf16 = jnp.float32, jnp.bfloat16

    def shape(dims, kind):
        return jax.ShapeDtypeStruct(dims, kind)

    moving = [
        lax.dynamic_slice(tokens, (core * share, k * part, 0), (share, part, width))
        for k in range(chunks)
    ]
    mask = jnp.tile(key_mask.reshape(chunks, part), (1, PER_TILE))
    order = jnp.concatenate(
        [(core - k) % cores * share + jnp.arange(share, dtype=jnp.int32) for k in range(cores)]
    )

    total = jnp.full((8, LANES), jnp.sum(weights).astype(f32))
    passing = total
    for _ in range(holders - 1):
        passing = ring(passing, "seq")
        total = total + passing
    factor = weights.astype(f32) * lax.rsqrt(total[0, 0]) / math.sqrt(HEAD_DIM)

    def exchange(logits):
        return [logits] + [ring(logits, "seq", k) for k in range(1, holders)]

    depth = PER_TILE * part
    spans = rows * LANES
    query, logits, values = call(
        own_kernel,
        [
            shape((tiles, cells, spans), bf16),
            shape((chunks, tiles, cells, depth), f32),
            shape((chunks, tiles, depth, spans), bf16),
        ],
        [order, factor, tokens, w_query, w_key, w_value],
        2 * rows * cells * inner * (3 * width + cells * PER_TILE),
        scalars=2,
        scratch=[pltpu.VMEM((chunks, tiles, depth, spans), bf16)],
    )
    units = [(exchange(logits), mask, values)]

    def project(pieces, count):
        return call(
            functools.partial(project_kernel, chunks=count, pieces=cores),
            [shape((count, tiles, cells, depth), f32), shape((count, tiles, depth, spans), bf16)],
            [query, w_key, w_value] + pieces,
            2 * rows * part * count * inner * (2 * width + cells * PER_TILE),
            scratch=[pltpu.VMEM((1, tiles, depth, spans), bf16)],
        )

    for step in range(1, blocks):
        moving = [ring(piece, "res") for piece in moving]
        mask = ring(mask, "res")
        pieces = [[piece] + [ring(piece, "head", k) for k in range(1, cores)] for piece in moving]
        if step < blocks - 1:
            logits, values = project(sum(pieces, []), chunks)
            units.append((exchange(logits), mask, values))
        else:
            for k in range(chunks):
                logits, values = project(pieces[k], 1)
                units.append((exchange(logits), mask[k : k + 1], values))

    state = []
    state_shape = [
        shape((tiles, cells, LANES), f32),
        shape((tiles, cells, LANES), f32),
        shape((tiles, cells, spans), f32),
    ]

    def flatten(group):
        return sum([list(u[0]) + [u[1], u[2]] for u in group], [])

    def work(group):
        return sum(2 * u[0][0].size * spans for u in group)

    groups = []
    early = units[: len(units) - chunks] if blocks > 1 else []
    for at in range(0, len(early), 3):
        groups.append(early[at : at + 3])
    groups += [[unit] for unit in units[len(early) :]]
    for group in groups[:-1]:
        state = call(
            functools.partial(absorb_kernel, sizes=[len(u[0]) for u in group], carried=bool(state)),
            state_shape,
            flatten(group) + list(state),
            work(group),
        )
    group = groups[-1]
    columns = width // cores
    outs = [
        lax.dynamic_slice(w_out, (0, (core + k) % cores * columns), (inner, columns))
        for k in range(cores)
    ]
    attended, sent = call(
        functools.partial(finish_kernel, sizes=[len(u[0]) for u in group], carried=bool(state)),
        [shape((rows, cells, inner), bf16), shape((rows, cells, columns), bf16)],
        [order] + flatten(group) + list(state) + [outs[1 % cores]],
        work(group) + 2 * rows * cells * inner * columns,
        scalars=1,
    )

    def output(w):
        return call(
            output_kernel,
            shape((rows, cells, columns), f32),
            [order, attended, w],
            2 * rows * cells * inner * columns,
            scalars=1,
        )

    if cores == 1:
        return output(outs[0]).astype(bf16)
    received = [ring(sent, "head")]
    for k in range(2, cores):
        received.append(ring(output(outs[k]).astype(bf16), "head", k))
    result = output(outs[0])
    for value in received:
        result = result + value.astype(f32)
    return result.astype(bf16)


def solution(mesh):
    in_specs = (
        P(("grp", "seq"), "res", None),
        P(("grp", "seq")),
        P(("grp", "res")),
        P(None, "head"),
        P(None, "head"),
        P(None, "head"),
        P("head", None),
    )
    out_specs = P(("grp", "seq"), "res", "head")
    return jax.shard_map(shards, mesh=mesh, in_specs=in_specs, out_specs=out_specs, check_vma=False)
```

time: 244 us -> 88.4 us (0.36)
  waiting for transfers between devices: 116 us -> 53.5 us
  blocking collectives: 61 us -> 0 us
  matrix products: 15.9 us -> 0 us
  local copies, waits for them, and re-layouts: 18.9 us -> 4.29 us
  between operations: 14.6 us -> 1.53 us
  Pallas kernels: 0 us -> 12.2 us
  starting transfers between devices: 3.32 us -> 14.9 us
  other arithmetic: 13.2 us -> 1.69 us
    all_gather x10 -> x0, blocking collectives: 54.6 us -> none  [the longest x4 21.1 us: consume(): probs = lax.all_gather(probs, 'seq', axis=1, tiled=True)]
    reduce_scatter x4 -> x0, waiting for transfers between devices: 31.3 us -> none  [consume(): summed = lax.psum_scatter(tiles, 'seq', scatter_dimension=1, tiled=True)]
    ppermute x3 -> x22, waiting for transfers between devices: 76 us -> 53.5 us  [ring(): lax.ppermute(value, axis, [(i, (i + by) % length) for i in range(length)])]
    dot_general x9 -> x0, matrix products: 15 us -> none  [the longest x4 9.02 us: scores(): jnp.einsum('rihe,rjhe->hij', q_part, k_part, preferred_element_type=jnp.f...]
    pallas_call x0 -> x9, Pallas kernels: none -> 12.2 us  [call(): pl.pallas_call(kernel, out_shape=out_shape, in_specs=specs, out_specs=who...]
    ppermute x3 -> x22, starting transfers between devices: 3.15 us -> 14.9 us  [ring(): lax.ppermute(value, axis, [(i, (i + by) % length) for i in range(length)])]
    unnamed x3 -> x0, waiting for transfers between devices: 8.7 us -> none
    psum x1 -> x0, blocking collectives: 6.37 us -> none  [shards(): total = lax.psum(jnp.sum(weights).astype(jnp.float32), 'seq')]
  transfers between devices with their start and end apart: 8 -> 22, of which waited for: 7 -> 12; matrix products, arithmetic and copies ran while one was open for 5% -> 2% of each run, Pallas kernels for 0% -> 12%
where the time goes in v1:
time: 88.4 us; the launch traced here: 88.2 us
  waiting for transfers between devices  53.5 us (61%)
  starting transfers between devices  14.9 us (17%)
  Pallas kernels  12.2 us (14%)
  local copies, waits for them, and re-layouts  4.29 us (5%)
  other arithmetic  1.69 us (2%)
  between operations  1.53 us (2%)
    ppermute x22, waiting for transfers between devices, ring(): lax.ppermute(value, axis, [(i, (i + by) % length) for i in range(length)])  53.5 us
    ppermute x22, starting transfers between devices, ring(): lax.ppermute(value, axis, [(i, (i + by) % length) for i in range(length)])  14.9 us
    pallas_call x9, Pallas kernels, call(): pl.pallas_call(kernel, out_shape=out_shape, in_specs=specs, out_specs=who...  12.2 us
    unnamed x14, local copies, waits for them, and re-layouts  2.35 us
  transfers between devices with their start and end apart: 22, of which 12 were waited for; matrix products, arithmetic and copies ran while one was open for 2% of the time, Pallas kernels for 12%

profile of v1, /device:TPU:0, one launch (start us, length us, event | category | flops | bytes accessed | tf_op | source)
XLA Modules:
  0.0 88.2 jit_solution(2016787979046732313)
XLA Ops:
  0.0 1.2 %constant_dynamic-slice_fusion.2 = (bf16[3,64,768]{2,1,0:T(8,128)(2,1)S(1)}, bf16[3,64,768]{2,1,0:T(8,128)(2,1)S(1)}) fusion(bf16[6,128,768]{2,1,0:T(8,128)(2,1)} %tokens.1, s32[]{:T(128)S(6)} %select_n.29), kind=kLoop, calls=%fused_computation.4 | loop fusion | bytes 1179652 | tf_op jit(solution)/shard_map/dynamic_slice | solution.py:198
  1.2 3.1 %collective-permute-start.9 = (bf16[3,64,768]{2,1,0:T(8,128)(2,1)S(1)}, bf16[3,64,768]{2,1,0:T(8,128)(2,1)S(1)}, u32[]{:S(2)}, u32[]{:S(2)}) collective-permute-start(bf16[3,64,768]{2,1,0:T(8,128)(2,1)S(1)} %get-tuple-element.43), channel_id=1, source_target_pairs={{0,4},{4,8},{8,12},{12,0},{1,5},{5,9},{9,13},{13,1},{2,6},{6,10},{... | collective-permute-start | bytes 884744 | tf_op jit(solution)/shard_map/ppermute | solution.py:20
  4.3 1.6 %collective-permute-start.1 = (bf16[3,64,768]{2,1,0:T(8,128)(2,1)S(1)}, bf16[3,64,768]{2,1,0:T(8,128)(2,1)S(1)}, u32[]{:S(2)}, u32[]{:S(2)}) collective-permute-start(bf16[3,64,768]{2,1,0:T(8,128)(2,1)S(1)} %get-tuple-element.44), channel_id=1, source_target_pairs={{0,4},{4,8},{8,12},{12,0},{1,5},{5,9},{9,13},{13,1},{2,6},{6,10},{... | collective-permute-start | bytes 884744 | tf_op jit(solution)/shard_map/ppermute | solution.py:20
  5.9 0.6 reduce_sum.9
  7.2 1.6 %collective-permute-start = (f32[8,128]{1,0:T(8,128)S(1)}, f32[8,128]{1,0:T(8,128)S(1)}, u32[]{:S(2)}, u32[]{:S(2)}) collective-permute-start(f32[8,128]{1,0:T(8,128)S(1)} %broadcast_in_dim.3), channel_id=1, source_target_pairs={{0,2},{2,0},{1,3},{3,1},{4,6},{6,4},{5,7},{7,5},{8,10},{10,8},{9,1... | collective-permute-start | bytes 12296 | tf_op jit(solution)/shard_map/ppermute | solution.py:20
  8.8 0.1 tile.10
  8.8 0.1 tile.12.refs_2_
  8.9 1.6 %collective-permute-start.6 = (s32[2,128]{1,0:T(2,128)S(1)}, s32[2,128]{1,0:T(2,128)S(1)}, u32[]{:S(2)}, u32[]{:S(2)}) collective-permute-start(s32[2,128]{1,0:T(2,128)S(1)} %tile.12.refs_2_), channel_id=1, source_target_pairs={{0,4},{4,8},{8,12},{12,0},{1,5},{5,9},{9,13},{13,1},{2,6},{6,10},{... | collective-permute-start | bytes 3080 | tf_op jit(solution)/shard_map/ppermute | solution.py:20
  10.5 3.7 %collective-permute-done.9.refs_3_ = bf16[3,64,768]{2,1,0:T(8,128)(2,1)S(1)} collective-permute-done((bf16[3,64,768]{2,1,0:T(8,128)(2,1)S(1)}, bf16[3,64,768]{2,1,0:T(8,128)(2,1)S(1)}, u32[]{:S(2)}, u32[]{:S(2)}) %collective-permute-start.9) | collective-permute-done | bytes 294944 | tf_op jit(solution)/shard_map/ppermute | solution.py:20
  14.2 0.0 collective-permute-start.10
  14.2 0.0 collective-permute-start.15
  14.2 6.3 %collective-permute-done.1.refs_5_ = bf16[3,64,768]{2,1,0:T(8,128)(2,1)S(1)} collective-permute-done((bf16[3,64,768]{2,1,0:T(8,128)(2,1)S(1)}, bf16[3,64,768]{2,1,0:T(8,128)(2,1)S(1)}, u32[]{:S(2)}, u32[]{:S(2)}) %collective-permute-start.1) | collective-permute-done | bytes 294944 | tf_op jit(solution)/shard_map/ppermute | solution.py:20
  20.5 0.0 collective-permute-start.2
  20.5 0.1 pad_add_fusion.order
  20.6 0.0 collective-permute-done
  20.6 0.5 slice.9
  21.8 0.1 collective-permute-start.16
  21.9 5.0 %collective-permute-done.10.refs_3_ = bf16[3,64,768]{2,1,0:T(8,128)(2,1)S(1)} collective-permute-done((bf16[3,64,768]{2,1,0:T(8,128)(2,1)S(1)}, bf16[3,64,768]{2,1,0:T(8,128)(2,1)S(1)}, u32[]{:S(2)}, u32[]{:S(2)}) %collective-permute-start.10) | collective-permute-done | bytes 294944 | tf_op jit(solution)/shard_map/ppermute | solution.py:20
  26.9 0.0 collective-permute-start.18
  26.9 0.0 collective-permute-done.6.refs_6_
  26.9 0.0 collective-permute-start.11
  26.9 6.0 %collective-permute-done.2.refs_5_ = bf16[3,64,768]{2,1,0:T(8,128)(2,1)S(1)} collective-permute-done((bf16[3,64,768]{2,1,0:T(8,128)(2,1)S(1)}, bf16[3,64,768]{2,1,0:T(8,128)(2,1)S(1)}, u32[]{:S(2)}, u32[]{:S(2)}) %collective-permute-start.2) | collective-permute-done | bytes 294944 | tf_op jit(solution)/shard_map/ppermute | solution.py:20
  32.9 0.0 collective-permute-start.19
  32.9 0.0 collective-permute-done.15.refs_4_
  32.9 0.3 collective-permute-start.3
  33.2 0.0 copy-start.2
  33.2 1.3 %copy-done.2 = bf16[6,128,768]{2,1,0:T(8,128)(2,1)S(1)} copy-done((bf16[6,128,768]{2,1,0:T(8,128)(2,1)S(1)}, bf16[6,128,768]{2,1,0:T(8,128)(2,1)}, u32[]{:S(2)}) %copy-start.2) | copy-done | bytes 1179672
  34.5 1.1 %copy-done.3 = bf16[768,384]{1,0:T(8,128)(2,1)S(1)} copy-done((bf16[768,384]{1,0:T(8,128)(2,1)S(1)}, bf16[768,384]{1,0:T(8,128)(2,1)}, u32[]{:S(2)}) %copy-start.3) | copy-done | bytes 589848
  35.5 3.0 %shard_map.73 = (bf16[3,128,768]{2,1,0:T(8,128)(2,1)S(1)}, f32[2,3,128,128]{3,2,1,0:T(8,128)S(1)}, bf16[2,3,128,768]{3,2,1,0:T(8,128)(2,1)S(1)}) custom-call(s32[6]{0:T(128)S(1)} %pad_add_fusion.order, f32[6]{0:T(128)S(1)} %multiply_multiply_fusion.factor, bf16[6,128,768]{2,1,0:T(8,128)(2,1)S(1)} %copy-done.2, bf16[768,384]{1,0:T(8,128)(2,1)S(1)} %copy-done.3, ...), custom_call_target="tpu_custom_call" | custom-call | flops 1509949440 | bytes 2949168 | tf_op jit(solution)/shard_map/pallas_call | solution.py:31
  38.6 0.0 collective-permute-done.16.refs_6_
  38.6 1.6 %collective-permute-start.7 = (s32[2,128]{1,0:T(2,128)S(1)}, s32[2,128]{1,0:T(2,128)S(1)}, u32[]{:S(2)}, u32[]{:S(2)}) collective-permute-start(s32[2,128]{1,0:T(2,128)S(1)} %collective-permute-done.6.refs_6_), channel_id=1, source_target_pairs={{0,4},{4,8},{8,12},{12,0},{1,5},{5,9},{9,13},{13,1},{2,6},{6,10},{... | collective-permute-start | bytes 3080 | tf_op jit(solution)/shard_map/ppermute | solution.py:20
  40.2 0.0 collective-permute-done.11.refs_3_
  40.2 0.0 collective-permute-start.12
  40.2 4.8 %collective-permute-done.3.refs_3_ = bf16[3,64,768]{2,1,0:T(8,128)(2,1)S(1)} collective-permute-done((bf16[3,64,768]{2,1,0:T(8,128)(2,1)S(1)}, bf16[3,64,768]{2,1,0:T(8,128)(2,1)S(1)}, u32[]{:S(2)}, u32[]{:S(2)}) %collective-permute-start.3) | collective-permute-done | bytes 294944 | tf_op jit(solution)/shard_map/ppermute | solution.py:20
  45.0 0.0 collective-permute-start.4
  45.0 1.8 %shard_map.76 = (f32[2,3,128,128]{3,2,1,0:T(8,128)S(1)}, bf16[2,3,128,768]{3,2,1,0:T(8,128)(2,1)S(1)}) custom-call(bf16[3,128,768]{2,1,0:T(8,128)(2,1)S(1)} %get-tuple-element.24.refs_0_, bf16[768,384]{1,0:T(8,128)(2,1)S(1)} %copy-done, bf16[768,384]{1,0:T(8,128)(2,1)S(1)} %copy-done.1, bf16[3,64,768]{2,1,0:T(8,128)(2,1)S(1)} %collective-permute-done.9.refs_3_, ...), custom_call_target="tpu_custom_call" | custom-call | flops 1056964608 | bytes 2949120 | tf_op jit(solution)/shard_map/pallas_call | solution.py:31
  46.8 0.0 collective-permute-done.18.refs_4_
  46.8 1.6 %collective-permute-start.14 = (f32[2,3,128,128]{3,2,1,0:T(8,128)S(1)}, f32[2,3,128,128]{3,2,1,0:T(8,128)S(1)}, u32[]{:S(2)}, u32[]{:S(2)}) collective-permute-start(f32[2,3,128,128]{3,2,1,0:T(8,128)S(1)} %get-tuple-element.29.refs_0_), channel_id=1, source_target_pairs={{0,2},{2,0},{1,3},{3,1},{4,6},{6,4},{5,7},{7,5},{8,10},{10,8},{9,1... | collective-permute-start | bytes 1179656 | tf_op jit(solution)/shard_map/ppermute | solution.py:20
  48.3 0.0 collective-permute-done.19.refs_6_
  48.3 0.5 collective-permute-start.17
  48.9 1.7 %shard_map.77 = (f32[2,3,128,128]{3,2,1,0:T(8,128)S(1)}, bf16[2,3,128,768]{3,2,1,0:T(8,128)(2,1)S(1)}) custom-call(bf16[3,128,768]{2,1,0:T(8,128)(2,1)S(1)} %get-tuple-element.24.refs_0_, bf16[768,384]{1,0:T(8,128)(2,1)S(1)} %copy-done, bf16[768,384]{1,0:T(8,128)(2,1)S(1)} %copy-done.1, bf16[3,64,768]{2,1,0:T(8,128)(2,1)S(1)} %collective-permute-done.10.refs_3_, ...), custom_call_target="tpu_custom_call" | custom-call | flops 1056964608 | bytes 2949120 | tf_op jit(solution)/shard_map/pallas_call | solution.py:31
  50.6 0.0 collective-permute-done.7.refs_10_
  50.6 1.6 %collective-permute-start.20 = (f32[2,3,128,128]{3,2,1,0:T(8,128)S(1)}, f32[2,3,128,128]{3,2,1,0:T(8,128)S(1)}, u32[]{:S(2)}, u32[]{:S(2)}) collective-permute-start(f32[2,3,128,128]{3,2,1,0:T(8,128)S(1)} %get-tuple-element.33.refs_8_), channel_id=1, source_target_pairs={{0,2},{2,0},{1,3},{3,1},{4,6},{6,4},{5,7},{7,5},{8,10},{10,8},{9,1... | collective-permute-start | bytes 1179656 | tf_op jit(solution)/shard_map/ppermute | solution.py:20
  52.2 0.1 constant_dynamic-slice_fusion
  52.2 0.0 collective-permute-done.12.refs_4_
  52.3 0.2 collective-permute-start.8
  52.5 0.9 %shard_map.75 = (f32[1,3,128,128]{3,2,1,0:T(8,128)S(1)}, bf16[1,3,128,768]{3,2,1,0:T(8,128)(2,1)S(1)}) custom-call(bf16[3,128,768]{2,1,0:T(8,128)(2,1)S(1)} %get-tuple-element.24.refs_0_, bf16[768,384]{1,0:T(8,128)(2,1)S(1)} %copy-done, bf16[768,384]{1,0:T(8,128)(2,1)S(1)} %copy-done.1, bf16[3,64,768]{2,1,0:T(8,128)(2,1)S(1)} %collective-permute-done.11.refs_3_, ...), custom_call_target="tpu_custom_call" | custom-call | flops 528482304 | bytes 2359296 | tf_op jit(solution)/shard_map/pallas_call | solution.py:31
  53.5 0.0 collective-permute-done.4.refs_4_
  53.5 0.6 collective-permute-start.13
  54.1 0.9 %shard_map.74 = (f32[1,3,128,128]{3,2,1,0:T(8,128)S(1)}, bf16[1,3,128,768]{3,2,1,0:T(8,128)(2,1)S(1)}) custom-call(bf16[3,128,768]{2,1,0:T(8,128)(2,1)S(1)} %get-tuple-element.24.refs_0_, bf16[768,384]{1,0:T(8,128)(2,1)S(1)} %copy-done, bf16[768,384]{1,0:T(8,128)(2,1)S(1)} %copy-done.1, bf16[3,64,768]{2,1,0:T(8,128)(2,1)S(1)} %collective-permute-done.3.refs_3_, ...), custom_call_target="tpu_custom_call" | custom-call | flops 528482304 | bytes 2359296 | tf_op jit(solution)/shard_map/pallas_call | solution.py:31
  55.0 2.8 %collective-permute-done.8 = s32[2,128]{1,0:T(2,128)S(1)} collective-permute-done((s32[2,128]{1,0:T(2,128)S(1)}, s32[2,128]{1,0:T(2,128)S(1)}, u32[]{:S(2)}, u32[]{:S(2)}) %collective-permute-start.8) | collective-permute-done | bytes 1056 | tf_op jit(solution)/shard_map/ppermute | solution.py:20
  57.9 0.5 collective-permute-start.5
  58.4 0.4 collective-permute-done.14.refs_1_
  58.8 8.4 %collective-permute-done.17.refs_5_ = f32[2,3,128,128]{3,2,1,0:T(8,128)S(1)} collective-permute-done((f32[2,3,128,128]{3,2,1,0:T(8,128)S(1)}, f32[2,3,128,128]{3,2,1,0:T(8,128)S(1)}, u32[]{:S(2)}, u32[]{:S(2)}) %collective-permute-start.17) | collective-permute-done | bytes 393248 | tf_op jit(solution)/shard_map/ppermute | solution.py:20
  67.3 8.4 %collective-permute-done.20.refs_9_ = f32[2,3,128,128]{3,2,1,0:T(8,128)S(1)} collective-permute-done((f32[2,3,128,128]{3,2,1,0:T(8,128)S(1)}, f32[2,3,128,128]{3,2,1,0:T(8,128)S(1)}, u32[]{:S(2)}, u32[]{:S(2)}) %collective-permute-start.20) | collective-permute-done | bytes 393248 | tf_op jit(solution)/shard_map/ppermute | solution.py:20
  75.7 0.8 shard_map.78
  76.5 3.4 %collective-permute-done.13.refs_1_ = f32[1,3,128,128]{3,2,1,0:T(8,128)S(1)} collective-permute-done((f32[1,3,128,128]{3,2,1,0:T(8,128)S(1)}, f32[1,3,128,128]{3,2,1,0:T(8,128)S(1)}, u32[]{:S(2)}, u32[]{:S(2)}) %collective-permute-start.13) | collective-permute-done | bytes 196640 | tf_op jit(solution)/shard_map/ppermute | solution.py:20
  79.9 0.4 shard_map.79
  80.3 3.3 %collective-permute-done.5.refs_1_ = f32[1,3,128,128]{3,2,1,0:T(8,128)S(1)} collective-permute-done((f32[1,3,128,128]{3,2,1,0:T(8,128)S(1)}, f32[1,3,128,128]{3,2,1,0:T(8,128)S(1)}, u32[]{:S(2)}, u32[]{:S(2)}) %collective-permute-start.5) | collective-permute-done | bytes 196640 | tf_op jit(solution)/shard_map/ppermute | solution.py:20
  83.6 1.5 %shard_map.80 = (bf16[6,128,384]{2,1,0:T(8,128)(2,1)S(1)}, bf16[6,128,384]{2,1,0:T(8,128)(2,1)S(1)}) custom-call(s32[6]{0:T(128)S(1)} %pad_add_fusion.order, f32[1,3,128,128]{3,2,1,0:T(8,128)S(1)} %get-tuple-element.25.refs_0_, f32[1,3,128,128]{3,2,1,0:T(8,128)S(1)} %collective-permute-done.5.refs_1_, s32[1,128]{1,0:T(1,128)S(1)} %get-tuple-element.48.refs_2_, ...), custom_call_target="tpu_custom_call" | custom-call | flops 301989888 | bytes 2851352 | tf_op jit(solution)/shard_map/pallas_call | solution.py:31
  85.1 0.1 collective-permute-start.21
  85.2 1.1 %shard_map.81 = f32[6,128,384]{2,1,0:T(8,128)S(1)} custom-call(s32[6]{0:T(128)S(1)} %pad_add_fusion.order, bf16[6,128,384]{2,1,0:T(8,128)(2,1)S(1)} %get-tuple-element.41.attended, bf16[384,384]{1,0:T(8,128)(2,1)S(1)} %get-tuple-element.45.w_own), custom_call_target="tpu_custom_call" | custom-call | flops 226492416 | bytes 884760 | tf_op jit(solution)/shard_map/pallas_call | solution.py:31
  86.3 0.9 %collective-permute-done.21 = bf16[6,128,384]{2,1,0:T(8,128)(2,1)S(1)} collective-permute-done((bf16[6,128,384]{2,1,0:T(8,128)(2,1)S(1)}, bf16[6,128,384]{2,1,0:T(8,128)(2,1)S(1)}, u32[]{:S(2)}, u32[]{:S(2)}) %collective-permute-start.21) | collective-permute-done | bytes 589856 | tf_op jit(solution)/shard_map/ppermute | solution.py:20
  87.2 1.0 %add_convert_fusion = bf16[6,128,384]{2,1,0:T(8,128)(2,1)} fusion(f32[6,128,384]{2,1,0:T(8,128)S(1)} %shard_map.81, bf16[6,128,384]{2,1,0:T(8,128)(2,1)S(1)} %collective-permute-done.21), kind=kLoop, calls=%fused_computation | loop fusion | flops 884736 | bytes 2359296 | tf_op jit(solution)/shard_map/convert_element_type | solution.py:309
  (17 shorter events, 0.0 us)
Async XLA Ops:
  0.0 5.9 %copy-start.6 = (s32[6]{0:T(128)S(1)}, s32[6]{0:T(128)}, u32[]{:S(2)}) copy-start(s32[6]{0:T(128)} %param.8) | copy-start | bytes 76
  0.0 8.8 %copy-start.5 = (s32[128]{0:T(128)S(1)}, s32[128]{0:T(128)}, u32[]{:S(2)}) copy-start(s32[128]{0:T(128)} %param.9) | copy-start | bytes 1540
  0.0 33.2 %copy-start = (bf16[768,384]{1,0:T(8,128)(2,1)S(1)}, bf16[768,384]{1,0:T(8,128)(2,1)}, u32[]{:S(2)}) copy-start(bf16[768,384]{1,0:T(8,128)(2,1)} %refs_1_.7) | copy-start | bytes 1769476
  0.0 33.2 %copy-start.1 = (bf16[768,384]{1,0:T(8,128)(2,1)S(1)}, bf16[768,384]{1,0:T(8,128)(2,1)}, u32[]{:S(2)}) copy-start(bf16[768,384]{1,0:T(8,128)(2,1)} %refs_2_.7) | copy-start | bytes 1769476
  1.2 13.0 %collective-permute-start.9 = (bf16[3,64,768]{2,1,0:T(8,128)(2,1)S(1)}, bf16[3,64,768]{2,1,0:T(8,128)(2,1)S(1)}, u32[]{:S(2)}, u32[]{:S(2)}) collective-permute-start(bf16[3,64,768]{2,1,0:T(8,128)(2,1)S(1)} %get-tuple-element.43), channel_id=1, source_target_pairs={{0,4},{4,8},{8,12},{12,0},{1,5},{5,9},{9,13},{13,1},{2,6},{6,10},{... | collective-permute-start | bytes 884744 | tf_op jit(solution)/shard_map/ppermute | solution.py:20
  4.3 16.2 %collective-permute-start.1 = (bf16[3,64,768]{2,1,0:T(8,128)(2,1)S(1)}, bf16[3,64,768]{2,1,0:T(8,128)(2,1)S(1)}, u32[]{:S(2)}, u32[]{:S(2)}) collective-permute-start(bf16[3,64,768]{2,1,0:T(8,128)(2,1)S(1)} %get-tuple-element.44), channel_id=1, source_target_pairs={{0,4},{4,8},{8,12},{12,0},{1,5},{5,9},{9,13},{13,1},{2,6},{6,10},{... | collective-permute-start | bytes 884744 | tf_op jit(solution)/shard_map/ppermute | solution.py:20
  7.2 13.4 %collective-permute-start = (f32[8,128]{1,0:T(8,128)S(1)}, f32[8,128]{1,0:T(8,128)S(1)}, u32[]{:S(2)}, u32[]{:S(2)}) collective-permute-start(f32[8,128]{1,0:T(8,128)S(1)} %broadcast_in_dim.3), channel_id=1, source_target_pairs={{0,2},{2,0},{1,3},{3,1},{4,6},{6,4},{5,7},{7,5},{8,10},{10,8},{9,1... | collective-permute-start | bytes 12296 | tf_op jit(solution)/shard_map/ppermute | solution.py:20
  8.9 17.9 %collective-permute-start.6 = (s32[2,128]{1,0:T(2,128)S(1)}, s32[2,128]{1,0:T(2,128)S(1)}, u32[]{:S(2)}, u32[]{:S(2)}) collective-permute-start(s32[2,128]{1,0:T(2,128)S(1)} %tile.12.refs_2_), channel_id=1, source_target_pairs={{0,4},{4,8},{8,12},{12,0},{1,5},{5,9},{9,13},{13,1},{2,6},{6,10},{... | collective-permute-start | bytes 3080 | tf_op jit(solution)/shard_map/ppermute | solution.py:20
  14.2 12.7 %collective-permute-start.10 = (bf16[3,64,768]{2,1,0:T(8,128)(2,1)S(1)}, bf16[3,64,768]{2,1,0:T(8,128)(2,1)S(1)}, u32[]{:S(2)}, u32[]{:S(2)}) collective-permute-start(bf16[3,64,768]{2,1,0:T(8,128)(2,1)S(1)} %collective-permute-done.9.refs_3_), channel_id=1, source_target_pairs={{0,4},{4,8},{8,12},{12,0},{1,5},{5,9},{9,13},{13,1},{2,6},{6,10},{... | collective-permute-start | bytes 884744 | tf_op jit(solution)/shard_map/ppermute | solution.py:20
  14.2 18.7 %collective-permute-start.15 = (bf16[3,64,768]{2,1,0:T(8,128)(2,1)S(1)}, bf16[3,64,768]{2,1,0:T(8,128)(2,1)S(1)}, u32[]{:S(2)}, u32[]{:S(2)}) collective-permute-start(bf16[3,64,768]{2,1,0:T(8,128)(2,1)S(1)} %collective-permute-done.9.refs_3_), channel_id=1, source_target_pairs={{0,1},{1,0},{2,3},{3,2},{4,5},{5,4},{6,7},{7,6},{8,9},{9,8},{10,11... | collective-permute-start | bytes 884744 | tf_op jit(solution)/shard_map/ppermute | solution.py:20
  20.5 12.4 %collective-permute-start.2 = (bf16[3,64,768]{2,1,0:T(8,128)(2,1)S(1)}, bf16[3,64,768]{2,1,0:T(8,128)(2,1)S(1)}, u32[]{:S(2)}, u32[]{:S(2)}) collective-permute-start(bf16[3,64,768]{2,1,0:T(8,128)(2,1)S(1)} %collective-permute-done.1.refs_5_), channel_id=1, source_target_pairs={{0,4},{4,8},{8,12},{12,0},{1,5},{5,9},{9,13},{13,1},{2,6},{6,10},{... | collective-permute-start | bytes 884744 | tf_op jit(solution)/shard_map/ppermute | solution.py:20
  21.8 16.7 %collective-permute-start.16 = (bf16[3,64,768]{2,1,0:T(8,128)(2,1)S(1)}, bf16[3,64,768]{2,1,0:T(8,128)(2,1)S(1)}, u32[]{:S(2)}, u32[]{:S(2)}) collective-permute-start(bf16[3,64,768]{2,1,0:T(8,128)(2,1)S(1)} %collective-permute-done.1.refs_5_), channel_id=1, source_target_pairs={{0,1},{1,0},{2,3},{3,2},{4,5},{5,4},{6,7},{7,6},{8,9},{9,8},{10,11... | collective-permute-start | bytes 884744 | tf_op jit(solution)/shard_map/ppermute | solution.py:20
  26.9 19.9 %collective-permute-start.18 = (bf16[3,64,768]{2,1,0:T(8,128)(2,1)S(1)}, bf16[3,64,768]{2,1,0:T(8,128)(2,1)S(1)}, u32[]{:S(2)}, u32[]{:S(2)}) collective-permute-start(bf16[3,64,768]{2,1,0:T(8,128)(2,1)S(1)} %collective-permute-done.10.refs_3_), channel_id=1, source_target_pairs={{0,1},{1,0},{2,3},{3,2},{4,5},{5,4},{6,7},{7,6},{8,9},{9,8},{10,11... | collective-permute-start | bytes 884744 | tf_op jit(solution)/shard_map/ppermute | solution.py:20
  26.9 13.3 %collective-permute-start.11 = (bf16[3,64,768]{2,1,0:T(8,128)(2,1)S(1)}, bf16[3,64,768]{2,1,0:T(8,128)(2,1)S(1)}, u32[]{:S(2)}, u32[]{:S(2)}) collective-permute-start(bf16[3,64,768]{2,1,0:T(8,128)(2,1)S(1)} %collective-permute-done.10.refs_3_), channel_id=1, source_target_pairs={{0,4},{4,8},{8,12},{12,0},{1,5},{5,9},{9,13},{13,1},{2,6},{6,10},{... | collective-permute-start | bytes 884744 | tf_op jit(solution)/shard_map/ppermute | solution.py:20
  32.9 15.4 %collective-permute-start.19 = (bf16[3,64,768]{2,1,0:T(8,128)(2,1)S(1)}, bf16[3,64,768]{2,1,0:T(8,128)(2,1)S(1)}, u32[]{:S(2)}, u32[]{:S(2)}) collective-permute-start(bf16[3,64,768]{2,1,0:T(8,128)(2,1)S(1)} %collective-permute-done.2.refs_5_), channel_id=1, source_target_pairs={{0,1},{1,0},{2,3},{3,2},{4,5},{5,4},{6,7},{7,6},{8,9},{9,8},{10,11... | collective-permute-start | bytes 884744 | tf_op jit(solution)/shard_map/ppermute | solution.py:20
  32.9 12.1 %collective-permute-start.3 = (bf16[3,64,768]{2,1,0:T(8,128)(2,1)S(1)}, bf16[3,64,768]{2,1,0:T(8,128)(2,1)S(1)}, u32[]{:S(2)}, u32[]{:S(2)}) collective-permute-start(bf16[3,64,768]{2,1,0:T(8,128)(2,1)S(1)} %collective-permute-done.2.refs_5_), channel_id=1, source_target_pairs={{0,4},{4,8},{8,12},{12,0},{1,5},{5,9},{9,13},{13,1},{2,6},{6,10},{... | collective-permute-start | bytes 884744 | tf_op jit(solution)/shard_map/ppermute | solution.py:20
  33.2 1.3 %copy-start.2 = (bf16[6,128,768]{2,1,0:T(8,128)(2,1)S(1)}, bf16[6,128,768]{2,1,0:T(8,128)(2,1)}, u32[]{:S(2)}) copy-start(bf16[6,128,768]{2,1,0:T(8,128)(2,1)} %tokens.1) | copy-start | bytes 3538948
  34.5 1.1 %copy-start.3 = (bf16[768,384]{1,0:T(8,128)(2,1)S(1)}, bf16[768,384]{1,0:T(8,128)(2,1)}, u32[]{:S(2)}) copy-start(bf16[768,384]{1,0:T(8,128)(2,1)} %w_query.1) | copy-start | bytes 1769476
  38.6 12.1 %collective-permute-start.7 = (s32[2,128]{1,0:T(2,128)S(1)}, s32[2,128]{1,0:T(2,128)S(1)}, u32[]{:S(2)}, u32[]{:S(2)}) collective-permute-start(s32[2,128]{1,0:T(2,128)S(1)} %collective-permute-done.6.refs_6_), channel_id=1, source_target_pairs={{0,4},{4,8},{8,12},{12,0},{1,5},{5,9},{9,13},{13,1},{2,6},{6,10},{... | collective-permute-start | bytes 3080 | tf_op jit(solution)/shard_map/ppermute | solution.py:20
  40.2 12.1 %collective-permute-start.12 = (bf16[3,64,768]{2,1,0:T(8,128)(2,1)S(1)}, bf16[3,64,768]{2,1,0:T(8,128)(2,1)S(1)}, u32[]{:S(2)}, u32[]{:S(2)}) collective-permute-start(bf16[3,64,768]{2,1,0:T(8,128)(2,1)S(1)} %collective-permute-done.11.refs_3_), channel_id=1, source_target_pairs={{0,1},{1,0},{2,3},{3,2},{4,5},{5,4},{6,7},{7,6},{8,9},{9,8},{10,11... | collective-permute-start | bytes 884744 | tf_op jit(solution)/shard_map/ppermute | solution.py:20
  45.0 8.5 %collective-permute-start.4 = (bf16[3,64,768]{2,1,0:T(8,128)(2,1)S(1)}, bf16[3,64,768]{2,1,0:T(8,128)(2,1)S(1)}, u32[]{:S(2)}, u32[]{:S(2)}) collective-permute-start(bf16[3,64,768]{2,1,0:T(8,128)(2,1)S(1)} %collective-permute-done.3.refs_3_), channel_id=1, source_target_pairs={{0,1},{1,0},{2,3},{3,2},{4,5},{5,4},{6,7},{7,6},{8,9},{9,8},{10,11... | collective-permute-start | bytes 884744 | tf_op jit(solution)/shard_map/ppermute | solution.py:20
  46.8 12.1 %collective-permute-start.14 = (f32[2,3,128,128]{3,2,1,0:T(8,128)S(1)}, f32[2,3,128,128]{3,2,1,0:T(8,128)S(1)}, u32[]{:S(2)}, u32[]{:S(2)}) collective-permute-start(f32[2,3,128,128]{3,2,1,0:T(8,128)S(1)} %get-tuple-element.29.refs_0_), channel_id=1, source_target_pairs={{0,2},{2,0},{1,3},{3,1},{4,6},{6,4},{5,7},{7,5},{8,10},{10,8},{9,1... | collective-permute-start | bytes 1179656 | tf_op jit(solution)/shard_map/ppermute | solution.py:20
  48.3 3.9 %copy-start.4 = (bf16[384,768]{1,0:T(8,128)(2,1)S(1)}, bf16[384,768]{1,0:T(8,128)(2,1)}, u32[]{:S(2)}) copy-start(bf16[384,768]{1,0:T(8,128)(2,1)} %param.13) | copy-start | bytes 1769476
  48.3 18.9 %collective-permute-start.17 = (f32[2,3,128,128]{3,2,1,0:T(8,128)S(1)}, f32[2,3,128,128]{3,2,1,0:T(8,128)S(1)}, u32[]{:S(2)}, u32[]{:S(2)}) collective-permute-start(f32[2,3,128,128]{3,2,1,0:T(8,128)S(1)} %get-tuple-element.31.refs_4_), channel_id=1, source_target_pairs={{0,2},{2,0},{1,3},{3,1},{4,6},{6,4},{5,7},{7,5},{8,10},{10,8},{9,1... | collective-permute-start | bytes 1179656 | tf_op jit(solution)/shard_map/ppermute | solution.py:20
  50.6 25.1 %collective-permute-start.20 = (f32[2,3,128,128]{3,2,1,0:T(8,128)S(1)}, f32[2,3,128,128]{3,2,1,0:T(8,128)S(1)}, u32[]{:S(2)}, u32[]{:S(2)}) collective-permute-start(f32[2,3,128,128]{3,2,1,0:T(8,128)S(1)} %get-tuple-element.33.refs_8_), channel_id=1, source_target_pairs={{0,2},{2,0},{1,3},{3,1},{4,6},{6,4},{5,7},{7,5},{8,10},{10,8},{9,1... | collective-permute-start | bytes 1179656 | tf_op jit(solution)/shard_map/ppermute | solution.py:20
  52.3 5.6 %collective-permute-start.8 = (s32[2,128]{1,0:T(2,128)S(1)}, s32[2,128]{1,0:T(2,128)S(1)}, u32[]{:S(2)}, u32[]{:S(2)}) collective-permute-start(s32[2,128]{1,0:T(2,128)S(1)} %collective-permute-done.7.refs_10_), channel_id=1, source_target_pairs={{0,4},{4,8},{8,12},{12,0},{1,5},{5,9},{9,13},{13,1},{2,6},{6,10},{... | collective-permute-start | bytes 3080 | tf_op jit(solution)/shard_map/ppermute | solution.py:20
  53.5 26.4 %collective-permute-start.13 = (f32[1,3,128,128]{3,2,1,0:T(8,128)S(1)}, f32[1,3,128,128]{3,2,1,0:T(8,128)S(1)}, u32[]{:S(2)}, u32[]{:S(2)}) collective-permute-start(f32[1,3,128,128]{3,2,1,0:T(8,128)S(1)} %get-tuple-element.27.refs_0_), channel_id=1, source_target_pairs={{0,2},{2,0},{1,3},{3,1},{4,6},{6,4},{5,7},{7,5},{8,10},{10,8},{9,1... | collective-permute-start | bytes 589832 | tf_op jit(solution)/shard_map/ppermute | solution.py:20
  57.9 25.8 %collective-permute-start.5 = (f32[1,3,128,128]{3,2,1,0:T(8,128)S(1)}, f32[1,3,128,128]{3,2,1,0:T(8,128)S(1)}, u32[]{:S(2)}, u32[]{:S(2)}) collective-permute-start(f32[1,3,128,128]{3,2,1,0:T(8,128)S(1)} %get-tuple-element.25.refs_0_), channel_id=1, source_target_pairs={{0,2},{2,0},{1,3},{3,1},{4,6},{6,4},{5,7},{7,5},{8,10},{10,8},{9,1... | collective-permute-start | bytes 589832 | tf_op jit(solution)/shard_map/ppermute | solution.py:20
  85.1 2.1 %collective-permute-start.21 = (bf16[6,128,384]{2,1,0:T(8,128)(2,1)S(1)}, bf16[6,128,384]{2,1,0:T(8,128)(2,1)S(1)}, u32[]{:S(2)}, u32[]{:S(2)}) collective-permute-start(bf16[6,128,384]{2,1,0:T(8,128)(2,1)S(1)} %get-tuple-element.42), channel_id=1, source_target_pairs={{0,1},{1,0},{2,3},{3,2},{4,5},{5,4},{6,7},{7,6},{8,9},{9,8},{10,11... | collective-permute-start | bytes 1769480 | tf_op jit(solution)/shard_map/ppermute | solution.py:20

commit v2 on v1

--- a/solution.py
+++ b/solution.py
@@ -8,9 +8,11 @@
 from jax.experimental.pallas import tpu as pltpu
 from jax.sharding import PartitionSpec as P
 
+
 HEAD_DIM = 64
 LANES = 128
 PER_TILE = LANES // HEAD_DIM
+CHUNKS = 2
 MASKED = -1000000000.0
 VMEM_LIMIT = 24 * 1024 * 1024
 
@@ -95,14 +97,20 @@
             logits[chunk, tile] = dot_nt(query[tile], keys[0, tile])
 
 
-def own_kernel(order, factor, tokens, w_query, w_key, w_value, query, logits, values, keys):
-    rows, cells, width = tokens.shape
+def own_kernel(order, *refs):
+    counts, refs = refs[:-8], refs[-8:]
+    tokens, w_query, w_key, w_value, query, logits, values, keys = refs
+    rows, cells, _ = tokens.shape
     chunks = logits.shape[0]
     part = cells // chunks
+    total = sum(count[row] for count in counts for row in range(rows))
+    scale = lax.rsqrt(jnp.full((1, query.shape[0] * LANES), total, jnp.int32).astype(jnp.float32))
     for row in range(rows):
         source = order[row]
         block = tokens[source]
-        scaled = (dot(block, w_query[...]) * factor[source]).astype(jnp.bfloat16)
+        count = jnp.full(scale.shape, counts[0][source], jnp.int32).astype(jnp.float32)
+        factor = count * scale / math.sqrt(HEAD_DIM)
+        scaled = (dot(block, w_query[...]) * factor).astype(jnp.bfloat16)
         for tile in range(query.shape[0]):
             query[tile, :, row * LANES : (row + 1) * LANES] = scaled[:, tile * LANES : (tile + 1) * LANES]
         key = dot(block, w_key[...]).astype(jnp.bfloat16)
@@ -161,9 +169,9 @@
     units, refs = read_units(refs, sizes)
     state = refs[:3] if carried else None
     w_send, attended, sent = refs[-3:]
-    rows, cells, _ = attended.shape
+    rows, _, _ = attended.shape
     for tile in range(attended.shape[2] // LANES):
-        top, denom, accum = absorb(units, state, tile, rows)
+        _, denom, accum = absorb(units, state, tile, rows)
         denom = per_head(denom, sum_over)
         for row in range(rows):
             part = accum[:, row * LANES : (row + 1) * LANES] / denom
@@ -187,6 +195,7 @@
     core = lax.axis_index("head")
     part = HEAD_DIM
     chunks = cells // part
+    assert chunks == CHUNKS
     share = rows // cores
     assert share * cores == rows and chunks * part == cells and tiles * LANES == inner
     f32, bf16 = jnp.float32, jnp.bfloat16
@@ -203,12 +212,9 @@
         [(core - k) % cores * share + jnp.arange(share, dtype=jnp.int32) for k in range(cores)]
     )
 
-    total = jnp.full((8, LANES), jnp.sum(weights).astype(f32))
-    passing = total
-    for _ in range(holders - 1):
-        passing = ring(passing, "seq")
-        total = total + passing
-    factor = weights.astype(f32) * lax.rsqrt(total[0, 0]) / math.sqrt(HEAD_DIM)
+    counts = [weights]
+    for k in range(1, holders):
+        counts.append(ring(weights, "seq", k))
 
     def exchange(logits):
         return [logits] + [ring(logits, "seq", k) for k in range(1, holders)]
@@ -222,33 +228,32 @@
             shape((chunks, tiles, cells, depth), f32),
             shape((chunks, tiles, depth, spans), bf16),
         ],
-        [order, factor, tokens, w_query, w_key, w_value],
+        [order] + counts + [tokens, w_query, w_key, w_value],
         2 * rows * cells * inner * (3 * width + cells * PER_TILE),
-        scalars=2,
-        scratch=[pltpu.VMEM((chunks, tiles, depth, spans), bf16)],
+        1 + holders,
+        [pltpu.VMEM((chunks, tiles, depth, spans), bf16)],
     )
     units = [(exchange(logits), mask, values)]
 
-    def project(pieces, count):
+    def project(pieces):
         return call(
-            functools.partial(project_kernel, chunks=count, pieces=cores),
-            [shape((count, tiles, cells, depth), f32), shape((count, tiles, depth, spans), bf16)],
+            functools.partial(project_kernel, chunks=1, pieces=cores),
+            [shape((1, tiles, cells, depth), f32), shape((1, tiles, depth, spans), bf16)],
             [query, w_key, w_value] + pieces,
-            2 * rows * part * count * inner * (2 * width + cells * PER_TILE),
-            scratch=[pltpu.VMEM((1, tiles, depth, spans), bf16)],
+            2 * rows * part * inner * (2 * width + cells * PER_TILE),
+            0,
+            [pltpu.VMEM((1, tiles, depth, spans), bf16)],
         )
 
-    for step in range(1, blocks):
-        moving = [ring(piece, "res") for piece in moving]
+    for _ in range(1, blocks):
+        moving = [ring(moving[k], "res") for k in range(chunks)]
         mask = ring(mask, "res")
-        pieces = [[piece] + [ring(piece, "head", k) for k in range(1, cores)] for piece in moving]
-        if step < blocks - 1:
-            logits, values = project(sum(pieces, []), chunks)
-            units.append((exchange(logits), mask, values))
-        else:
-            for k in range(chunks):
-                logits, values = project(pieces[k], 1)
-                units.append((exchange(logits), mask[k : k + 1], values))
+        for k in range(chunks):
+            pieces = [moving[k]]
+            for j in range(1, cores):
+                pieces.append(ring(moving[k], "head", j))
+            logits, values = project(pieces)
+            units.append((exchange(logits), mask[k : k + 1], values))
 
     state = []
     state_shape = [
@@ -263,11 +268,7 @@
     def work(group):
         return sum(2 * u[0][0].size * spans for u in group)
 
-    groups = []
-    early = units[: len(units) - chunks] if blocks > 1 else []
-    for at in range(0, len(early), 3):
-        groups.append(early[at : at + 3])
-    groups += [[unit] for unit in units[len(early) :]]
+    groups = [units[at : at + 3] for at in range(0, len(units) - 1, 3)] + [units[-1:]]
     for group in groups[:-1]:
         state = call(
             functools.partial(absorb_kernel, sizes=[len(u[0]) for u in group], carried=bool(state)),
@@ -286,7 +287,7 @@
         [shape((rows, cells, inner), bf16), shape((rows, cells, columns), bf16)],
         [order] + flatten(group) + list(state) + [outs[1 % cores]],
         work(group) + 2 * rows * cells * inner * columns,
-        scalars=1,
+        1,
     )
 
     def output(w):
@@ -295,7 +296,7 @@
             shape((rows, cells, columns), f32),
             [order, attended, w],
             2 * rows * cells * inner * columns,
-            scalars=1,
+            1,
         )
 
     if cores == 1:
@@ -320,4 +321,5 @@
         P("head", None),
     )
     out_specs = P(("grp", "seq"), "res", "head")
+
     return jax.shard_map(shards, mesh=mesh, in_specs=in_specs, out_specs=out_specs, check_vma=False)

time: 88.4 us -> 85.3 us (0.965)
  waiting for transfers between devices: 53.5 us -> 47.6 us
  starting transfers between devices: 14.9 us -> 19 us
  between operations: 1.53 us -> 0.22 us
    ppermute x22 -> x24, waiting for transfers between devices: 53.5 us -> 47.6 us  [ring(): lax.ppermute(value, axis, [(i, (i + by) % length) for i in range(length)])]
    ppermute x22 -> x24, starting transfers between devices: 14.9 us -> 19 us  [ring(): lax.ppermute(value, axis, [(i, (i + by) % length) for i in range(length)])]
    unnamed x14 -> x12, local copies, waits for them, and re-layouts: 2.35 us -> 1.08 us
    dynamic_slice x1, local copies, waits for them, and re-layouts: 0.06 us -> 1.11 us  [shards(): lax.dynamic_slice(w_out, (0, (core + k) % cores * columns), (inner, colum...]
    pallas_call x9 -> x11, Pallas kernels: 12.2 us -> 12.4 us  [call(): pl.pallas_call(kernel, out_shape=out_shape, in_specs=specs, out_specs=who...]
  transfers between devices with their start and end apart: 22 -> 24, of which waited for: 12 -> 13; matrix products, arithmetic and copies ran while one was open for 2% -> 3% of each run, Pallas kernels for 12% -> 13%
where the time goes in v2:
time: 85.3 us; the launch traced here: 85.1 us
  waiting for transfers between devices  47.6 us (56%)
  starting transfers between devices  19 us (22%)
  Pallas kernels  12.4 us (15%)
  local copies, waits for them, and re-layouts  3.62 us (4%)
  other arithmetic  2.3 us (3%)
    ppermute x24, waiting for transfers between devices, ring(): lax.ppermute(value, axis, [(i, (i + by) % length) for i in range(length)])  47.6 us
    ppermute x24, starting transfers between devices, ring(): lax.ppermute(value, axis, [(i, (i + by) % length) for i in range(length)])  19 us
    pallas_call x11, Pallas kernels, call(): pl.pallas_call(kernel, out_shape=out_shape, in_specs=specs, out_specs=who...  12.4 us
  transfers between devices with their start and end apart: 24, of which 13 were waited for; matrix products, arithmetic and copies ran while one was open for 3% of the time, Pallas kernels for 13%

profile of v2, /device:TPU:0, one launch (start us, length us, event | category | flops | bytes accessed | tf_op | source)
XLA Modules:
  0.0 85.1 jit_solution(17094404052583984564)
XLA Ops:
  0.0 1.2 %constant_dynamic-slice_fusion.2 = (bf16[3,64,768]{2,1,0:T(8,128)(2,1)S(1)}, bf16[3,64,768]{2,1,0:T(8,128)(2,1)S(1)}) fusion(bf16[6,128,768]{2,1,0:T(8,128)(2,1)} %refs_2_.7, s32[]{:T(128)S(6)} %select_n.29), kind=kLoop, calls=%fused_computation.3 | loop fusion | bytes 1179652 | tf_op jit(solution)/shard_map/dynamic_slice | solution.py:207
  1.3 3.1 %collective-permute-start.9 = (bf16[3,64,768]{2,1,0:T(8,128)(2,1)S(1)}, bf16[3,64,768]{2,1,0:T(8,128)(2,1)S(1)}, u32[]{:S(2)}, u32[]{:S(2)}) collective-permute-start(bf16[3,64,768]{2,1,0:T(8,128)(2,1)S(1)} %get-tuple-element.51), channel_id=1, source_target_pairs={{0,4},{4,8},{8,12},{12,0},{1,5},{5,9},{9,13},{13,1},{2,6},{6,10},{... | collective-permute-start | bytes 884744 | tf_op jit(solution)/shard_map/ppermute | solution.py:22
  4.4 1.6 %collective-permute-start.1 = (bf16[3,64,768]{2,1,0:T(8,128)(2,1)S(1)}, bf16[3,64,768]{2,1,0:T(8,128)(2,1)S(1)}, u32[]{:S(2)}, u32[]{:S(2)}) collective-permute-start(bf16[3,64,768]{2,1,0:T(8,128)(2,1)S(1)} %get-tuple-element.52), channel_id=1, source_target_pairs={{0,4},{4,8},{8,12},{12,0},{1,5},{5,9},{9,13},{13,1},{2,6},{6,10},{... | collective-permute-start | bytes 884744 | tf_op jit(solution)/shard_map/ppermute | solution.py:22
  6.0 1.5 %collective-permute-start = (s32[6]{0:T(128)S(1)}, s32[6]{0:T(128)S(1)}, u32[]{:S(2)}, u32[]{:S(2)}) collective-permute-start(s32[6]{0:T(128)S(1)} %copy-done.4), channel_id=1, source_target_pairs={{0,2},{2,0},{1,3},{3,1},{4,6},{6,4},{5,7},{7,5},{8,10},{10,8},{9,1... | collective-permute-start | bytes 80 | tf_op jit(solution)/shard_map/ppermute | solution.py:22
  7.5 0.1 tile.10
  7.5 0.1 tile.12.refs_2_
  7.6 1.6 %collective-permute-start.6 = (s32[2,128]{1,0:T(2,128)S(1)}, s32[2,128]{1,0:T(2,128)S(1)}, u32[]{:S(2)}, u32[]{:S(2)}) collective-permute-start(s32[2,128]{1,0:T(2,128)S(1)} %tile.12.refs_2_), channel_id=1, source_target_pairs={{0,4},{4,8},{8,12},{12,0},{1,5},{5,9},{9,13},{13,1},{2,6},{6,10},{... | collective-permute-start | bytes 3080 | tf_op jit(solution)/shard_map/ppermute | solution.py:22
  9.2 5.1 %collective-permute-done.9.refs_3_ = bf16[3,64,768]{2,1,0:T(8,128)(2,1)S(1)} collective-permute-done((bf16[3,64,768]{2,1,0:T(8,128)(2,1)S(1)}, bf16[3,64,768]{2,1,0:T(8,128)(2,1)S(1)}, u32[]{:S(2)}, u32[]{:S(2)}) %collective-permute-start.9) | collective-permute-done | bytes 294944 | tf_op jit(solution)/shard_map/ppermute | solution.py:22
  14.3 0.0 collective-permute-start.10
  14.3 6.3 %collective-permute-done.1.refs_3_ = bf16[3,64,768]{2,1,0:T(8,128)(2,1)S(1)} collective-permute-done((bf16[3,64,768]{2,1,0:T(8,128)(2,1)S(1)}, bf16[3,64,768]{2,1,0:T(8,128)(2,1)S(1)}, u32[]{:S(2)}, u32[]{:S(2)}) %collective-permute-start.1) | collective-permute-done | bytes 294944 | tf_op jit(solution)/shard_map/ppermute | solution.py:22
  20.6 0.0 collective-permute-start.2
  20.6 0.6 iota_add_fusion
  21.2 0.8 pad_add_fusion.order
  21.9 1.1 %constant_dynamic-slice_fusion = (bf16[384,384]{1,0:T(8,128)(2,1)S(1)}, bf16[384,384]{1,0:T(8,128)(2,1)S(1)}) fusion(bf16[384,768]{1,0:T(8,128)(2,1)} %param.13, s32[]{:T(128)S(6)} %select_n.32, s32[]{:T(128)S(6)} %select_n.31), kind=kLoop, calls=%fused_computation.1 | loop fusion | bytes 1179656 | tf_op jit(solution)/shard_map/dynamic_slice | solution.py:282
  23.0 0.1 collective-permute-start.19
  23.1 0.0 collective-permute-done.refs_1_
  23.1 0.5 collective-permute-start.21
  23.6 3.3 %collective-permute-done.10.refs_3_ = bf16[3,64,768]{2,1,0:T(8,128)(2,1)S(1)} collective-permute-done((bf16[3,64,768]{2,1,0:T(8,128)(2,1)S(1)}, bf16[3,64,768]{2,1,0:T(8,128)(2,1)S(1)}, u32[]{:S(2)}, u32[]{:S(2)}) %collective-permute-start.10) | collective-permute-done | bytes 294944 | tf_op jit(solution)/shard_map/ppermute | solution.py:22
  26.9 0.0 collective-permute-start.15
  26.9 6.3 %collective-permute-done.2.refs_3_ = bf16[3,64,768]{2,1,0:T(8,128)(2,1)S(1)} collective-permute-done((bf16[3,64,768]{2,1,0:T(8,128)(2,1)S(1)}, bf16[3,64,768]{2,1,0:T(8,128)(2,1)S(1)}, u32[]{:S(2)}, u32[]{:S(2)}) %collective-permute-start.2) | collective-permute-done | bytes 294944 | tf_op jit(solution)/shard_map/ppermute | solution.py:22
  33.3 0.0 collective-permute-start.3
  33.3 0.0 copy-start.3
  33.3 1.1 %copy-done.3 = bf16[768,384]{1,0:T(8,128)(2,1)S(1)} copy-done((bf16[768,384]{1,0:T(8,128)(2,1)S(1)}, bf16[768,384]{1,0:T(8,128)(2,1)}, u32[]{:S(2)}) %copy-start.3) | copy-done | bytes 589848
  34.3 3.0 %shard_map.73 = (bf16[3,128,768]{2,1,0:T(8,128)(2,1)S(1)}, f32[2,3,128,128]{3,2,1,0:T(8,128)S(1)}, bf16[2,3,128,768]{3,2,1,0:T(8,128)(2,1)S(1)}) custom-call(s32[6]{0:T(128)S(1)} %pad_add_fusion.order, s32[6]{0:T(128)S(1)} %copy-done.4, s32[6]{0:T(128)S(1)} %collective-permute-done.refs_1_, bf16[6,128,768]{2,1,0:T(8,128)(2,1)S(1)} %copy-done.2, ...), custom_call_target="tpu_custom_call" | custom-call | flops 1509949440 | bytes 2949192 | tf_op jit(solution)/shard_map/pallas_call | solution.py:33
  37.3 0.0 collective-permute-done.6
  37.3 1.6 %collective-permute-start.7 = (s32[2,128]{1,0:T(2,128)S(1)}, s32[2,128]{1,0:T(2,128)S(1)}, u32[]{:S(2)}, u32[]{:S(2)}) collective-permute-start(s32[2,128]{1,0:T(2,128)S(1)} %collective-permute-done.6), channel_id=1, source_target_pairs={{0,4},{4,8},{8,12},{12,0},{1,5},{5,9},{9,13},{13,1},{2,6},{6,10},{... | collective-permute-start | bytes 3080 | tf_op jit(solution)/shard_map/ppermute | solution.py:22
  38.9 6.2 %collective-permute-done.7 = s32[2,128]{1,0:T(2,128)S(1)} collective-permute-done((s32[2,128]{1,0:T(2,128)S(1)}, s32[2,128]{1,0:T(2,128)S(1)}, u32[]{:S(2)}, u32[]{:S(2)}) %collective-permute-start.7) | collective-permute-done | bytes 1056 | tf_op jit(solution)/shard_map/ppermute | solution.py:22
  45.1 1.5 %collective-permute-start.18 = (f32[2,3,128,128]{3,2,1,0:T(8,128)S(1)}, f32[2,3,128,128]{3,2,1,0:T(8,128)S(1)}, u32[]{:S(2)}, u32[]{:S(2)}) collective-permute-start(f32[2,3,128,128]{3,2,1,0:T(8,128)S(1)} %get-tuple-element.37.refs_0_), channel_id=1, source_target_pairs={{0,2},{2,0},{1,3},{3,1},{4,6},{6,4},{5,7},{7,5},{8,10},{10,8},{9,1... | collective-permute-start | bytes 1179656 | tf_op jit(solution)/shard_map/ppermute | solution.py:22
  46.6 0.0 collective-permute-done.19.refs_4_
  46.6 0.0 collective-permute-start.11
  46.6 0.0 collective-permute-done.21.refs_4_
  46.6 0.5 collective-permute-start.13
  47.1 0.0 collective-permute-done.15.refs_3_
  47.1 0.1 collective-permute-start.16
  47.2 0.0 collective-permute-done.3.refs_3_
  47.2 0.4 collective-permute-start.4
  47.6 0.9 %shard_map.78 = (f32[1,3,128,128]{3,2,1,0:T(8,128)S(1)}, bf16[1,3,128,768]{3,2,1,0:T(8,128)(2,1)S(1)}) custom-call(bf16[3,128,768]{2,1,0:T(8,128)(2,1)S(1)} %get-tuple-element.28.refs_0_, bf16[768,384]{1,0:T(8,128)(2,1)S(1)} %copy-done, bf16[768,384]{1,0:T(8,128)(2,1)S(1)} %copy-done.1, bf16[3,64,768]{2,1,0:T(8,128)(2,1)S(1)} %collective-permute-done.9.refs_3_, ...), custom_call_target="tpu_custom_call" | custom-call | flops 528482304 | bytes 2359296 | tf_op jit(solution)/shard_map/pallas_call | solution.py:33
  48.6 0.9 %shard_map.79 = (f32[1,3,128,128]{3,2,1,0:T(8,128)S(1)}, bf16[1,3,128,768]{3,2,1,0:T(8,128)(2,1)S(1)}) custom-call(bf16[3,128,768]{2,1,0:T(8,128)(2,1)S(1)} %get-tuple-element.28.refs_0_, bf16[768,384]{1,0:T(8,128)(2,1)S(1)} %copy-done, bf16[768,384]{1,0:T(8,128)(2,1)S(1)} %copy-done.1, bf16[3,64,768]{2,1,0:T(8,128)(2,1)S(1)} %collective-permute-done.1.refs_3_, ...), custom_call_target="tpu_custom_call" | custom-call | flops 528482304 | bytes 2359296 | tf_op jit(solution)/shard_map/pallas_call | solution.py:33
  49.6 0.6 collective-permute-start.20
  50.2 1.0 %shard_map.75 = (f32[1,3,128,128]{3,2,1,0:T(8,128)S(1)}, bf16[1,3,128,768]{3,2,1,0:T(8,128)(2,1)S(1)}) custom-call(bf16[3,128,768]{2,1,0:T(8,128)(2,1)S(1)} %get-tuple-element.28.refs_0_, bf16[768,384]{1,0:T(8,128)(2,1)S(1)} %copy-done, bf16[768,384]{1,0:T(8,128)(2,1)S(1)} %copy-done.1, bf16[3,64,768]{2,1,0:T(8,128)(2,1)S(1)} %collective-permute-done.10.refs_3_, ...), custom_call_target="tpu_custom_call" | custom-call | flops 528482304 | bytes 2359296 | tf_op jit(solution)/shard_map/pallas_call | solution.py:33
  51.1 0.0 collective-permute-done.13.refs_4_
  51.1 0.2 collective-permute-start.8
  51.4 1.0 %shard_map.76 = (f32[1,3,128,128]{3,2,1,0:T(8,128)S(1)}, bf16[1,3,128,768]{3,2,1,0:T(8,128)(2,1)S(1)}) custom-call(bf16[3,128,768]{2,1,0:T(8,128)(2,1)S(1)} %get-tuple-element.28.refs_0_, bf16[768,384]{1,0:T(8,128)(2,1)S(1)} %copy-done, bf16[768,384]{1,0:T(8,128)(2,1)S(1)} %copy-done.1, bf16[3,64,768]{2,1,0:T(8,128)(2,1)S(1)} %collective-permute-done.2.refs_3_, ...), custom_call_target="tpu_custom_call" | custom-call | flops 528482304 | bytes 2359296 | tf_op jit(solution)/shard_map/pallas_call | solution.py:33
  52.4 1.6 %collective-permute-start.22 = (f32[1,3,128,128]{3,2,1,0:T(8,128)S(1)}, f32[1,3,128,128]{3,2,1,0:T(8,128)S(1)}, u32[]{:S(2)}, u32[]{:S(2)}) collective-permute-start(f32[1,3,128,128]{3,2,1,0:T(8,128)S(1)} %get-tuple-element.41.refs_8_), channel_id=1, source_target_pairs={{0,2},{2,0},{1,3},{3,1},{4,6},{6,4},{5,7},{7,5},{8,10},{10,8},{9,1... | collective-permute-start | bytes 589832 | tf_op jit(solution)/shard_map/ppermute | solution.py:22
  53.9 1.0 %shard_map.77 = (f32[1,3,128,128]{3,2,1,0:T(8,128)S(1)}, bf16[1,3,128,768]{3,2,1,0:T(8,128)(2,1)S(1)}) custom-call(bf16[3,128,768]{2,1,0:T(8,128)(2,1)S(1)} %get-tuple-element.28.refs_0_, bf16[768,384]{1,0:T(8,128)(2,1)S(1)} %copy-done, bf16[768,384]{1,0:T(8,128)(2,1)S(1)} %copy-done.1, bf16[3,64,768]{2,1,0:T(8,128)(2,1)S(1)} %collective-permute-done.15.refs_3_, ...), custom_call_target="tpu_custom_call" | custom-call | flops 528482304 | bytes 2359296 | tf_op jit(solution)/shard_map/pallas_call | solution.py:33
  54.9 0.6 collective-permute-start.12
  55.5 1.0 %shard_map.74 = (f32[1,3,128,128]{3,2,1,0:T(8,128)S(1)}, bf16[1,3,128,768]{3,2,1,0:T(8,128)(2,1)S(1)}) custom-call(bf16[3,128,768]{2,1,0:T(8,128)(2,1)S(1)} %get-tuple-element.28.refs_0_, bf16[768,384]{1,0:T(8,128)(2,1)S(1)} %copy-done, bf16[768,384]{1,0:T(8,128)(2,1)S(1)} %copy-done.1, bf16[3,64,768]{2,1,0:T(8,128)(2,1)S(1)} %collective-permute-done.3.refs_3_, ...), custom_call_target="tpu_custom_call" | custom-call | flops 528482304 | bytes 2359296 | tf_op jit(solution)/shard_map/pallas_call | solution.py:33
  56.4 0.3 collective-permute-done.8
  56.7 1.5 %collective-permute-start.14 = (f32[1,3,128,128]{3,2,1,0:T(8,128)S(1)}, f32[1,3,128,128]{3,2,1,0:T(8,128)S(1)}, u32[]{:S(2)}, u32[]{:S(2)}) collective-permute-start(f32[1,3,128,128]{3,2,1,0:T(8,128)S(1)} %get-tuple-element.33.refs_4_), channel_id=1, source_target_pairs={{0,2},{2,0},{1,3},{3,1},{4,6},{6,4},{5,7},{7,5},{8,10},{10,8},{9,1... | collective-permute-start | bytes 589832 | tf_op jit(solution)/shard_map/ppermute | solution.py:22
  58.2 0.5 collective-permute-start.17
  58.8 2.5 %collective-permute-done.20.refs_5_ = f32[1,3,128,128]{3,2,1,0:T(8,128)S(1)} collective-permute-done((f32[1,3,128,128]{3,2,1,0:T(8,128)S(1)}, f32[1,3,128,128]{3,2,1,0:T(8,128)S(1)}, u32[]{:S(2)}, u32[]{:S(2)}) %collective-permute-start.20) | collective-permute-done | bytes 196640 | tf_op jit(solution)/shard_map/ppermute | solution.py:22
  61.3 1.5 %collective-permute-start.5 = (f32[1,3,128,128]{3,2,1,0:T(8,128)S(1)}, f32[1,3,128,128]{3,2,1,0:T(8,128)S(1)}, u32[]{:S(2)}, u32[]{:S(2)}) collective-permute-start(f32[1,3,128,128]{3,2,1,0:T(8,128)S(1)} %get-tuple-element.29.refs_0_), channel_id=1, source_target_pairs={{0,2},{2,0},{1,3},{3,1},{4,6},{6,4},{5,7},{7,5},{8,10},{10,8},{9,1... | collective-permute-start | bytes 589832 | tf_op jit(solution)/shard_map/ppermute | solution.py:22
  62.8 2.7 %collective-permute-done.22.refs_9_ = f32[1,3,128,128]{3,2,1,0:T(8,128)S(1)} collective-permute-done((f32[1,3,128,128]{3,2,1,0:T(8,128)S(1)}, f32[1,3,128,128]{3,2,1,0:T(8,128)S(1)}, u32[]{:S(2)}, u32[]{:S(2)}) %collective-permute-start.22) | collective-permute-done | bytes 196640 | tf_op jit(solution)/shard_map/ppermute | solution.py:22
  65.5 0.6 shard_map.80
  66.1 3.6 %collective-permute-done.12.refs_1_ = f32[1,3,128,128]{3,2,1,0:T(8,128)S(1)} collective-permute-done((f32[1,3,128,128]{3,2,1,0:T(8,128)S(1)}, f32[1,3,128,128]{3,2,1,0:T(8,128)S(1)}, u32[]{:S(2)}, u32[]{:S(2)}) %collective-permute-start.12) | collective-permute-done | bytes 196640 | tf_op jit(solution)/shard_map/ppermute | solution.py:22
  69.7 4.2 %collective-permute-done.14.refs_5_ = f32[1,3,128,128]{3,2,1,0:T(8,128)S(1)} collective-permute-done((f32[1,3,128,128]{3,2,1,0:T(8,128)S(1)}, f32[1,3,128,128]{3,2,1,0:T(8,128)S(1)}, u32[]{:S(2)}, u32[]{:S(2)}) %collective-permute-start.14) | collective-permute-done | bytes 196640 | tf_op jit(solution)/shard_map/ppermute | solution.py:22
  73.9 4.2 %collective-permute-done.17.refs_9_ = f32[1,3,128,128]{3,2,1,0:T(8,128)S(1)} collective-permute-done((f32[1,3,128,128]{3,2,1,0:T(8,128)S(1)}, f32[1,3,128,128]{3,2,1,0:T(8,128)S(1)}, u32[]{:S(2)}, u32[]{:S(2)}) %collective-permute-start.17) | collective-permute-done | bytes 196640 | tf_op jit(solution)/shard_map/ppermute | solution.py:22
  78.2 0.6 shard_map.81
  78.8 1.9 %collective-permute-done.5.refs_1_ = f32[1,3,128,128]{3,2,1,0:T(8,128)S(1)} collective-permute-done((f32[1,3,128,128]{3,2,1,0:T(8,128)S(1)}, f32[1,3,128,128]{3,2,1,0:T(8,128)S(1)}, u32[]{:S(2)}, u32[]{:S(2)}) %collective-permute-start.5) | collective-permute-done | bytes 196640 | tf_op jit(solution)/shard_map/ppermute | solution.py:22
  80.6 1.5 %shard_map.82 = (bf16[6,128,384]{2,1,0:T(8,128)(2,1)S(1)}, bf16[6,128,384]{2,1,0:T(8,128)(2,1)S(1)}) custom-call(s32[6]{0:T(128)S(1)} %pad_add_fusion.order, f32[1,3,128,128]{3,2,1,0:T(8,128)S(1)} %get-tuple-element.29.refs_0_, f32[1,3,128,128]{3,2,1,0:T(8,128)S(1)} %collective-permute-done.5.refs_1_, s32[1,128]{1,0:T(1,128)S(1)} %get-tuple-element.58.refs_2_, ...), custom_call_target="tpu_custom_call" | custom-call | flops 301989888 | bytes 2851352 | tf_op jit(solution)/shard_map/pallas_call | solution.py:33
  82.1 0.1 collective-permute-start.23
  82.2 1.1 %shard_map.83 = f32[6,128,384]{2,1,0:T(8,128)S(1)} custom-call(s32[6]{0:T(128)S(1)} %pad_add_fusion.order, bf16[6,128,384]{2,1,0:T(8,128)(2,1)S(1)} %get-tuple-element.49.attended, bf16[384,384]{1,0:T(8,128)(2,1)S(1)} %get-tuple-element.53.w_own), custom_call_target="tpu_custom_call" | custom-call | flops 226492416 | bytes 884760 | tf_op jit(solution)/shard_map/pallas_call | solution.py:33
  83.3 0.9 %collective-permute-done.23 = bf16[6,128,384]{2,1,0:T(8,128)(2,1)S(1)} collective-permute-done((bf16[6,128,384]{2,1,0:T(8,128)(2,1)S(1)}, bf16[6,128,384]{2,1,0:T(8,128)(2,1)S(1)}, u32[]{:S(2)}, u32[]{:S(2)}) %collective-permute-start.23) | collective-permute-done | bytes 589856 | tf_op jit(solution)/shard_map/ppermute | solution.py:22
  84.2 1.0 %add_convert_fusion = bf16[6,128,384]{2,1,0:T(8,128)(2,1)} fusion(f32[6,128,384]{2,1,0:T(8,128)S(1)} %shard_map.83, bf16[6,128,384]{2,1,0:T(8,128)(2,1)S(1)} %collective-permute-done.23), kind=kLoop, calls=%fused_computation | loop fusion | flops 884736 | bytes 2359296 | tf_op jit(solution)/shard_map/convert_element_type | solution.py:310
  (18 shorter events, 0.0 us)
Async XLA Ops:
  0.0 6.0 %copy-start.4 = (s32[6]{0:T(128)S(1)}, s32[6]{0:T(128)}, u32[]{:S(2)}) copy-start(s32[6]{0:T(128)} %refs_0_.1) | copy-start | bytes 76
  0.0 7.5 %copy-start.5 = (s32[128]{0:T(128)S(1)}, s32[128]{0:T(128)}, u32[]{:S(2)}) copy-start(s32[128]{0:T(128)} %param.9) | copy-start | bytes 1540
  0.0 33.3 %copy-start = (bf16[768,384]{1,0:T(8,128)(2,1)S(1)}, bf16[768,384]{1,0:T(8,128)(2,1)}, u32[]{:S(2)}) copy-start(bf16[768,384]{1,0:T(8,128)(2,1)} %refs_1_.11) | copy-start | bytes 1769476
  0.0 33.3 %copy-start.1 = (bf16[768,384]{1,0:T(8,128)(2,1)S(1)}, bf16[768,384]{1,0:T(8,128)(2,1)}, u32[]{:S(2)}) copy-start(bf16[768,384]{1,0:T(8,128)(2,1)} %refs_2_.13) | copy-start | bytes 1769476
  0.0 33.3 %copy-start.2 = (bf16[6,128,768]{2,1,0:T(8,128)(2,1)S(1)}, bf16[6,128,768]{2,1,0:T(8,128)(2,1)}, u32[]{:S(2)}) copy-start(bf16[6,128,768]{2,1,0:T(8,128)(2,1)} %refs_2_.7) | copy-start | bytes 3538948
  1.3 13.0 %collective-permute-start.9 = (bf16[3,64,768]{2,1,0:T(8,128)(2,1)S(1)}, bf16[3,64,768]{2,1,0:T(8,128)(2,1)S(1)}, u32[]{:S(2)}, u32[]{:S(2)}) collective-permute-start(bf16[3,64,768]{2,1,0:T(8,128)(2,1)S(1)} %get-tuple-element.51), channel_id=1, source_target_pairs={{0,4},{4,8},{8,12},{12,0},{1,5},{5,9},{9,13},{13,1},{2,6},{6,10},{... | collective-permute-start | bytes 884744 | tf_op jit(solution)/shard_map/ppermute | solution.py:22
  4.4 16.2 %collective-permute-start.1 = (bf16[3,64,768]{2,1,0:T(8,128)(2,1)S(1)}, bf16[3,64,768]{2,1,0:T(8,128)(2,1)S(1)}, u32[]{:S(2)}, u32[]{:S(2)}) collective-permute-start(bf16[3,64,768]{2,1,0:T(8,128)(2,1)S(1)} %get-tuple-element.52), channel_id=1, source_target_pairs={{0,4},{4,8},{8,12},{12,0},{1,5},{5,9},{9,13},{13,1},{2,6},{6,10},{... | collective-permute-start | bytes 884744 | tf_op jit(solution)/shard_map/ppermute | solution.py:22
  6.0 17.2 %collective-permute-start = (s32[6]{0:T(128)S(1)}, s32[6]{0:T(128)S(1)}, u32[]{:S(2)}, u32[]{:S(2)}) collective-permute-start(s32[6]{0:T(128)S(1)} %copy-done.4), channel_id=1, source_target_pairs={{0,2},{2,0},{1,3},{3,1},{4,6},{6,4},{5,7},{7,5},{8,10},{10,8},{9,1... | collective-permute-start | bytes 80 | tf_op jit(solution)/shard_map/ppermute | solution.py:22
  7.6 29.7 %collective-permute-start.6 = (s32[2,128]{1,0:T(2,128)S(1)}, s32[2,128]{1,0:T(2,128)S(1)}, u32[]{:S(2)}, u32[]{:S(2)}) collective-permute-start(s32[2,128]{1,0:T(2,128)S(1)} %tile.12.refs_2_), channel_id=1, source_target_pairs={{0,4},{4,8},{8,12},{12,0},{1,5},{5,9},{9,13},{13,1},{2,6},{6,10},{... | collective-permute-start | bytes 3080 | tf_op jit(solution)/shard_map/ppermute | solution.py:22
  14.3 12.7 %collective-permute-start.10 = (bf16[3,64,768]{2,1,0:T(8,128)(2,1)S(1)}, bf16[3,64,768]{2,1,0:T(8,128)(2,1)S(1)}, u32[]{:S(2)}, u32[]{:S(2)}) collective-permute-start(bf16[3,64,768]{2,1,0:T(8,128)(2,1)S(1)} %collective-permute-done.9.refs_3_), channel_id=1, source_target_pairs={{0,4},{4,8},{8,12},{12,0},{1,5},{5,9},{9,13},{13,1},{2,6},{6,10},{... | collective-permute-start | bytes 884744 | tf_op jit(solution)/shard_map/ppermute | solution.py:22
  20.6 12.7 %collective-permute-start.2 = (bf16[3,64,768]{2,1,0:T(8,128)(2,1)S(1)}, bf16[3,64,768]{2,1,0:T(8,128)(2,1)S(1)}, u32[]{:S(2)}, u32[]{:S(2)}) collective-permute-start(bf16[3,64,768]{2,1,0:T(8,128)(2,1)S(1)} %collective-permute-done.1.refs_3_), channel_id=1, source_target_pairs={{0,4},{4,8},{8,12},{12,0},{1,5},{5,9},{9,13},{13,1},{2,6},{6,10},{... | collective-permute-start | bytes 884744 | tf_op jit(solution)/shard_map/ppermute | solution.py:22
  23.0 23.6 %collective-permute-start.19 = (bf16[3,64,768]{2,1,0:T(8,128)(2,1)S(1)}, bf16[3,64,768]{2,1,0:T(8,128)(2,1)S(1)}, u32[]{:S(2)}, u32[]{:S(2)}) collective-permute-start(bf16[3,64,768]{2,1,0:T(8,128)(2,1)S(1)} %collective-permute-done.9.refs_3_), channel_id=1, source_target_pairs={{0,1},{1,0},{2,3},{3,2},{4,5},{5,4},{6,7},{7,6},{8,9},{9,8},{10,11... | collective-permute-start | bytes 884744 | tf_op jit(solution)/shard_map/ppermute | solution.py:22
  23.1 23.5 %collective-permute-start.21 = (bf16[3,64,768]{2,1,0:T(8,128)(2,1)S(1)}, bf16[3,64,768]{2,1,0:T(8,128)(2,1)S(1)}, u32[]{:S(2)}, u32[]{:S(2)}) collective-permute-start(bf16[3,64,768]{2,1,0:T(8,128)(2,1)S(1)} %collective-permute-done.1.refs_3_), channel_id=1, source_target_pairs={{0,1},{1,0},{2,3},{3,2},{4,5},{5,4},{6,7},{7,6},{8,9},{9,8},{10,11... | collective-permute-start | bytes 884744 | tf_op jit(solution)/shard_map/ppermute | solution.py:22
  26.9 20.2 %collective-permute-start.15 = (bf16[3,64,768]{2,1,0:T(8,128)(2,1)S(1)}, bf16[3,64,768]{2,1,0:T(8,128)(2,1)S(1)}, u32[]{:S(2)}, u32[]{:S(2)}) collective-permute-start(bf16[3,64,768]{2,1,0:T(8,128)(2,1)S(1)} %collective-permute-done.10.refs_3_), channel_id=1, source_target_pairs={{0,4},{4,8},{8,12},{12,0},{1,5},{5,9},{9,13},{13,1},{2,6},{6,10},{... | collective-permute-start | bytes 884744 | tf_op jit(solution)/shard_map/ppermute | solution.py:22
  33.3 13.9 %collective-permute-start.3 = (bf16[3,64,768]{2,1,0:T(8,128)(2,1)S(1)}, bf16[3,64,768]{2,1,0:T(8,128)(2,1)S(1)}, u32[]{:S(2)}, u32[]{:S(2)}) collective-permute-start(bf16[3,64,768]{2,1,0:T(8,128)(2,1)S(1)} %collective-permute-done.2.refs_3_), channel_id=1, source_target_pairs={{0,4},{4,8},{8,12},{12,0},{1,5},{5,9},{9,13},{13,1},{2,6},{6,10},{... | collective-permute-start | bytes 884744 | tf_op jit(solution)/shard_map/ppermute | solution.py:22
  33.3 1.1 %copy-start.3 = (bf16[768,384]{1,0:T(8,128)(2,1)S(1)}, bf16[768,384]{1,0:T(8,128)(2,1)}, u32[]{:S(2)}) copy-start(bf16[768,384]{1,0:T(8,128)(2,1)} %refs_3_.1) | copy-start | bytes 1769476
  37.3 7.8 %collective-permute-start.7 = (s32[2,128]{1,0:T(2,128)S(1)}, s32[2,128]{1,0:T(2,128)S(1)}, u32[]{:S(2)}, u32[]{:S(2)}) collective-permute-start(s32[2,128]{1,0:T(2,128)S(1)} %collective-permute-done.6), channel_id=1, source_target_pairs={{0,4},{4,8},{8,12},{12,0},{1,5},{5,9},{9,13},{13,1},{2,6},{6,10},{... | collective-permute-start | bytes 3080 | tf_op jit(solution)/shard_map/ppermute | solution.py:22
  45.1 13.1 %collective-permute-start.18 = (f32[2,3,128,128]{3,2,1,0:T(8,128)S(1)}, f32[2,3,128,128]{3,2,1,0:T(8,128)S(1)}, u32[]{:S(2)}, u32[]{:S(2)}) collective-permute-start(f32[2,3,128,128]{3,2,1,0:T(8,128)S(1)} %get-tuple-element.37.refs_0_), channel_id=1, source_target_pairs={{0,2},{2,0},{1,3},{3,1},{4,6},{6,4},{5,7},{7,5},{8,10},{10,8},{9,1... | collective-permute-start | bytes 1179656 | tf_op jit(solution)/shard_map/ppermute | solution.py:22
  46.6 2.9 %collective-permute-start.11 = (bf16[3,64,768]{2,1,0:T(8,128)(2,1)S(1)}, bf16[3,64,768]{2,1,0:T(8,128)(2,1)S(1)}, u32[]{:S(2)}, u32[]{:S(2)}) collective-permute-start(bf16[3,64,768]{2,1,0:T(8,128)(2,1)S(1)} %collective-permute-done.10.refs_3_), channel_id=1, source_target_pairs={{0,1},{1,0},{2,3},{3,2},{4,5},{5,4},{6,7},{7,6},{8,9},{9,8},{10,11... | collective-permute-start | bytes 884744 | tf_op jit(solution)/shard_map/ppermute | solution.py:22
  46.6 4.5 %collective-permute-start.13 = (bf16[3,64,768]{2,1,0:T(8,128)(2,1)S(1)}, bf16[3,64,768]{2,1,0:T(8,128)(2,1)S(1)}, u32[]{:S(2)}, u32[]{:S(2)}) collective-permute-start(bf16[3,64,768]{2,1,0:T(8,128)(2,1)S(1)} %collective-permute-done.2.refs_3_), channel_id=1, source_target_pairs={{0,1},{1,0},{2,3},{3,2},{4,5},{5,4},{6,7},{7,6},{8,9},{9,8},{10,11... | collective-permute-start | bytes 884744 | tf_op jit(solution)/shard_map/ppermute | solution.py:22
  47.1 5.2 %collective-permute-start.16 = (bf16[3,64,768]{2,1,0:T(8,128)(2,1)S(1)}, bf16[3,64,768]{2,1,0:T(8,128)(2,1)S(1)}, u32[]{:S(2)}, u32[]{:S(2)}) collective-permute-start(bf16[3,64,768]{2,1,0:T(8,128)(2,1)S(1)} %collective-permute-done.15.refs_3_), channel_id=1, source_target_pairs={{0,1},{1,0},{2,3},{3,2},{4,5},{5,4},{6,7},{7,6},{8,9},{9,8},{10,11... | collective-permute-start | bytes 884744 | tf_op jit(solution)/shard_map/ppermute | solution.py:22
  47.2 7.7 %collective-permute-start.4 = (bf16[3,64,768]{2,1,0:T(8,128)(2,1)S(1)}, bf16[3,64,768]{2,1,0:T(8,128)(2,1)S(1)}, u32[]{:S(2)}, u32[]{:S(2)}) collective-permute-start(bf16[3,64,768]{2,1,0:T(8,128)(2,1)S(1)} %collective-permute-done.3.refs_3_), channel_id=1, source_target_pairs={{0,1},{1,0},{2,3},{3,2},{4,5},{5,4},{6,7},{7,6},{8,9},{9,8},{10,11... | collective-permute-start | bytes 884744 | tf_op jit(solution)/shard_map/ppermute | solution.py:22
  49.6 11.8 %collective-permute-start.20 = (f32[1,3,128,128]{3,2,1,0:T(8,128)S(1)}, f32[1,3,128,128]{3,2,1,0:T(8,128)S(1)}, u32[]{:S(2)}, u32[]{:S(2)}) collective-permute-start(f32[1,3,128,128]{3,2,1,0:T(8,128)S(1)} %get-tuple-element.39.refs_4_), channel_id=1, source_target_pairs={{0,2},{2,0},{1,3},{3,1},{4,6},{6,4},{5,7},{7,5},{8,10},{10,8},{9,1... | collective-permute-start | bytes 589832 | tf_op jit(solution)/shard_map/ppermute | solution.py:22
  51.1 5.6 %collective-permute-start.8 = (s32[2,128]{1,0:T(2,128)S(1)}, s32[2,128]{1,0:T(2,128)S(1)}, u32[]{:S(2)}, u32[]{:S(2)}) collective-permute-start(s32[2,128]{1,0:T(2,128)S(1)} %collective-permute-done.7), channel_id=1, source_target_pairs={{0,4},{4,8},{8,12},{12,0},{1,5},{5,9},{9,13},{13,1},{2,6},{6,10},{... | collective-permute-start | bytes 3080 | tf_op jit(solution)/shard_map/ppermute | solution.py:22
  52.4 13.2 %collective-permute-start.22 = (f32[1,3,128,128]{3,2,1,0:T(8,128)S(1)}, f32[1,3,128,128]{3,2,1,0:T(8,128)S(1)}, u32[]{:S(2)}, u32[]{:S(2)}) collective-permute-start(f32[1,3,128,128]{3,2,1,0:T(8,128)S(1)} %get-tuple-element.41.refs_8_), channel_id=1, source_target_pairs={{0,2},{2,0},{1,3},{3,1},{4,6},{6,4},{5,7},{7,5},{8,10},{10,8},{9,1... | collective-permute-start | bytes 589832 | tf_op jit(solution)/shard_map/ppermute | solution.py:22
  54.9 14.8 %collective-permute-start.12 = (f32[1,3,128,128]{3,2,1,0:T(8,128)S(1)}, f32[1,3,128,128]{3,2,1,0:T(8,128)S(1)}, u32[]{:S(2)}, u32[]{:S(2)}) collective-permute-start(f32[1,3,128,128]{3,2,1,0:T(8,128)S(1)} %get-tuple-element.31.refs_0_), channel_id=1, source_target_pairs={{0,2},{2,0},{1,3},{3,1},{4,6},{6,4},{5,7},{7,5},{8,10},{10,8},{9,1... | collective-permute-start | bytes 589832 | tf_op jit(solution)/shard_map/ppermute | solution.py:22
  56.7 17.2 %collective-permute-start.14 = (f32[1,3,128,128]{3,2,1,0:T(8,128)S(1)}, f32[1,3,128,128]{3,2,1,0:T(8,128)S(1)}, u32[]{:S(2)}, u32[]{:S(2)}) collective-permute-start(f32[1,3,128,128]{3,2,1,0:T(8,128)S(1)} %get-tuple-element.33.refs_4_), channel_id=1, source_target_pairs={{0,2},{2,0},{1,3},{3,1},{4,6},{6,4},{5,7},{7,5},{8,10},{10,8},{9,1... | collective-permute-start | bytes 589832 | tf_op jit(solution)/shard_map/ppermute | solution.py:22
  58.2 19.9 %collective-permute-start.17 = (f32[1,3,128,128]{3,2,1,0:T(8,128)S(1)}, f32[1,3,128,128]{3,2,1,0:T(8,128)S(1)}, u32[]{:S(2)}, u32[]{:S(2)}) collective-permute-start(f32[1,3,128,128]{3,2,1,0:T(8,128)S(1)} %get-tuple-element.35.refs_8_), channel_id=1, source_target_pairs={{0,2},{2,0},{1,3},{3,1},{4,6},{6,4},{5,7},{7,5},{8,10},{10,8},{9,1... | collective-permute-start | bytes 589832 | tf_op jit(solution)/shard_map/ppermute | solution.py:22
  61.3 19.3 %collective-permute-start.5 = (f32[1,3,128,128]{3,2,1,0:T(8,128)S(1)}, f32[1,3,128,128]{3,2,1,0:T(8,128)S(1)}, u32[]{:S(2)}, u32[]{:S(2)}) collective-permute-start(f32[1,3,128,128]{3,2,1,0:T(8,128)S(1)} %get-tuple-element.29.refs_0_), channel_id=1, source_target_pairs={{0,2},{2,0},{1,3},{3,1},{4,6},{6,4},{5,7},{7,5},{8,10},{10,8},{9,1... | collective-permute-start | bytes 589832 | tf_op jit(solution)/shard_map/ppermute | solution.py:22
  82.1 2.1 %collective-permute-start.23 = (bf16[6,128,384]{2,1,0:T(8,128)(2,1)S(1)}, bf16[6,128,384]{2,1,0:T(8,128)(2,1)S(1)}, u32[]{:S(2)}, u32[]{:S(2)}) collective-permute-start(bf16[6,128,384]{2,1,0:T(8,128)(2,1)S(1)} %get-tuple-element.50), channel_id=1, source_target_pairs={{0,1},{1,0},{2,3},{3,2},{4,5},{5,4},{6,7},{7,6},{8,9},{9,8},{10,11... | collective-permute-start | bytes 1769480 | tf_op jit(solution)/shard_map/ppermute | solution.py:22

commit v3 on v2

v3 whole, which is shorter than its diff:
```python
import functools
import math

import jax
import jax.numpy as jnp
from jax import lax
from jax.experimental import pallas as pl
from jax.experimental.pallas import tpu as pltpu
from jax.sharding import PartitionSpec as P


HEAD_DIM = 64
LANES = 128
PER_TILE = LANES // HEAD_DIM
CHUNKS = 2
MARK_ROWS = 16
MASKED = -1000000000.0
VMEM_LIMIT = 24 * 1024 * 1024


def ring(value, axis, by=1):
    length = lax.axis_size(axis)
    return lax.ppermute(value, axis, [(i, (i + by) % length) for i in range(length)])


def whole(count):
    return [pl.BlockSpec(memory_space=pltpu.VMEM) for _ in range(count)]


def call(kernel, out_shape, args, flops, scalars=0, scratch=()):
    specs = [pl.BlockSpec(memory_space=pltpu.SMEM)] * scalars + whole(len(args) - scalars)
    multiple = isinstance(out_shape, (list, tuple))
    size = sum(a.size * a.dtype.itemsize for a in args)
    return pl.pallas_call(
        kernel,
        out_shape=out_shape,
        in_specs=specs,
        out_specs=whole(len(out_shape)) if multiple else whole(1)[0],
        scratch_shapes=list(scratch),
        cost_estimate=pl.CostEstimate(flops=int(flops), transcendentals=0, bytes_accessed=int(size)),
        compiler_params=pltpu.CompilerParams(vmem_limit_bytes=VMEM_LIMIT),
    )(*args)


def lane_head(shape):
    return lax.broadcasted_iota(jnp.int32, shape, len(shape) - 1) // HEAD_DIM


def dot(a, b):
    return jnp.dot(a, b, preferred_element_type=jnp.float32)


def dot_nt(a, b):
    return lax.dot_general(a, b, (((1,), (1,)), ((), ())), preferred_element_type=jnp.float32)


def per_head(value, pick):
    heads = lane_head(value.shape)
    parts = [pick(value, heads == h) for h in range(PER_TILE)]
    out = parts[-1]
    for h in range(PER_TILE - 2, -1, -1):
        out = jnp.where(heads == h, parts[h], out)
    return jnp.broadcast_to(out, value.shape)


def max_over(value, keep):
    return jnp.max(jnp.where(keep, value, -jnp.inf), axis=-1, keepdims=True)


def sum_over(value, keep):
    return jnp.sum(jnp.where(keep, value, 0.0), axis=-1, keepdims=True)


def spread(target, chunk, flat, first_row, cells):
    rows = flat.shape[0] // cells
    tiles = flat.shape[1] // LANES
    heads = lane_head((cells, LANES))
    for tile in range(tiles):
        for row in range(rows):
            part = flat[row * cells : (row + 1) * cells, tile * LANES : (tile + 1) * LANES]
            at = slice((first_row + row) * LANES, (first_row + row + 1) * LANES)
            for h in range(PER_TILE):
                kept = jnp.where(heads == h, part, jnp.zeros_like(part))
                target[chunk, tile, h * cells : (h + 1) * cells, at] = kept


def own_row(row, share, cores):
    core = lax.axis_index("head")
    return lax.rem(core + (cores - row // share), cores) * share + row % share


def live_lanes(mask, chunk):
    turned = pltpu.roll(mask, HEAD_DIM, 1)
    first = lane_head(mask.shape) == 0
    return (jnp.where(first, mask, turned) if chunk == 0 else jnp.where(first, turned, mask))[:1] > 0


def score(query, keys, live, masked):
    return jnp.where(live, dot_nt(query, keys), masked)


def pack_kernel(tokens, mask, packed, landing, done, *, chunk, share):
    _, part, width = landing.shape
    core = lax.axis_index("head")
    copy = pltpu.make_async_copy(
        tokens.at[pl.ds(core * share, share), pl.ds(chunk * part, part)], landing, done
    )
    copy.start()
    size = share * part
    tail = packed.shape[0] - width // LANES * size
    packed[width // LANES * size :] = jnp.broadcast_to(
        mask[...].astype(jnp.float32), (tail, LANES)
    ).astype(jnp.bfloat16)
    copy.wait()
    for tile in range(width // LANES):
        at = slice(tile * LANES, (tile + 1) * LANES)
        packed[tile * size : (tile + 1) * size] = landing[:, :, at].reshape(size, LANES)


def unpack(packed, width, size):
    return jnp.concatenate(
        [packed[tile * size : (tile + 1) * size] for tile in range(width // LANES)], axis=1
    )


def project_kernel(*refs, order, masked):
    query, w_key, w_value = refs[:3]
    pieces = refs[3:-3]
    logits, values, keys = refs[-3:]
    tiles, width = query.shape[0], w_key.shape[0]
    chunks = len(order)
    per_chunk = len(pieces) // chunks
    part = keys.shape[2] // PER_TILE
    size = (pieces[0].shape[0] - MARK_ROWS) * LANES // width
    for at in range(chunks):
        own = pieces[at * per_chunk : (at + 1) * per_chunk]
        flat = jnp.concatenate([unpack(piece, width, size) for piece in own], axis=0)
        spread(keys, 0, dot(flat, w_key[...]).astype(jnp.bfloat16), 0, part)
        mask = own[0][own[0].shape[0] - MARK_ROWS :].astype(jnp.float32)
        live = live_lanes(mask[:8], order[at])
        for tile in range(tiles):
            logits[at, tile] = score(query[tile], keys[0, tile], live, masked)
        spread(values, at, dot(flat, w_value[...]).astype(jnp.bfloat16), 0, part)


def own_kernel(*refs, cores, masked):
    counts, refs = refs[:-9], refs[-9:]
    mask, tokens, w_query, w_key, w_value, query, logits, values, keys = refs
    rows, cells, _ = tokens.shape
    chunks = logits.shape[0]
    part = cells // chunks
    total = sum(count[row] for count in counts for row in range(rows))
    scale = lax.rsqrt(jnp.full((1, query.shape[0] * LANES), total, jnp.int32).astype(jnp.float32))
    for row in range(rows):
        source = own_row(row, rows // cores, cores)
        block = tokens[source]
        count = jnp.full(scale.shape, counts[0][source], jnp.int32).astype(jnp.float32)
        factor = count * scale / math.sqrt(HEAD_DIM)
        scaled = (dot(block, w_query[...]) * factor).astype(jnp.bfloat16)
        for tile in range(query.shape[0]):
            query[tile, :, row * LANES : (row + 1) * LANES] = scaled[:, tile * LANES : (tile + 1) * LANES]
        key = dot(block, w_key[...]).astype(jnp.bfloat16)
        value = dot(block, w_value[...]).astype(jnp.bfloat16)
        for chunk in range(chunks):
            spread(keys, chunk, key[chunk * part : (chunk + 1) * part], row, part)
            spread(values, chunk, value[chunk * part : (chunk + 1) * part], row, part)
    marks = jnp.broadcast_to(mask[...].astype(jnp.float32), (8, LANES))
    for chunk in range(chunks):
        live = live_lanes(marks, chunk)
        for tile in range(query.shape[0]):
            logits[chunk, tile] = score(query[tile], keys[chunk, tile], live, masked)


def absorb(units, state, tile, rows):
    scores, mixed = [], []
    for tiles, values in units:
        for chunk in range(tiles[0].shape[0]):
            total = tiles[0][chunk, tile]
            for other in tiles[1:]:
                total = total + other[chunk, tile]
            scores.append(total)
            mixed.append(values[chunk, tile])
    top = functools.reduce(jnp.maximum, scores)
    top = per_head(top, max_over)
    if state is not None:
        before = state[0][tile]
        top = jnp.maximum(top, before)
        rescale = jnp.exp(before - top)
    expo = [jnp.exp(score - top) for score in scores]
    denom = functools.reduce(jnp.add, expo)
    probs = jnp.concatenate([e.astype(jnp.bfloat16) for e in expo], axis=1)
    accum = dot(probs, jnp.concatenate(mixed, axis=0))
    if state is not None:
        denom = denom + state[1][tile] * rescale
        accum = accum + state[2][tile] * jnp.concatenate([rescale] * rows, axis=1)
    return top, denom, accum


def read_units(refs, sizes):
    units, at = [], 0
    for size in sizes:
        units.append((refs[at : at + size], refs[at + size]))
        at += size + 1
    return units, refs[at:]


def absorb_kernel(*refs, sizes, carried):
    units, refs = read_units(refs, sizes)
    state = refs[:3] if carried else None
    top, denom, accum = refs[-3:]
    rows = accum.shape[2] // LANES
    for tile in range(accum.shape[0]):
        top[tile], denom[tile], accum[tile] = absorb(units, state, tile, rows)


def columns_of(w_out, ahead, cores):
    columns = w_out.shape[1] // cores
    at = lax.rem(lax.axis_index("head") + ahead, cores) * columns
    return w_out[:, pl.ds(pl.multiple_of(at, LANES), columns)]


def finish_kernel(*refs, sizes, carried, cores):
    units, refs = read_units(refs, sizes)
    state = refs[:3] if carried else None
    w_out, attended, sent = refs[-3:]
    rows, _, _ = attended.shape
    for tile in range(attended.shape[2] // LANES):
        _, denom, accum = absorb(units, state, tile, rows)
        denom = per_head(denom, sum_over)
        for row in range(rows):
            part = accum[:, row * LANES : (row + 1) * LANES] / denom
            attended[row, :, tile * LANES : (tile + 1) * LANES] = part.astype(jnp.bfloat16)
    write_output(attended, columns_of(w_out, 1 % cores, cores), sent, cores)


def write_output(attended, w, target, cores):
    rows = attended.shape[0]
    for row in range(rows):
        target[own_row(row, rows // cores, cores)] = dot(attended[row], w).astype(target.dtype)


def output_kernel(attended, w_out, kept, *, ahead, cores):
    write_output(attended, columns_of(w_out, ahead, cores), kept, cores)


def batches(blocks):
    every = tuple(range(CHUNKS))
    out = []
    for step in range(1, blocks):
        if step < blocks - 2:
            out.append((step, every))
        else:
            out += [(step, (k,)) for k in every]
    return out


def shards(tokens, weights, key_mask, w_query, w_key, w_value, w_out):
    rows, cells, width = tokens.shape
    inner = w_query.shape[1]
    tiles = inner // LANES
    blocks = lax.axis_size("res")
    holders = lax.axis_size("seq")
    cores = lax.axis_size("head")
    part = HEAD_DIM
    share = rows // cores
    assert share * cores == rows and tiles * LANES == inner and part * CHUNKS == cells == LANES
    f32, bf16 = jnp.float32, jnp.bfloat16
    masked = MASKED / holders
    shape = pltpu.VMEM
    key_mask = key_mask.reshape(1, cells)

    length = share * part * width // LANES + MARK_ROWS
    moving = [
        pl.pallas_call(
            functools.partial(pack_kernel, chunk=k, share=share),
            out_shape=shape((length, LANES), bf16),
            in_specs=[pl.BlockSpec(memory_space=pl.ANY)] + whole(1),
            out_specs=whole(1)[0],
            scratch_shapes=[shape((share, part, width), bf16), pltpu.SemaphoreType.DMA],
            compiler_params=pltpu.CompilerParams(vmem_limit_bytes=VMEM_LIMIT),
        )(tokens, key_mask)
        for k in range(CHUNKS)
    ]
    counts = [weights]
    for k in range(1, holders):
        counts.append(ring(weights, "seq", k))

    def exchange(logits):
        return [logits] + [ring(logits, "seq", k) for k in range(1, holders)]

    depth = PER_TILE * part
    spans = rows * LANES
    query, logits, values = call(
        functools.partial(own_kernel, cores=cores, masked=masked),
        [
            shape((tiles, cells, spans), bf16),
            shape((CHUNKS, tiles, cells, depth), f32),
            shape((CHUNKS, tiles, depth, spans), bf16),
        ],
        counts + [key_mask, tokens, w_query, w_key, w_value],
        2 * rows * cells * inner * (3 * width + cells * PER_TILE),
        holders,
        [pltpu.VMEM((CHUNKS, tiles, depth, spans), bf16)],
    )
    units = [(exchange(logits), values)]

    pieces = {}
    for step in range(1, blocks):
        moving = [ring(moving[k], "res") for k in range(CHUNKS)]
        for k in range(CHUNKS):
            pieces[step, k] = [moving[k]] + [ring(moving[k], "head", j) for j in range(1, cores)]
    for step, taken in batches(blocks):
        count = len(taken)
        logits, values = call(
            functools.partial(project_kernel, order=taken, masked=masked),
            [shape((count, tiles, cells, depth), f32), shape((count, tiles, depth, spans), bf16)],
            [query, w_key, w_value] + sum([pieces[step, k] for k in taken], []),
            2 * rows * part * count * inner * (2 * width + cells * PER_TILE),
            0,
            [pltpu.VMEM((1, tiles, depth, spans), bf16)],
        )
        units.append((exchange(logits), values))

    state = []
    state_shape = [
        shape((tiles, cells, LANES), f32),
        shape((tiles, cells, LANES), f32),
        shape((tiles, cells, spans), f32),
    ]

    def flatten(group):
        return sum([list(u[0]) + [u[1]] for u in group], [])

    def work(group):
        return sum(2 * u[0][0].size * spans for u in group)

    cuts = groups_of(len(units))
    for cut in cuts[:-1]:
        group = units[slice(*cut)]
        state = call(
            functools.partial(absorb_kernel, sizes=[len(u[0]) for u in group], carried=bool(state)),
            state_shape,
            flatten(group) + list(state),
            work(group),
        )
    group = units[slice(*cuts[-1])]
    columns = width // cores
    attended, sent = call(
        functools.partial(
            finish_kernel, sizes=[len(u[0]) for u in group], carried=bool(state), cores=cores
        ),
        [shape((rows, cells, inner), bf16), shape((rows, cells, columns), bf16)],
        flatten(group) + list(state) + [w_out],
        work(group) + 2 * rows * cells * inner * columns,
    )

    def output(k):
        return call(
            functools.partial(output_kernel, ahead=k, cores=cores),
            shape((rows, cells, columns), f32),
            [attended, w_out],
            2 * rows * cells * inner * columns,
        )

    if cores == 1:
        return sent
    received = [ring(sent, "head")]
    for k in range(2, cores):
        received.append(ring(output(k).astype(bf16), "head", k))
    result = output(0)
    for value in received:
        result = result + value.astype(f32)
    return result.astype(bf16)


def groups_of(count):
    return [(at, min(at + 3, count - 1)) for at in range(0, count - 1, 3)] + [(count - 1, count)]


def solution(mesh):
    in_specs = (
        P(("grp", "seq"), "res", None),
        P(("grp", "seq")),
        P(("grp", "res")),
        P(None, "head"),
        P(None, "head"),
        P(None, "head"),
        P("head", None),
    )
    out_specs = P(("grp", "seq"), "res", "head")

    return jax.shard_map(shards, mesh=mesh, in_specs=in_specs, out_specs=out_specs, check_vma=False)
```

time: 85.3 us -> 84.7 us (level)
  waiting for transfers between devices: 47.6 us -> 54.8 us
  starting transfers between devices: 19 us -> 14.7 us
  local copies, waits for them, and re-layouts: 3.62 us -> 1.95 us
  other arithmetic: 2.3 us -> 0.93 us
    ppermute x24 -> x20, waiting for transfers between devices: 47.6 us -> 54.8 us  [ring(): lax.ppermute(value, axis, [(i, (i + by) % length) for i in range(length)])]
    ppermute x24 -> x20, starting transfers between devices: 19 us -> 14.7 us  [ring(): lax.ppermute(value, axis, [(i, (i + by) % length) for i in range(length)])]
    dynamic_slice x2 -> x0, local copies, waits for them, and re-layouts: 2.36 us -> none  [the longest x1 1.25 us: shards(): lax.dynamic_slice(tokens, (core * share, k * part, 0), (share, part, width))]
    unnamed x12 -> x18, local copies, waits for them, and re-layouts: 1.08 us -> 1.95 us
    pallas_call x11 -> x10, Pallas kernels: 12.4 us -> 11.7 us  [call(): pl.pallas_call(kernel, out_shape=out_shape, in_specs=specs, out_specs=who...]
  transfers between devices with their start and end apart: 24 -> 20, of which waited for: 13 -> 13; matrix products, arithmetic and copies ran while one was open for 3% -> 0% of each run, Pallas kernels for 13% -> 13%
where the time goes in v3:
time: 84.7 us; the launch traced here: 84.5 us
  waiting for transfers between devices  54.8 us (65%)
  starting transfers between devices  14.7 us (17%)
  Pallas kernels  11.9 us (14%)
  local copies, waits for them, and re-layouts  1.95 us (2%)
  other arithmetic  0.93 us (1%)
    ppermute x20, waiting for transfers between devices, ring(): lax.ppermute(value, axis, [(i, (i + by) % length) for i in range(length)])  54.8 us
    ppermute x20, starting transfers between devices, ring(): lax.ppermute(value, axis, [(i, (i + by) % length) for i in range(length)])  14.7 us
    pallas_call x10, Pallas kernels, call(): pl.pallas_call(kernel, out_shape=out_shape, in_specs=specs, out_specs=who...  11.7 us
    unnamed x18, local copies, waits for them, and re-layouts  1.95 us
  transfers between devices with their start and end apart: 20, of which 13 were waited for; matrix products, arithmetic and copies ran while one was open for 0% of the time, Pallas kernels for 13%

profile of v3, /device:TPU:0, one launch (start us, length us, event | category | flops | bytes accessed | tf_op | source)
XLA Modules:
  0.0 84.5 jit_solution(15225674444672915769)
XLA Ops:
  0.0 1.3 %copy-done.2 = bf16[6,128,768]{2,1,0:T(8,128)(2,1)S(1)} copy-done((bf16[6,128,768]{2,1,0:T(8,128)(2,1)S(1)}, bf16[6,128,768]{2,1,0:T(8,128)(2,1)}, u32[]{:S(2)}) %copy-start.2) | copy-done | bytes 1179672
  1.3 0.7 copy-done.5
  1.9 0.0 copy-start.6
  1.9 0.0 copy-start.7
  2.0 0.1 shard_map.77
  2.1 3.1 %collective-permute-start.8 = (bf16[1168,128]{1,0:T(8,128)(2,1)S(1)}, bf16[1168,128]{1,0:T(8,128)(2,1)S(1)}, u32[]{:S(2)}, u32[]{:S(2)}) collective-permute-start(bf16[1168,128]{1,0:T(8,128)(2,1)S(1)} %shard_map.77), channel_id=1, source_target_pairs={{0,4},{4,8},{8,12},{12,0},{1,5},{5,9},{9,13},{13,1},{2,6},{6,10},{... | collective-permute-start | bytes 897032 | tf_op jit(solution)/shard_map/ppermute | solution.py:23
  5.2 0.1 shard_map.74
  5.3 1.6 %collective-permute-start.1 = (bf16[1168,128]{1,0:T(8,128)(2,1)S(1)}, bf16[1168,128]{1,0:T(8,128)(2,1)S(1)}, u32[]{:S(2)}, u32[]{:S(2)}) collective-permute-start(bf16[1168,128]{1,0:T(8,128)(2,1)S(1)} %shard_map.74), channel_id=1, source_target_pairs={{0,4},{4,8},{8,12},{12,0},{1,5},{5,9},{9,13},{13,1},{2,6},{6,10},{... | collective-permute-start | bytes 897032 | tf_op jit(solution)/shard_map/ppermute | solution.py:23
  6.9 8.2 %collective-permute-done.8.refs_3_ = bf16[1168,128]{1,0:T(8,128)(2,1)S(1)} collective-permute-done((bf16[1168,128]{1,0:T(8,128)(2,1)S(1)}, bf16[1168,128]{1,0:T(8,128)(2,1)S(1)}, u32[]{:S(2)}, u32[]{:S(2)}) %collective-permute-start.8) | collective-permute-done | bytes 299040 | tf_op jit(solution)/shard_map/ppermute | solution.py:23
  15.1 0.0 collective-permute-start.9
  15.1 6.4 %collective-permute-done.1.refs_5_ = bf16[1168,128]{1,0:T(8,128)(2,1)S(1)} collective-permute-done((bf16[1168,128]{1,0:T(8,128)(2,1)S(1)}, bf16[1168,128]{1,0:T(8,128)(2,1)S(1)}, u32[]{:S(2)}, u32[]{:S(2)}) %collective-permute-start.1) | collective-permute-done | bytes 299040 | tf_op jit(solution)/shard_map/ppermute | solution.py:23
  21.5 0.0 collective-permute-start.2
  21.5 0.0 collective-permute-start.14
  21.6 6.4 %collective-permute-done.9.refs_3_ = bf16[1168,128]{1,0:T(8,128)(2,1)S(1)} collective-permute-done((bf16[1168,128]{1,0:T(8,128)(2,1)S(1)}, bf16[1168,128]{1,0:T(8,128)(2,1)S(1)}, u32[]{:S(2)}, u32[]{:S(2)}) %collective-permute-start.9) | collective-permute-done | bytes 299040 | tf_op jit(solution)/shard_map/ppermute | solution.py:23
  28.0 0.0 collective-permute-start.10
  28.0 0.0 collective-permute-start.15
  28.0 6.4 %collective-permute-done.2.refs_3_ = bf16[1168,128]{1,0:T(8,128)(2,1)S(1)} collective-permute-done((bf16[1168,128]{1,0:T(8,128)(2,1)S(1)}, bf16[1168,128]{1,0:T(8,128)(2,1)S(1)}, u32[]{:S(2)}, u32[]{:S(2)}) %collective-permute-start.2) | collective-permute-done | bytes 299040 | tf_op jit(solution)/shard_map/ppermute | solution.py:23
  34.4 0.0 collective-permute-start.3
  34.4 0.0 copy-done.8
  34.4 1.7 %collective-permute-start = (s32[6]{0:T(128)S(1)}, s32[6]{0:T(128)S(1)}, u32[]{:S(2)}, u32[]{:S(2)}) collective-permute-start(s32[6]{0:T(128)S(1)} %copy-done.8), channel_id=1, source_target_pairs={{0,2},{2,0},{1,3},{3,1},{4,6},{6,4},{5,7},{7,5},{8,10},{10,8},{9,1... | collective-permute-start | bytes 80 | tf_op jit(solution)/shard_map/ppermute | solution.py:23
  36.1 1.9 %collective-permute-done.refs_1_ = s32[6]{0:T(128)S(1)} collective-permute-done((s32[6]{0:T(128)S(1)}, s32[6]{0:T(128)S(1)}, u32[]{:S(2)}, u32[]{:S(2)}) %collective-permute-start) | collective-permute-done | bytes 56 | tf_op jit(solution)/shard_map/ppermute | solution.py:23
  37.9 0.0 collective-permute-start.17
  37.9 0.0 collective-permute-done.14.refs_4_
  37.9 0.5 collective-permute-start.6
  38.5 2.3 %collective-permute-done.10.refs_3_ = bf16[1168,128]{1,0:T(8,128)(2,1)S(1)} collective-permute-done((bf16[1168,128]{1,0:T(8,128)(2,1)S(1)}, bf16[1168,128]{1,0:T(8,128)(2,1)S(1)}, u32[]{:S(2)}, u32[]{:S(2)}) %collective-permute-start.10) | collective-permute-done | bytes 299040 | tf_op jit(solution)/shard_map/ppermute | solution.py:23
  40.8 0.0 collective-permute-start.11
  40.8 0.0 copy-done
  40.8 0.0 copy-done.1
  40.8 0.0 copy-done.3
  40.8 0.0 copy-done.6
  40.8 0.0 copy-done.7
  40.8 2.9 %shard_map.73 = (bf16[3,128,768]{2,1,0:T(8,128)(2,1)S(1)}, f32[2,3,128,128]{3,2,1,0:T(8,128)S(1)}, bf16[2,3,128,768]{3,2,1,0:T(8,128)(2,1)S(1)}) custom-call(s32[6]{0:T(128)S(1)} %copy-done.8, s32[6]{0:T(128)S(1)} %collective-permute-done.refs_1_, s32[1,128]{1,0:T(1,128)S(1)} %bitcast.3, bf16[6,128,768]{2,1,0:T(8,128)(2,1)S(1)} %copy-done.3, ...), custom_call_target="tpu_custom_call" | custom-call | flops 1509949440 | bytes 2949680 | tf_op jit(solution)/shard_map/pallas_call | solution.py:34
  43.7 0.0 collective-permute-done.15.refs_6_
  43.8 1.8 %collective-permute-start.13 = (f32[2,3,128,128]{3,2,1,0:T(8,128)S(1)}, f32[2,3,128,128]{3,2,1,0:T(8,128)S(1)}, u32[]{:S(2)}, u32[]{:S(2)}) collective-permute-start(f32[2,3,128,128]{3,2,1,0:T(8,128)S(1)} %get-tuple-element.33.refs_0_), channel_id=1, source_target_pairs={{0,2},{2,0},{1,3},{3,1},{4,6},{6,4},{5,7},{7,5},{8,10},{10,8},{9,1... | collective-permute-start | bytes 1179656 | tf_op jit(solution)/shard_map/ppermute | solution.py:23
  45.5 0.8 collective-permute-done.3.refs_3_
  46.3 0.0 collective-permute-start.4
  46.3 1.9 %shard_map.79 = (f32[2,3,128,128]{3,2,1,0:T(8,128)S(1)}, bf16[2,3,128,768]{3,2,1,0:T(8,128)(2,1)S(1)}) custom-call(bf16[3,128,768]{2,1,0:T(8,128)(2,1)S(1)} %get-tuple-element.26.refs_0_, bf16[768,384]{1,0:T(8,128)(2,1)S(1)} %copy-done, bf16[768,384]{1,0:T(8,128)(2,1)S(1)} %copy-done.1, bf16[1168,128]{1,0:T(8,128)(2,1)S(1)} %collective-permute-done.8.refs_3_, ...), custom_call_target="tpu_custom_call" | custom-call | flops 1056964608 | bytes 2965504 | tf_op jit(solution)/shard_map/pallas_call | solution.py:34
  48.3 0.0 collective-permute-done.17.refs_4_
  48.3 1.6 %collective-permute-start.16 = (f32[2,3,128,128]{3,2,1,0:T(8,128)S(1)}, f32[2,3,128,128]{3,2,1,0:T(8,128)S(1)}, u32[]{:S(2)}, u32[]{:S(2)}) collective-permute-start(f32[2,3,128,128]{3,2,1,0:T(8,128)S(1)} %get-tuple-element.35.refs_3_), channel_id=1, source_target_pairs={{0,2},{2,0},{1,3},{3,1},{4,6},{6,4},{5,7},{7,5},{8,10},{10,8},{9,1... | collective-permute-start | bytes 1179656 | tf_op jit(solution)/shard_map/ppermute | solution.py:23
  49.9 1.1 %shard_map.80 = (f32[1,3,128,128]{3,2,1,0:T(8,128)S(1)}, bf16[1,3,128,768]{3,2,1,0:T(8,128)(2,1)S(1)}) custom-call(bf16[3,128,768]{2,1,0:T(8,128)(2,1)S(1)} %get-tuple-element.26.refs_0_, bf16[768,384]{1,0:T(8,128)(2,1)S(1)} %copy-done, bf16[768,384]{1,0:T(8,128)(2,1)S(1)} %copy-done.1, bf16[1168,128]{1,0:T(8,128)(2,1)S(1)} %collective-permute-done.9.refs_3_, ...), custom_call_target="tpu_custom_call" | custom-call | flops 528482304 | bytes 2367488 | tf_op jit(solution)/shard_map/pallas_call | solution.py:34
  50.9 0.0 collective-permute-done.6.refs_4_
  50.9 0.6 collective-permute-start.18
  51.5 1.1 %shard_map.76 = (f32[1,3,128,128]{3,2,1,0:T(8,128)S(1)}, bf16[1,3,128,768]{3,2,1,0:T(8,128)(2,1)S(1)}) custom-call(bf16[3,128,768]{2,1,0:T(8,128)(2,1)S(1)} %get-tuple-element.26.refs_0_, bf16[768,384]{1,0:T(8,128)(2,1)S(1)} %copy-done, bf16[768,384]{1,0:T(8,128)(2,1)S(1)} %copy-done.1, bf16[1168,128]{1,0:T(8,128)(2,1)S(1)} %collective-permute-done.2.refs_3_, ...), custom_call_target="tpu_custom_call" | custom-call | flops 528482304 | bytes 2367488 | tf_op jit(solution)/shard_map/pallas_call | solution.py:34
  52.6 0.0 collective-permute-done.11.refs_4_
  52.6 1.6 %collective-permute-start.7 = (f32[1,3,128,128]{3,2,1,0:T(8,128)S(1)}, f32[1,3,128,128]{3,2,1,0:T(8,128)S(1)}, u32[]{:S(2)}, u32[]{:S(2)}) collective-permute-start(f32[1,3,128,128]{3,2,1,0:T(8,128)S(1)} %get-tuple-element.29.refs_0_), channel_id=1, source_target_pairs={{0,2},{2,0},{1,3},{3,1},{4,6},{6,4},{5,7},{7,5},{8,10},{10,8},{9,1... | collective-permute-start | bytes 589832 | tf_op jit(solution)/shard_map/ppermute | solution.py:23
  54.2 1.1 %shard_map.78 = (f32[1,3,128,128]{3,2,1,0:T(8,128)S(1)}, bf16[1,3,128,768]{3,2,1,0:T(8,128)(2,1)S(1)}) custom-call(bf16[3,128,768]{2,1,0:T(8,128)(2,1)S(1)} %get-tuple-element.26.refs_0_, bf16[768,384]{1,0:T(8,128)(2,1)S(1)} %copy-done, bf16[768,384]{1,0:T(8,128)(2,1)S(1)} %copy-done.1, bf16[1168,128]{1,0:T(8,128)(2,1)S(1)} %collective-permute-done.10.refs_3_, ...), custom_call_target="tpu_custom_call" | custom-call | flops 528482304 | bytes 2367488 | tf_op jit(solution)/shard_map/pallas_call | solution.py:34
  55.2 0.0 collective-permute-done.4.refs_4_
  55.2 0.6 collective-permute-start.12
  55.8 1.1 %shard_map.75 = (f32[1,3,128,128]{3,2,1,0:T(8,128)S(1)}, bf16[1,3,128,768]{3,2,1,0:T(8,128)(2,1)S(1)}) custom-call(bf16[3,128,768]{2,1,0:T(8,128)(2,1)S(1)} %get-tuple-element.26.refs_0_, bf16[768,384]{1,0:T(8,128)(2,1)S(1)} %copy-done, bf16[768,384]{1,0:T(8,128)(2,1)S(1)} %copy-done.1, bf16[1168,128]{1,0:T(8,128)(2,1)S(1)} %collective-permute-done.3.refs_3_, ...), custom_call_target="tpu_custom_call" | custom-call | flops 528482304 | bytes 2367488 | tf_op jit(solution)/shard_map/pallas_call | solution.py:34
  56.9 0.0 collective-permute-done.13.refs_1_
  56.9 1.6 %collective-permute-start.5 = (f32[1,3,128,128]{3,2,1,0:T(8,128)S(1)}, f32[1,3,128,128]{3,2,1,0:T(8,128)S(1)}, u32[]{:S(2)}, u32[]{:S(2)}) collective-permute-start(f32[1,3,128,128]{3,2,1,0:T(8,128)S(1)} %get-tuple-element.27.refs_0_), channel_id=1, source_target_pairs={{0,2},{2,0},{1,3},{3,1},{4,6},{6,4},{5,7},{7,5},{8,10},{10,8},{9,1... | collective-permute-start | bytes 589832 | tf_op jit(solution)/shard_map/ppermute | solution.py:23
  58.4 5.8 %collective-permute-done.16.refs_4_ = f32[2,3,128,128]{3,2,1,0:T(8,128)S(1)} collective-permute-done((f32[2,3,128,128]{3,2,1,0:T(8,128)S(1)}, f32[2,3,128,128]{3,2,1,0:T(8,128)S(1)}, u32[]{:S(2)}, u32[]{:S(2)}) %collective-permute-start.16) | collective-permute-done | bytes 393248 | tf_op jit(solution)/shard_map/ppermute | solution.py:23
  64.2 4.2 %collective-permute-done.18.refs_7_ = f32[1,3,128,128]{3,2,1,0:T(8,128)S(1)} collective-permute-done((f32[1,3,128,128]{3,2,1,0:T(8,128)S(1)}, f32[1,3,128,128]{3,2,1,0:T(8,128)S(1)}, u32[]{:S(2)}, u32[]{:S(2)}) %collective-permute-start.18) | collective-permute-done | bytes 196640 | tf_op jit(solution)/shard_map/ppermute | solution.py:23
  68.4 0.8 shard_map.81
  69.2 3.4 %collective-permute-done.7.refs_1_ = f32[1,3,128,128]{3,2,1,0:T(8,128)S(1)} collective-permute-done((f32[1,3,128,128]{3,2,1,0:T(8,128)S(1)}, f32[1,3,128,128]{3,2,1,0:T(8,128)S(1)}, u32[]{:S(2)}, u32[]{:S(2)}) %collective-permute-start.7) | collective-permute-done | bytes 196640 | tf_op jit(solution)/shard_map/ppermute | solution.py:23
  72.7 4.2 %collective-permute-done.12.refs_4_ = f32[1,3,128,128]{3,2,1,0:T(8,128)S(1)} collective-permute-done((f32[1,3,128,128]{3,2,1,0:T(8,128)S(1)}, f32[1,3,128,128]{3,2,1,0:T(8,128)S(1)}, u32[]{:S(2)}, u32[]{:S(2)}) %collective-permute-start.12) | collective-permute-done | bytes 196640 | tf_op jit(solution)/shard_map/ppermute | solution.py:23
  76.9 0.4 shard_map.82
  77.3 3.3 %collective-permute-done.5.refs_1_ = f32[1,3,128,128]{3,2,1,0:T(8,128)S(1)} collective-permute-done((f32[1,3,128,128]{3,2,1,0:T(8,128)S(1)}, f32[1,3,128,128]{3,2,1,0:T(8,128)S(1)}, u32[]{:S(2)}, u32[]{:S(2)}) %collective-permute-start.5) | collective-permute-done | bytes 196640 | tf_op jit(solution)/shard_map/ppermute | solution.py:23
  80.6 0.0 copy-done.4
  80.6 0.9 %shard_map.83 = (bf16[6,128,384]{2,1,0:T(8,128)(2,1)S(1)}, bf16[6,128,384]{2,1,0:T(8,128)(2,1)S(1)}) custom-call(f32[1,3,128,128]{3,2,1,0:T(8,128)S(1)} %get-tuple-element.27.refs_0_, f32[1,3,128,128]{3,2,1,0:T(8,128)S(1)} %collective-permute-done.5.refs_1_, bf16[1,3,128,768]{3,2,1,0:T(8,128)(2,1)S(1)} %get-tuple-element.28.refs_2_, ...), custom_call_target="tpu_custom_call" | custom-call | flops 301989888 | bytes 3145728 | tf_op jit(solution)/shard_map/pallas_call | solution.py:34
  81.5 0.1 collective-permute-start.19
  81.6 0.6 shard_map.84
  82.2 1.4 %collective-permute-done.19 = bf16[6,128,384]{2,1,0:T(8,128)(2,1)S(1)} collective-permute-done((bf16[6,128,384]{2,1,0:T(8,128)(2,1)S(1)}, bf16[6,128,384]{2,1,0:T(8,128)(2,1)S(1)}, u32[]{:S(2)}, u32[]{:S(2)}) %collective-permute-start.19) | collective-permute-done | bytes 589856 | tf_op jit(solution)/shard_map/ppermute | solution.py:23
  83.6 0.9 %add_convert_fusion = bf16[6,128,384]{2,1,0:T(8,128)(2,1)} fusion(f32[6,128,384]{2,1,0:T(8,128)S(1)} %shard_map.84, bf16[6,128,384]{2,1,0:T(8,128)(2,1)S(1)} %collective-permute-done.19), kind=kLoop, calls=%fused_computation | loop fusion | flops 884736 | bytes 2359296 | tf_op jit(solution)/shard_map/convert_element_type | solution.py:373
  (7 shorter events, 0.0 us)
Async XLA Ops:
  0.0 1.3 %copy-start.2 = (bf16[6,128,768]{2,1,0:T(8,128)(2,1)S(1)}, bf16[6,128,768]{2,1,0:T(8,128)(2,1)}, u32[]{:S(2)}) copy-start(bf16[6,128,768]{2,1,0:T(8,128)(2,1)} %tokens.3) | copy-start | bytes 3538948
  1.3 0.7 copy-start.5
  1.9 32.4 %copy-start.8 = (s32[6]{0:T(128)S(1)}, s32[6]{0:T(128)}, u32[]{:S(2)}) copy-start(s32[6]{0:T(128)} %refs_0_.1) | copy-start | bytes 76
  1.9 38.8 %copy-start = (bf16[768,384]{1,0:T(8,128)(2,1)S(1)}, bf16[768,384]{1,0:T(8,128)(2,1)}, u32[]{:S(2)}) copy-start(bf16[768,384]{1,0:T(8,128)(2,1)} %refs_1_.9) | copy-start | bytes 1769476
  1.9 38.8 %copy-start.1 = (bf16[768,384]{1,0:T(8,128)(2,1)S(1)}, bf16[768,384]{1,0:T(8,128)(2,1)}, u32[]{:S(2)}) copy-start(bf16[768,384]{1,0:T(8,128)(2,1)} %refs_2_.9) | copy-start | bytes 1769476
  1.9 38.8 %copy-start.3 = (bf16[6,128,768]{2,1,0:T(8,128)(2,1)S(1)}, bf16[6,128,768]{2,1,0:T(8,128)(2,1)}, u32[]{:S(2)}) copy-start(bf16[6,128,768]{2,1,0:T(8,128)(2,1)} %tokens.3) | copy-start | bytes 3538948
  1.9 38.9 %copy-start.6 = (s32[128]{0:T(128)S(1)}, s32[128]{0:T(128)}, u32[]{:S(2)}) copy-start(s32[128]{0:T(128)} %param.9) | copy-start | bytes 1540
  1.9 38.9 %copy-start.7 = (bf16[768,384]{1,0:T(8,128)(2,1)S(1)}, bf16[768,384]{1,0:T(8,128)(2,1)}, u32[]{:S(2)}) copy-start(bf16[768,384]{1,0:T(8,128)(2,1)} %refs_4_.1) | copy-start | bytes 1769476
  2.1 13.1 %collective-permute-start.8 = (bf16[1168,128]{1,0:T(8,128)(2,1)S(1)}, bf16[1168,128]{1,0:T(8,128)(2,1)S(1)}, u32[]{:S(2)}, u32[]{:S(2)}) collective-permute-start(bf16[1168,128]{1,0:T(8,128)(2,1)S(1)} %shard_map.77), channel_id=1, source_target_pairs={{0,4},{4,8},{8,12},{12,0},{1,5},{5,9},{9,13},{13,1},{2,6},{6,10},{... | collective-permute-start | bytes 897032 | tf_op jit(solution)/shard_map/ppermute | solution.py:23
  5.3 16.3 %collective-permute-start.1 = (bf16[1168,128]{1,0:T(8,128)(2,1)S(1)}, bf16[1168,128]{1,0:T(8,128)(2,1)S(1)}, u32[]{:S(2)}, u32[]{:S(2)}) collective-permute-start(bf16[1168,128]{1,0:T(8,128)(2,1)S(1)} %shard_map.74), channel_id=1, source_target_pairs={{0,4},{4,8},{8,12},{12,0},{1,5},{5,9},{9,13},{13,1},{2,6},{6,10},{... | collective-permute-start | bytes 897032 | tf_op jit(solution)/shard_map/ppermute | solution.py:23
  15.1 12.8 %collective-permute-start.9 = (bf16[1168,128]{1,0:T(8,128)(2,1)S(1)}, bf16[1168,128]{1,0:T(8,128)(2,1)S(1)}, u32[]{:S(2)}, u32[]{:S(2)}) collective-permute-start(bf16[1168,128]{1,0:T(8,128)(2,1)S(1)} %collective-permute-done.8.refs_3_), channel_id=1, source_target_pairs={{0,4},{4,8},{8,12},{12,0},{1,5},{5,9},{9,13},{13,1},{2,6},{6,10},{... | collective-permute-start | bytes 897032 | tf_op jit(solution)/shard_map/ppermute | solution.py:23
  21.5 12.8 %collective-permute-start.2 = (bf16[1168,128]{1,0:T(8,128)(2,1)S(1)}, bf16[1168,128]{1,0:T(8,128)(2,1)S(1)}, u32[]{:S(2)}, u32[]{:S(2)}) collective-permute-start(bf16[1168,128]{1,0:T(8,128)(2,1)S(1)} %collective-permute-done.1.refs_5_), channel_id=1, source_target_pairs={{0,4},{4,8},{8,12},{12,0},{1,5},{5,9},{9,13},{13,1},{2,6},{6,10},{... | collective-permute-start | bytes 897032 | tf_op jit(solution)/shard_map/ppermute | solution.py:23
  21.5 16.4 %collective-permute-start.14 = (bf16[1168,128]{1,0:T(8,128)(2,1)S(1)}, bf16[1168,128]{1,0:T(8,128)(2,1)S(1)}, u32[]{:S(2)}, u32[]{:S(2)}) collective-permute-start(bf16[1168,128]{1,0:T(8,128)(2,1)S(1)} %collective-permute-done.8.refs_3_), channel_id=1, source_target_pairs={{0,1},{1,0},{2,3},{3,2},{4,5},{5,4},{6,7},{7,6},{8,9},{9,8},{10,11... | collective-permute-start | bytes 897032 | tf_op jit(solution)/shard_map/ppermute | solution.py:23
  28.0 12.8 %collective-permute-start.10 = (bf16[1168,128]{1,0:T(8,128)(2,1)S(1)}, bf16[1168,128]{1,0:T(8,128)(2,1)S(1)}, u32[]{:S(2)}, u32[]{:S(2)}) collective-permute-start(bf16[1168,128]{1,0:T(8,128)(2,1)S(1)} %collective-permute-done.9.refs_3_), channel_id=1, source_target_pairs={{0,4},{4,8},{8,12},{12,0},{1,5},{5,9},{9,13},{13,1},{2,6},{6,10},{... | collective-permute-start | bytes 897032 | tf_op jit(solution)/shard_map/ppermute | solution.py:23
  28.0 15.8 %collective-permute-start.15 = (bf16[1168,128]{1,0:T(8,128)(2,1)S(1)}, bf16[1168,128]{1,0:T(8,128)(2,1)S(1)}, u32[]{:S(2)}, u32[]{:S(2)}) collective-permute-start(bf16[1168,128]{1,0:T(8,128)(2,1)S(1)} %collective-permute-done.1.refs_5_), channel_id=1, source_target_pairs={{0,1},{1,0},{2,3},{3,2},{4,5},{5,4},{6,7},{7,6},{8,9},{9,8},{10,11... | collective-permute-start | bytes 897032 | tf_op jit(solution)/shard_map/ppermute | solution.py:23
  34.4 12.0 %collective-permute-start.3 = (bf16[1168,128]{1,0:T(8,128)(2,1)S(1)}, bf16[1168,128]{1,0:T(8,128)(2,1)S(1)}, u32[]{:S(2)}, u32[]{:S(2)}) collective-permute-start(bf16[1168,128]{1,0:T(8,128)(2,1)S(1)} %collective-permute-done.2.refs_3_), channel_id=1, source_target_pairs={{0,4},{4,8},{8,12},{12,0},{1,5},{5,9},{9,13},{13,1},{2,6},{6,10},{... | collective-permute-start | bytes 897032 | tf_op jit(solution)/shard_map/ppermute | solution.py:23
  34.4 3.6 %collective-permute-start = (s32[6]{0:T(128)S(1)}, s32[6]{0:T(128)S(1)}, u32[]{:S(2)}, u32[]{:S(2)}) collective-permute-start(s32[6]{0:T(128)S(1)} %copy-done.8), channel_id=1, source_target_pairs={{0,2},{2,0},{1,3},{3,1},{4,6},{6,4},{5,7},{7,5},{8,10},{10,8},{9,1... | collective-permute-start | bytes 80 | tf_op jit(solution)/shard_map/ppermute | solution.py:23
  37.9 10.3 %collective-permute-start.17 = (bf16[1168,128]{1,0:T(8,128)(2,1)S(1)}, bf16[1168,128]{1,0:T(8,128)(2,1)S(1)}, u32[]{:S(2)}, u32[]{:S(2)}) collective-permute-start(bf16[1168,128]{1,0:T(8,128)(2,1)S(1)} %collective-permute-done.9.refs_3_), channel_id=1, source_target_pairs={{0,1},{1,0},{2,3},{3,2},{4,5},{5,4},{6,7},{7,6},{8,9},{9,8},{10,11... | collective-permute-start | bytes 897032 | tf_op jit(solution)/shard_map/ppermute | solution.py:23
  37.9 13.0 %collective-permute-start.6 = (bf16[1168,128]{1,0:T(8,128)(2,1)S(1)}, bf16[1168,128]{1,0:T(8,128)(2,1)S(1)}, u32[]{:S(2)}, u32[]{:S(2)}) collective-permute-start(bf16[1168,128]{1,0:T(8,128)(2,1)S(1)} %collective-permute-done.2.refs_3_), channel_id=1, source_target_pairs={{0,1},{1,0},{2,3},{3,2},{4,5},{5,4},{6,7},{7,6},{8,9},{9,8},{10,11... | collective-permute-start | bytes 897032 | tf_op jit(solution)/shard_map/ppermute | solution.py:23
  40.8 11.8 %collective-permute-start.11 = (bf16[1168,128]{1,0:T(8,128)(2,1)S(1)}, bf16[1168,128]{1,0:T(8,128)(2,1)S(1)}, u32[]{:S(2)}, u32[]{:S(2)}) collective-permute-start(bf16[1168,128]{1,0:T(8,128)(2,1)S(1)} %collective-permute-done.10.refs_3_), channel_id=1, source_target_pairs={{0,1},{1,0},{2,3},{3,2},{4,5},{5,4},{6,7},{7,6},{8,9},{9,8},{10,11... | collective-permute-start | bytes 897032 | tf_op jit(solution)/shard_map/ppermute | solution.py:23
  43.8 13.1 %collective-permute-start.13 = (f32[2,3,128,128]{3,2,1,0:T(8,128)S(1)}, f32[2,3,128,128]{3,2,1,0:T(8,128)S(1)}, u32[]{:S(2)}, u32[]{:S(2)}) collective-permute-start(f32[2,3,128,128]{3,2,1,0:T(8,128)S(1)} %get-tuple-element.33.refs_0_), channel_id=1, source_target_pairs={{0,2},{2,0},{1,3},{3,1},{4,6},{6,4},{5,7},{7,5},{8,10},{10,8},{9,1... | collective-permute-start | bytes 1179656 | tf_op jit(solution)/shard_map/ppermute | solution.py:23
  46.3 8.9 %collective-permute-start.4 = (bf16[1168,128]{1,0:T(8,128)(2,1)S(1)}, bf16[1168,128]{1,0:T(8,128)(2,1)S(1)}, u32[]{:S(2)}, u32[]{:S(2)}) collective-permute-start(bf16[1168,128]{1,0:T(8,128)(2,1)S(1)} %collective-permute-done.3.refs_3_), channel_id=1, source_target_pairs={{0,1},{1,0},{2,3},{3,2},{4,5},{5,4},{6,7},{7,6},{8,9},{9,8},{10,11... | collective-permute-start | bytes 897032 | tf_op jit(solution)/shard_map/ppermute | solution.py:23
  48.3 15.9 %collective-permute-start.16 = (f32[2,3,128,128]{3,2,1,0:T(8,128)S(1)}, f32[2,3,128,128]{3,2,1,0:T(8,128)S(1)}, u32[]{:S(2)}, u32[]{:S(2)}) collective-permute-start(f32[2,3,128,128]{3,2,1,0:T(8,128)S(1)} %get-tuple-element.35.refs_3_), channel_id=1, source_target_pairs={{0,2},{2,0},{1,3},{3,1},{4,6},{6,4},{5,7},{7,5},{8,10},{10,8},{9,1... | collective-permute-start | bytes 1179656 | tf_op jit(solution)/shard_map/ppermute | solution.py:23
  50.9 17.5 %collective-permute-start.18 = (f32[1,3,128,128]{3,2,1,0:T(8,128)S(1)}, f32[1,3,128,128]{3,2,1,0:T(8,128)S(1)}, u32[]{:S(2)}, u32[]{:S(2)}) collective-permute-start(f32[1,3,128,128]{3,2,1,0:T(8,128)S(1)} %get-tuple-element.37.refs_6_), channel_id=1, source_target_pairs={{0,2},{2,0},{1,3},{3,1},{4,6},{6,4},{5,7},{7,5},{8,10},{10,8},{9,1... | collective-permute-start | bytes 589832 | tf_op jit(solution)/shard_map/ppermute | solution.py:23
  52.6 20.1 %collective-permute-start.7 = (f32[1,3,128,128]{3,2,1,0:T(8,128)S(1)}, f32[1,3,128,128]{3,2,1,0:T(8,128)S(1)}, u32[]{:S(2)}, u32[]{:S(2)}) collective-permute-start(f32[1,3,128,128]{3,2,1,0:T(8,128)S(1)} %get-tuple-element.29.refs_0_), channel_id=1, source_target_pairs={{0,2},{2,0},{1,3},{3,1},{4,6},{6,4},{5,7},{7,5},{8,10},{10,8},{9,1... | collective-permute-start | bytes 589832 | tf_op jit(solution)/shard_map/ppermute | solution.py:23
  55.2 21.6 %collective-permute-start.12 = (f32[1,3,128,128]{3,2,1,0:T(8,128)S(1)}, f32[1,3,128,128]{3,2,1,0:T(8,128)S(1)}, u32[]{:S(2)}, u32[]{:S(2)}) collective-permute-start(f32[1,3,128,128]{3,2,1,0:T(8,128)S(1)} %get-tuple-element.31.refs_3_), channel_id=1, source_target_pairs={{0,2},{2,0},{1,3},{3,1},{4,6},{6,4},{5,7},{7,5},{8,10},{10,8},{9,1... | collective-permute-start | bytes 589832 | tf_op jit(solution)/shard_map/ppermute | solution.py:23
  56.9 23.7 %collective-permute-start.5 = (f32[1,3,128,128]{3,2,1,0:T(8,128)S(1)}, f32[1,3,128,128]{3,2,1,0:T(8,128)S(1)}, u32[]{:S(2)}, u32[]{:S(2)}) collective-permute-start(f32[1,3,128,128]{3,2,1,0:T(8,128)S(1)} %get-tuple-element.27.refs_0_), channel_id=1, source_target_pairs={{0,2},{2,0},{1,3},{3,1},{4,6},{6,4},{5,7},{7,5},{8,10},{10,8},{9,1... | collective-permute-start | bytes 589832 | tf_op jit(solution)/shard_map/ppermute | solution.py:23
  76.9 3.7 %copy-start.4 = (bf16[384,768]{1,0:T(8,128)(2,1)S(1)}, bf16[384,768]{1,0:T(8,128)(2,1)}, u32[]{:S(2)}) copy-start(bf16[384,768]{1,0:T(8,128)(2,1)} %w_out.1) | copy-start | bytes 1769476
  81.5 2.1 %collective-permute-start.19 = (bf16[6,128,384]{2,1,0:T(8,128)(2,1)S(1)}, bf16[6,128,384]{2,1,0:T(8,128)(2,1)S(1)}, u32[]{:S(2)}, u32[]{:S(2)}) collective-permute-start(bf16[6,128,384]{2,1,0:T(8,128)(2,1)S(1)} %get-tuple-element.46), channel_id=1, source_target_pairs={{0,1},{1,0},{2,3},{3,2},{4,5},{5,4},{6,7},{7,6},{8,9},{9,8},{10,11... | collective-permute-start | bytes 1769480 | tf_op jit(solution)/shard_map/ppermute | solution.py:23

commit v4 on v3

--- a/solution.py
+++ b/solution.py
@@ -13,7 +13,7 @@
 LANES = 128
 PER_TILE = LANES // HEAD_DIM
 CHUNKS = 2
-MARK_ROWS = 16
+MARK_ROWS = 8
 MASKED = -1000000000.0
 VMEM_LIMIT = 24 * 1024 * 1024
 
@@ -99,48 +99,82 @@
     return jnp.where(live, dot_nt(query, keys), masked)
 
 
-def pack_kernel(tokens, mask, packed, landing, done, *, chunk, share):
+def pack_kernel(tokens, mask, packed, landing, marks, done, *, chunk, share):
     _, part, width = landing.shape
     core = lax.axis_index("head")
-    copy = pltpu.make_async_copy(
-        tokens.at[pl.ds(core * share, share), pl.ds(chunk * part, part)], landing, done
-    )
-    copy.start()
     size = share * part
-    tail = packed.shape[0] - width // LANES * size
-    packed[width // LANES * size :] = jnp.broadcast_to(
-        mask[...].astype(jnp.float32), (tail, LANES)
-    ).astype(jnp.bfloat16)
-    copy.wait()
+    used = width // LANES * size
+    copies = [
+        pltpu.make_async_copy(
+            tokens.at[pl.ds(core * share, share), pl.ds(chunk * part, part)], landing, done.at[0]
+        )
+    ]
+    if packed.shape[0] > used:
+        copies.append(pltpu.make_async_copy(mask, marks, done.at[1]))
+    for copy in copies:
+        copy.start()
+    for copy in copies:
+        copy.wait()
     for tile in range(width // LANES):
         at = slice(tile * LANES, (tile + 1) * LANES)
         packed[tile * size : (tile + 1) * size] = landing[:, :, at].reshape(size, LANES)
-
-
-def unpack(packed, width, size):
-    return jnp.concatenate(
-        [packed[tile * size : (tile + 1) * size] for tile in range(width // LANES)], axis=1
-    )
+    if packed.shape[0] > used:
+        tail = packed.shape[0] - used
+        packed[used:] = jnp.broadcast_to(marks[...].astype(jnp.float32), (tail, LANES)).astype(jnp.bfloat16)
+
+
+def unpack(pieces, width):
+    tiles = width // LANES
+    flats = []
+    for piece in pieces:
+        size = piece.shape[0] // tiles // HEAD_DIM * HEAD_DIM
+        flats.append(
+            jnp.concatenate([piece[tile * size : (tile + 1) * size] for tile in range(tiles)], axis=1)
+        )
+    return jnp.concatenate(flats, axis=0)
+
+
+def marks_of(piece):
+    return piece[piece.shape[0] - MARK_ROWS :].astype(jnp.float32)
 
 
 def project_kernel(*refs, order, masked):
     query, w_key, w_value = refs[:3]
     pieces = refs[3:-3]
     logits, values, keys = refs[-3:]
-    tiles, width = query.shape[0], w_key.shape[0]
-    chunks = len(order)
-    per_chunk = len(pieces) // chunks
+    width = w_key.shape[0]
+    per_chunk = len(pieces) // len(order)
     part = keys.shape[2] // PER_TILE
-    size = (pieces[0].shape[0] - MARK_ROWS) * LANES // width
-    for at in range(chunks):
-        own = pieces[at * per_chunk : (at + 1) * per_chunk]
-        flat = jnp.concatenate([unpack(piece, width, size) for piece in own], axis=0)
+    for at, chunk in enumerate(order):
+        flat = unpack(pieces[at * per_chunk : (at + 1) * per_chunk], width)
         spread(keys, 0, dot(flat, w_key[...]).astype(jnp.bfloat16), 0, part)
-        mask = own[0][own[0].shape[0] - MARK_ROWS :].astype(jnp.float32)
-        live = live_lanes(mask[:8], order[at])
-        for tile in range(tiles):
+        live = live_lanes(marks_of(pieces[0]), chunk)
+        for tile in range(query.shape[0]):
             logits[at, tile] = score(query[tile], keys[0, tile], live, masked)
         spread(values, at, dot(flat, w_value[...]).astype(jnp.bfloat16), 0, part)
+
+
+def early_kernel(query, w_key, piece, logits, keys):
+    spread(keys, 0, dot(unpack([piece], w_key.shape[0]), w_key[...]).astype(jnp.bfloat16), 0, HEAD_DIM)
+    for tile in range(query.shape[0]):
+        logits[0, tile] = dot_nt(query[tile, :, : keys.shape[3]], keys[0, tile])
+
+
+def late_kernel(query, w_key, marks, before, *refs, chunk, masked):
+    pieces, (logits, keys) = refs[:-2], refs[-2:]
+    flat = unpack(pieces, w_key.shape[0])
+    spread(keys, 0, dot(flat, w_key[...]).astype(jnp.bfloat16), 0, HEAD_DIM)
+    live = live_lanes(marks_of(marks), chunk)
+    skip = query.shape[2] - keys.shape[3]
+    for tile in range(query.shape[0]):
+        total = before[0, tile] + dot_nt(query[tile, :, skip:], keys[0, tile])
+        logits[0, tile] = jnp.where(live, total, masked)
+
+
+def values_kernel(w_value, *refs):
+    pieces, values = refs[:-1], refs[-1]
+    flat = unpack(pieces, w_value.shape[0])
+    spread(values, 0, dot(flat, w_value[...]).astype(jnp.bfloat16), 0, HEAD_DIM)
 
 
 def own_kernel(*refs, cores, masked):
@@ -269,16 +303,21 @@
     shape = pltpu.VMEM
     key_mask = key_mask.reshape(1, cells)
 
-    length = share * part * width // LANES + MARK_ROWS
+    length = share * part * width // LANES
+    hbm = pl.BlockSpec(memory_space=pltpu.HBM)
     moving = [
         pl.pallas_call(
             functools.partial(pack_kernel, chunk=k, share=share),
-            out_shape=shape((length, LANES), bf16),
-            in_specs=[pl.BlockSpec(memory_space=pl.ANY)] + whole(1),
+            out_shape=shape((length + (0 if k else MARK_ROWS), LANES), bf16),
+            in_specs=[hbm, hbm],
             out_specs=whole(1)[0],
-            scratch_shapes=[shape((share, part, width), bf16), pltpu.SemaphoreType.DMA],
+            scratch_shapes=[
+                shape((share, part, width), bf16),
+                shape((1, cells), jnp.int32),
+                pltpu.SemaphoreType.DMA((2,)),
+            ],
             compiler_params=pltpu.CompilerParams(vmem_limit_bytes=VMEM_LIMIT),
-        )(tokens, key_mask)
+        )(pltpu.with_memory_space_constraint(tokens, pltpu.HBM), pltpu.with_memory_space_constraint(key_mask, pltpu.HBM))
         for k in range(CHUNKS)
     ]
     counts = [weights]
@@ -304,22 +343,54 @@
     )
     units = [(exchange(logits), values)]
 
-    pieces = {}
+    pieces, moved = {}, {}
     for step in range(1, blocks):
         moving = [ring(moving[k], "res") for k in range(CHUNKS)]
+        moved[step] = moving[0]
         for k in range(CHUNKS):
             pieces[step, k] = [moving[k]] + [ring(moving[k], "head", j) for j in range(1, cores)]
+
+    def kernel(function, outs, args, rows, both, scratch_rows):
+        return call(
+            function,
+            outs,
+            args,
+            2 * rows * part * inner * (both * width + cells * PER_TILE),
+            0,
+            [shape((1, tiles, depth, scratch_rows * LANES), bf16)] if scratch_rows else (),
+        )
+
     for step, taken in batches(blocks):
         count = len(taken)
-        logits, values = call(
-            functools.partial(project_kernel, order=taken, masked=masked),
-            [shape((count, tiles, cells, depth), f32), shape((count, tiles, depth, spans), bf16)],
-            [query, w_key, w_value] + sum([pieces[step, k] for k in taken], []),
-            2 * rows * part * count * inner * (2 * width + cells * PER_TILE),
-            0,
-            [pltpu.VMEM((1, tiles, depth, spans), bf16)],
-        )
-        units.append((exchange(logits), values))
+        logits_shape = shape((count, tiles, cells, depth), f32)
+        values_shape = shape((count, tiles, depth, spans), bf16)
+        if count > 1 or cores == 1:
+            mine = sum([pieces[step, k] for k in taken], [])
+            project = functools.partial(project_kernel, order=taken, masked=masked)
+            logits, values = kernel(
+                project,
+                [logits_shape, values_shape],
+                [query, w_key, w_value] + mine,
+                rows * count,
+                2,
+                rows,
+            )
+            units.append((exchange(logits), values))
+            continue
+        mine, marks = pieces[step, taken[0]], moved[step]
+        early = kernel(early_kernel, logits_shape, [query, w_key, mine[0]], share, 1, share)
+        late = functools.partial(late_kernel, chunk=taken[0], masked=masked)
+        logits = kernel(
+            late,
+            logits_shape,
+            [query, w_key, marks, early] + mine[1:],
+            rows - share,
+            1,
+            rows - share,
+        )
+        shared = exchange(logits)
+        values = kernel(values_kernel, values_shape, [w_value] + mine, rows, 1, 0)
+        units.append((shared, values))
 
     state = []
     state_shape = [

time: 84.7 us -> 80.8 us (0.954)
  waiting for transfers between devices: 54.8 us -> 48.4 us
  Pallas kernels: 11.9 us -> 16.1 us
  local copies, waits for them, and re-layouts: 1.95 us -> 0.03 us
    ppermute x20, waiting for transfers between devices: 54.8 us -> 48.4 us  [ring(): lax.ppermute(value, axis, [(i, (i + by) % length) for i in range(length)])]
    pallas_call x10 -> x18, Pallas kernels: 11.7 us -> 13.9 us  [call(): pl.pallas_call(kernel, out_shape=out_shape, in_specs=specs, out_specs=who...]
    pallas_call x2, Pallas kernels: 0.18 us -> 2.22 us  [shards(): pl.pallas_call(functools.partial(pack_kernel, chunk=k, share=share), out_...]
    unnamed x18 -> x14, local copies, waits for them, and re-layouts: 1.95 us -> 0.03 us
  transfers between devices with their start and end apart: 20 -> 20, of which waited for: 13 -> 12; matrix products, arithmetic and copies ran while one was open for 0% -> 0% of each run, Pallas kernels for 13% -> 17%
where the time goes in v4:
time: 80.8 us; the launch traced here: 80.6 us
  waiting for transfers between devices  48.4 us (60%)
  Pallas kernels  16.1 us (20%)
  starting transfers between devices  14.9 us (18%)
  other arithmetic  0.93 us (1%)
    ppermute x20, waiting for transfers between devices, ring(): lax.ppermute(value, axis, [(i, (i + by) % length) for i in range(length)])  48.4 us
    ppermute x20, starting transfers between devices, ring(): lax.ppermute(value, axis, [(i, (i + by) % length) for i in range(length)])  14.9 us
    pallas_call x18, Pallas kernels, call(): pl.pallas_call(kernel, out_shape=out_shape, in_specs=specs, out_specs=who...  13.9 us
    pallas_call x2, Pallas kernels, shards(): pl.pallas_call(functools.partial(pack_kernel, chunk=k, share=share), out_...  2.22 us
  transfers between devices with their start and end apart: 20, of which 12 were waited for; matrix products, arithmetic and copies ran while one was open for 0% of the time, Pallas kernels for 17%

profile of v4, /device:TPU:0, one launch (start us, length us, event | category | flops | bytes accessed | tf_op | source)
XLA Modules:
  0.0 80.6 jit_solution(16024107658736019605)
XLA Ops:
  0.0 0.0 copy-start.5
  0.0 1.2 %shard_map.74 = bf16[1160,128]{1,0:T(8,128)(2,1)S(1)} custom-call(bf16[6,128,768]{2,1,0:T(8,128)(2,1)} %tokens.3, s32[1,128]{1,0:T(1,128)} %bitcast.1), custom_call_target="tpu_custom_call" | custom-call | tf_op jit(solution)/shard_map/pallas_call | solution.py:309
  1.2 3.1 %collective-permute-start.1 = (bf16[1160,128]{1,0:T(8,128)(2,1)S(1)}, bf16[1160,128]{1,0:T(8,128)(2,1)S(1)}, u32[]{:S(2)}, u32[]{:S(2)}) collective-permute-start(bf16[1160,128]{1,0:T(8,128)(2,1)S(1)} %shard_map.74), channel_id=1, source_target_pairs={{0,4},{4,8},{8,12},{12,0},{1,5},{5,9},{9,13},{13,1},{2,6},{6,10},{... | collective-permute-start | bytes 890888 | tf_op jit(solution)/shard_map/ppermute | solution.py:23
  4.3 1.0 %shard_map.75 = bf16[1152,128]{1,0:T(8,128)(2,1)S(1)} custom-call(bf16[6,128,768]{2,1,0:T(8,128)(2,1)} %tokens.3, s32[1,128]{1,0:T(1,128)} %bitcast.2), custom_call_target="tpu_custom_call" | custom-call | tf_op jit(solution)/shard_map/pallas_call | solution.py:309
  5.4 1.6 %collective-permute-start.4 = (bf16[1152,128]{1,0:T(8,128)(2,1)S(1)}, bf16[1152,128]{1,0:T(8,128)(2,1)S(1)}, u32[]{:S(2)}, u32[]{:S(2)}) collective-permute-start(bf16[1152,128]{1,0:T(8,128)(2,1)S(1)} %shard_map.75), channel_id=1, source_target_pairs={{0,4},{4,8},{8,12},{12,0},{1,5},{5,9},{9,13},{13,1},{2,6},{6,10},{... | collective-permute-start | bytes 884744 | tf_op jit(solution)/shard_map/ppermute | solution.py:23
  7.0 7.3 %collective-permute-done.1.refs_3_ = bf16[1160,128]{1,0:T(8,128)(2,1)S(1)} collective-permute-done((bf16[1160,128]{1,0:T(8,128)(2,1)S(1)}, bf16[1160,128]{1,0:T(8,128)(2,1)S(1)}, u32[]{:S(2)}, u32[]{:S(2)}) %collective-permute-start.1) | collective-permute-done | bytes 296992 | tf_op jit(solution)/shard_map/ppermute | solution.py:23
  14.3 0.0 collective-permute-start.2
  14.3 6.3 %collective-permute-done.4.refs_5_ = bf16[1152,128]{1,0:T(8,128)(2,1)S(1)} collective-permute-done((bf16[1152,128]{1,0:T(8,128)(2,1)S(1)}, bf16[1152,128]{1,0:T(8,128)(2,1)S(1)}, u32[]{:S(2)}, u32[]{:S(2)}) %collective-permute-start.4) | collective-permute-done | bytes 294944 | tf_op jit(solution)/shard_map/ppermute | solution.py:23
  20.6 0.0 collective-permute-start.5
  20.6 0.0 collective-permute-start.14
  20.6 6.4 %collective-permute-done.2.marks.piece.refs_0_ = bf16[1160,128]{1,0:T(8,128)(2,1)S(1)} collective-permute-done((bf16[1160,128]{1,0:T(8,128)(2,1)S(1)}, bf16[1160,128]{1,0:T(8,128)(2,1)S(1)}, u32[]{:S(2)}, u32[]{:S(2)}) %collective-permute-start.2) | collective-permute-done | bytes 296992 | tf_op jit(solution)/shard_map/ppermute | solution.py:23
  27.0 0.0 collective-permute-start.3
  27.0 0.0 collective-permute-start.15
  27.0 6.3 %collective-permute-done.5.piece.refs_0_ = bf16[1152,128]{1,0:T(8,128)(2,1)S(1)} collective-permute-done((bf16[1152,128]{1,0:T(8,128)(2,1)S(1)}, bf16[1152,128]{1,0:T(8,128)(2,1)S(1)}, u32[]{:S(2)}, u32[]{:S(2)}) %collective-permute-start.5) | collective-permute-done | bytes 294944 | tf_op jit(solution)/shard_map/ppermute | solution.py:23
  33.3 0.0 collective-permute-start.6
  33.3 1.7 %collective-permute-start = (s32[6]{0:T(128)S(1)}, s32[6]{0:T(128)S(1)}, u32[]{:S(2)}, u32[]{:S(2)}) collective-permute-start(s32[6]{0:T(128)S(1)} %copy-done.6), channel_id=1, source_target_pairs={{0,2},{2,0},{1,3},{3,1},{4,6},{6,4},{5,7},{7,5},{8,10},{10,8},{9,1... | collective-permute-start | bytes 80 | tf_op jit(solution)/shard_map/ppermute | solution.py:23
  35.0 1.9 %collective-permute-done.refs_1_ = s32[6]{0:T(128)S(1)} collective-permute-done((s32[6]{0:T(128)S(1)}, s32[6]{0:T(128)S(1)}, u32[]{:S(2)}, u32[]{:S(2)}) %collective-permute-start) | collective-permute-done | bytes 56 | tf_op jit(solution)/shard_map/ppermute | solution.py:23
  36.9 0.0 collective-permute-start.17
  36.9 0.0 copy-done
  36.9 2.9 %shard_map.73 = (bf16[3,128,768]{2,1,0:T(8,128)(2,1)S(1)}, f32[2,3,128,128]{3,2,1,0:T(8,128)S(1)}, bf16[2,3,128,768]{3,2,1,0:T(8,128)(2,1)S(1)}) custom-call(s32[6]{0:T(128)S(1)} %copy-done.6, s32[6]{0:T(128)S(1)} %collective-permute-done.refs_1_, s32[1,128]{1,0:T(1,128)S(1)} %bitcast.3, bf16[6,128,768]{2,1,0:T(8,128)(2,1)S(1)} %copy-done.2, ...), custom_call_target="tpu_custom_call" | custom-call | flops 1509949440 | bytes 2949680 | tf_op jit(solution)/shard_map/pallas_call | solution.py:34
  39.8 0.0 collective-permute-done.15.refs_6_
  39.8 1.8 %collective-permute-start.13 = (f32[2,3,128,128]{3,2,1,0:T(8,128)S(1)}, f32[2,3,128,128]{3,2,1,0:T(8,128)S(1)}, u32[]{:S(2)}, u32[]{:S(2)}) collective-permute-start(f32[2,3,128,128]{3,2,1,0:T(8,128)S(1)} %get-tuple-element.19.refs_0_), channel_id=1, source_target_pairs={{0,2},{2,0},{1,3},{3,1},{4,6},{6,4},{5,7},{7,5},{8,10},{10,8},{9,1... | collective-permute-start | bytes 1179656 | tf_op jit(solution)/shard_map/ppermute | solution.py:23
  41.6 0.0 collective-permute-done.14.refs_4_
  41.6 0.2 collective-permute-start.9
  41.8 3.3 %collective-permute-done.6.piece.refs_0_ = bf16[1152,128]{1,0:T(8,128)(2,1)S(1)} collective-permute-done((bf16[1152,128]{1,0:T(8,128)(2,1)S(1)}, bf16[1152,128]{1,0:T(8,128)(2,1)S(1)}, u32[]{:S(2)}, u32[]{:S(2)}) %collective-permute-start.6) | collective-permute-done | bytes 294944 | tf_op jit(solution)/shard_map/ppermute | solution.py:23
  45.1 0.0 collective-permute-start.7
  45.1 0.0 collective-permute-done.3.marks.piece.refs_0_
  45.1 0.5 collective-permute-start.11
  45.6 1.9 %shard_map.85 = (f32[2,3,128,128]{3,2,1,0:T(8,128)S(1)}, bf16[2,3,128,768]{3,2,1,0:T(8,128)(2,1)S(1)}) custom-call(bf16[3,128,768]{2,1,0:T(8,128)(2,1)S(1)} %get-tuple-element.18.query.refs_0_, bf16[768,384]{1,0:T(8,128)(2,1)S(1)} %copy-done, bf16[768,384]{1,0:T(8,128)(2,1)S(1)} %copy-done.1, bf16[1160,128]{1,0:T(8,128)(2,1)S(1)} %collective-permute-done.1.refs_3_, ...), custom_call_target="tpu_custom_call" | custom-call | flops 1056964608 | bytes 2953216 | tf_op jit(solution)/shard_map/pallas_call | solution.py:34
  47.6 0.0 collective-permute-done.17.refs_0_.refs_1_
  47.6 1.6 %collective-permute-start.16 = (f32[2,3,128,128]{3,2,1,0:T(8,128)S(1)}, f32[2,3,128,128]{3,2,1,0:T(8,128)S(1)}, u32[]{:S(2)}, u32[]{:S(2)}) collective-permute-start(f32[2,3,128,128]{3,2,1,0:T(8,128)S(1)} %get-tuple-element.21.refs_3_), channel_id=1, source_target_pairs={{0,2},{2,0},{1,3},{3,1},{4,6},{6,4},{5,7},{7,5},{8,10},{10,8},{9,1... | collective-permute-start | bytes 1179656 | tf_op jit(solution)/shard_map/ppermute | solution.py:23
  49.1 0.6 shard_map.86.before
  49.7 0.6 shard_map.87.refs_6_
  50.3 0.0 collective-permute-done.9.refs_0_.refs_1_
  50.3 0.6 collective-permute-start.18
  50.9 0.6 shard_map.79.before
  51.5 0.6 shard_map.80.refs_0_
  52.0 0.6 shard_map.82.before
  52.6 0.0 collective-permute-done.11.refs_0_.refs_1_
  52.6 1.6 %collective-permute-start.10 = (f32[1,3,128,128]{3,2,1,0:T(8,128)S(1)}, f32[1,3,128,128]{3,2,1,0:T(8,128)S(1)}, u32[]{:S(2)}, u32[]{:S(2)}) collective-permute-start(f32[1,3,128,128]{3,2,1,0:T(8,128)S(1)} %shard_map.80.refs_0_), channel_id=1, source_target_pairs={{0,2},{2,0},{1,3},{3,1},{4,6},{6,4},{5,7},{7,5},{8,10},{10,8},{9,1... | collective-permute-start | bytes 589832 | tf_op jit(solution)/shard_map/ppermute | solution.py:23
  54.2 0.6 shard_map.83.refs_3_
  54.7 0.0 collective-permute-done.7.refs_0_.refs_1_
  54.7 0.6 collective-permute-start.12
  55.4 0.6 shard_map.76.before
  55.9 0.6 shard_map.77.refs_0_
  56.5 0.0 collective-permute-done.13.refs_1_
  56.5 1.5 %collective-permute-start.8 = (f32[1,3,128,128]{3,2,1,0:T(8,128)S(1)}, f32[1,3,128,128]{3,2,1,0:T(8,128)S(1)}, u32[]{:S(2)}, u32[]{:S(2)}) collective-permute-start(f32[1,3,128,128]{3,2,1,0:T(8,128)S(1)} %shard_map.77.refs_0_), channel_id=1, source_target_pairs={{0,2},{2,0},{1,3},{3,1},{4,6},{6,4},{5,7},{7,5},{8,10},{10,8},{9,1... | collective-permute-start | bytes 589832 | tf_op jit(solution)/shard_map/ppermute | solution.py:23
  58.0 0.5 shard_map.81.refs_2_
  58.5 0.5 shard_map.88.refs_8_
  59.0 1.3 %collective-permute-done.16.refs_4_ = f32[2,3,128,128]{3,2,1,0:T(8,128)S(1)} collective-permute-done((f32[2,3,128,128]{3,2,1,0:T(8,128)S(1)}, f32[2,3,128,128]{3,2,1,0:T(8,128)S(1)}, u32[]{:S(2)}, u32[]{:S(2)}) %collective-permute-start.16) | collective-permute-done | bytes 393248 | tf_op jit(solution)/shard_map/ppermute | solution.py:23
  60.3 4.2 %collective-permute-done.18.refs_7_ = f32[1,3,128,128]{3,2,1,0:T(8,128)S(1)} collective-permute-done((f32[1,3,128,128]{3,2,1,0:T(8,128)S(1)}, f32[1,3,128,128]{3,2,1,0:T(8,128)S(1)}, u32[]{:S(2)}, u32[]{:S(2)}) %collective-permute-start.18) | collective-permute-done | bytes 196640 | tf_op jit(solution)/shard_map/ppermute | solution.py:23
  64.5 0.8 shard_map.89
  65.3 0.5 shard_map.78.refs_2_
  65.8 0.5 shard_map.84.refs_5_
  66.3 2.5 %collective-permute-done.10.refs_1_ = f32[1,3,128,128]{3,2,1,0:T(8,128)S(1)} collective-permute-done((f32[1,3,128,128]{3,2,1,0:T(8,128)S(1)}, f32[1,3,128,128]{3,2,1,0:T(8,128)S(1)}, u32[]{:S(2)}, u32[]{:S(2)}) %collective-permute-start.10) | collective-permute-done | bytes 196640 | tf_op jit(solution)/shard_map/ppermute | solution.py:23
  68.8 4.2 %collective-permute-done.12.refs_4_ = f32[1,3,128,128]{3,2,1,0:T(8,128)S(1)} collective-permute-done((f32[1,3,128,128]{3,2,1,0:T(8,128)S(1)}, f32[1,3,128,128]{3,2,1,0:T(8,128)S(1)}, u32[]{:S(2)}, u32[]{:S(2)}) %collective-permute-start.12) | collective-permute-done | bytes 196640 | tf_op jit(solution)/shard_map/ppermute | solution.py:23
  73.0 0.4 shard_map.90
  73.4 3.3 %collective-permute-done.8.refs_1_ = f32[1,3,128,128]{3,2,1,0:T(8,128)S(1)} collective-permute-done((f32[1,3,128,128]{3,2,1,0:T(8,128)S(1)}, f32[1,3,128,128]{3,2,1,0:T(8,128)S(1)}, u32[]{:S(2)}, u32[]{:S(2)}) %collective-permute-start.8) | collective-permute-done | bytes 196640 | tf_op jit(solution)/shard_map/ppermute | solution.py:23
  76.7 0.0 copy-done.3
  76.7 0.9 %shard_map.91 = (bf16[6,128,384]{2,1,0:T(8,128)(2,1)S(1)}, bf16[6,128,384]{2,1,0:T(8,128)(2,1)S(1)}) custom-call(f32[1,3,128,128]{3,2,1,0:T(8,128)S(1)} %shard_map.77.refs_0_, f32[1,3,128,128]{3,2,1,0:T(8,128)S(1)} %collective-permute-done.8.refs_1_, bf16[1,3,128,768]{3,2,1,0:T(8,128)(2,1)S(1)} %shard_map.78.refs_2_, ...), custom_call_target="tpu_custom_call" | custom-call | flops 301989888 | bytes 3145728 | tf_op jit(solution)/shard_map/pallas_call | solution.py:34
  77.6 0.1 collective-permute-start.19
  77.7 0.6 shard_map.92
  78.3 1.4 %collective-permute-done.19 = bf16[6,128,384]{2,1,0:T(8,128)(2,1)S(1)} collective-permute-done((bf16[6,128,384]{2,1,0:T(8,128)(2,1)S(1)}, bf16[6,128,384]{2,1,0:T(8,128)(2,1)S(1)}, u32[]{:S(2)}, u32[]{:S(2)}) %collective-permute-start.19) | collective-permute-done | bytes 589856 | tf_op jit(solution)/shard_map/ppermute | solution.py:23
  79.7 0.9 %add_convert_fusion = bf16[6,128,384]{2,1,0:T(8,128)(2,1)} fusion(f32[6,128,384]{2,1,0:T(8,128)S(1)} %shard_map.92, bf16[6,128,384]{2,1,0:T(8,128)(2,1)S(1)} %collective-permute-done.19), kind=kLoop, calls=%fused_computation | loop fusion | flops 884736 | bytes 2359296 | tf_op jit(solution)/shard_map/convert_element_type | solution.py:444
  (11 shorter events, 0.0 us)
Async XLA Ops:
  0.0 33.3 %copy-start.6 = (s32[6]{0:T(128)S(1)}, s32[6]{0:T(128)}, u32[]{:S(2)}) copy-start(s32[6]{0:T(128)} %refs_0_.1) | copy-start | bytes 76
  0.0 36.9 %copy-start = (bf16[768,384]{1,0:T(8,128)(2,1)S(1)}, bf16[768,384]{1,0:T(8,128)(2,1)}, u32[]{:S(2)}) copy-start(bf16[768,384]{1,0:T(8,128)(2,1)} %w_key.15) | copy-start | bytes 1769476
  0.0 36.9 %copy-start.1 = (bf16[768,384]{1,0:T(8,128)(2,1)S(1)}, bf16[768,384]{1,0:T(8,128)(2,1)}, u32[]{:S(2)}) copy-start(bf16[768,384]{1,0:T(8,128)(2,1)} %w_value.7) | copy-start | bytes 1769476
  0.0 36.9 %copy-start.2 = (bf16[6,128,768]{2,1,0:T(8,128)(2,1)S(1)}, bf16[6,128,768]{2,1,0:T(8,128)(2,1)}, u32[]{:S(2)}) copy-start(bf16[6,128,768]{2,1,0:T(8,128)(2,1)} %tokens.3) | copy-start | bytes 3538948
  0.0 36.9 %copy-start.4 = (s32[128]{0:T(128)S(1)}, s32[128]{0:T(128)}, u32[]{:S(2)}) copy-start(s32[128]{0:T(128)} %param.9) | copy-start | bytes 1540
  0.0 36.9 %copy-start.5 = (bf16[768,384]{1,0:T(8,128)(2,1)S(1)}, bf16[768,384]{1,0:T(8,128)(2,1)}, u32[]{:S(2)}) copy-start(bf16[768,384]{1,0:T(8,128)(2,1)} %refs_4_.1) | copy-start | bytes 1769476
  1.2 13.0 %collective-permute-start.1 = (bf16[1160,128]{1,0:T(8,128)(2,1)S(1)}, bf16[1160,128]{1,0:T(8,128)(2,1)S(1)}, u32[]{:S(2)}, u32[]{:S(2)}) collective-permute-start(bf16[1160,128]{1,0:T(8,128)(2,1)S(1)} %shard_map.74), channel_id=1, source_target_pairs={{0,4},{4,8},{8,12},{12,0},{1,5},{5,9},{9,13},{13,1},{2,6},{6,10},{... | collective-permute-start | bytes 890888 | tf_op jit(solution)/shard_map/ppermute | solution.py:23
  5.4 15.2 %collective-permute-start.4 = (bf16[1152,128]{1,0:T(8,128)(2,1)S(1)}, bf16[1152,128]{1,0:T(8,128)(2,1)S(1)}, u32[]{:S(2)}, u32[]{:S(2)}) collective-permute-start(bf16[1152,128]{1,0:T(8,128)(2,1)S(1)} %shard_map.75), channel_id=1, source_target_pairs={{0,4},{4,8},{8,12},{12,0},{1,5},{5,9},{9,13},{13,1},{2,6},{6,10},{... | collective-permute-start | bytes 884744 | tf_op jit(solution)/shard_map/ppermute | solution.py:23
  14.3 12.7 %collective-permute-start.2 = (bf16[1160,128]{1,0:T(8,128)(2,1)S(1)}, bf16[1160,128]{1,0:T(8,128)(2,1)S(1)}, u32[]{:S(2)}, u32[]{:S(2)}) collective-permute-start(bf16[1160,128]{1,0:T(8,128)(2,1)S(1)} %collective-permute-done.1.refs_3_), channel_id=1, source_target_pairs={{0,4},{4,8},{8,12},{12,0},{1,5},{5,9},{9,13},{13,1},{2,6},{6,10},{... | collective-permute-start | bytes 890888 | tf_op jit(solution)/shard_map/ppermute | solution.py:23
  20.6 12.7 %collective-permute-start.5 = (bf16[1152,128]{1,0:T(8,128)(2,1)S(1)}, bf16[1152,128]{1,0:T(8,128)(2,1)S(1)}, u32[]{:S(2)}, u32[]{:S(2)}) collective-permute-start(bf16[1152,128]{1,0:T(8,128)(2,1)S(1)} %collective-permute-done.4.refs_5_), channel_id=1, source_target_pairs={{0,4},{4,8},{8,12},{12,0},{1,5},{5,9},{9,13},{13,1},{2,6},{6,10},{... | collective-permute-start | bytes 884744 | tf_op jit(solution)/shard_map/ppermute | solution.py:23
  20.6 21.0 %collective-permute-start.14 = (bf16[1160,128]{1,0:T(8,128)(2,1)S(1)}, bf16[1160,128]{1,0:T(8,128)(2,1)S(1)}, u32[]{:S(2)}, u32[]{:S(2)}) collective-permute-start(bf16[1160,128]{1,0:T(8,128)(2,1)S(1)} %collective-permute-done.1.refs_3_), channel_id=1, source_target_pairs={{0,1},{1,0},{2,3},{3,2},{4,5},{5,4},{6,7},{7,6},{8,9},{9,8},{10,11... | collective-permute-start | bytes 890888 | tf_op jit(solution)/shard_map/ppermute | solution.py:23
  27.0 18.2 %collective-permute-start.3 = (bf16[1160,128]{1,0:T(8,128)(2,1)S(1)}, bf16[1160,128]{1,0:T(8,128)(2,1)S(1)}, u32[]{:S(2)}, u32[]{:S(2)}) collective-permute-start(bf16[1160,128]{1,0:T(8,128)(2,1)S(1)} %collective-permute-done.2.marks.piece.refs_0_), channel_id=1, source_target_pairs={{0,4},{4,8},{8,12},{12,0},{1,5},{5,9},{9,13},{13,1},{2,6},{6,10},{... | collective-permute-start | bytes 890888 | tf_op jit(solution)/shard_map/ppermute | solution.py:23
  27.0 12.9 %collective-permute-start.15 = (bf16[1152,128]{1,0:T(8,128)(2,1)S(1)}, bf16[1152,128]{1,0:T(8,128)(2,1)S(1)}, u32[]{:S(2)}, u32[]{:S(2)}) collective-permute-start(bf16[1152,128]{1,0:T(8,128)(2,1)S(1)} %collective-permute-done.4.refs_5_), channel_id=1, source_target_pairs={{0,1},{1,0},{2,3},{3,2},{4,5},{5,4},{6,7},{7,6},{8,9},{9,8},{10,11... | collective-permute-start | bytes 884744 | tf_op jit(solution)/shard_map/ppermute | solution.py:23
  33.3 11.8 %collective-permute-start.6 = (bf16[1152,128]{1,0:T(8,128)(2,1)S(1)}, bf16[1152,128]{1,0:T(8,128)(2,1)S(1)}, u32[]{:S(2)}, u32[]{:S(2)}) collective-permute-start(bf16[1152,128]{1,0:T(8,128)(2,1)S(1)} %collective-permute-done.5.piece.refs_0_), channel_id=1, source_target_pairs={{0,4},{4,8},{8,12},{12,0},{1,5},{5,9},{9,13},{13,1},{2,6},{6,10},{... | collective-permute-start | bytes 884744 | tf_op jit(solution)/shard_map/ppermute | solution.py:23
  33.3 3.6 %collective-permute-start = (s32[6]{0:T(128)S(1)}, s32[6]{0:T(128)S(1)}, u32[]{:S(2)}, u32[]{:S(2)}) collective-permute-start(s32[6]{0:T(128)S(1)} %copy-done.6), channel_id=1, source_target_pairs={{0,2},{2,0},{1,3},{3,1},{4,6},{6,4},{5,7},{7,5},{8,10},{10,8},{9,1... | collective-permute-start | bytes 80 | tf_op jit(solution)/shard_map/ppermute | solution.py:23
  36.9 10.7 %collective-permute-start.17 = (bf16[1160,128]{1,0:T(8,128)(2,1)S(1)}, bf16[1160,128]{1,0:T(8,128)(2,1)S(1)}, u32[]{:S(2)}, u32[]{:S(2)}) collective-permute-start(bf16[1160,128]{1,0:T(8,128)(2,1)S(1)} %collective-permute-done.2.marks.piece.refs_0_), channel_id=1, source_target_pairs={{0,1},{1,0},{2,3},{3,2},{4,5},{5,4},{6,7},{7,6},{8,9},{9,8},{10,11... | collective-permute-start | bytes 890888 | tf_op jit(solution)/shard_map/ppermute | solution.py:23
  39.8 16.6 %collective-permute-start.13 = (f32[2,3,128,128]{3,2,1,0:T(8,128)S(1)}, f32[2,3,128,128]{3,2,1,0:T(8,128)S(1)}, u32[]{:S(2)}, u32[]{:S(2)}) collective-permute-start(f32[2,3,128,128]{3,2,1,0:T(8,128)S(1)} %get-tuple-element.19.refs_0_), channel_id=1, source_target_pairs={{0,2},{2,0},{1,3},{3,1},{4,6},{6,4},{5,7},{7,5},{8,10},{10,8},{9,1... | collective-permute-start | bytes 1179656 | tf_op jit(solution)/shard_map/ppermute | solution.py:23
  41.6 8.7 %collective-permute-start.9 = (bf16[1152,128]{1,0:T(8,128)(2,1)S(1)}, bf16[1152,128]{1,0:T(8,128)(2,1)S(1)}, u32[]{:S(2)}, u32[]{:S(2)}) collective-permute-start(bf16[1152,128]{1,0:T(8,128)(2,1)S(1)} %collective-permute-done.5.piece.refs_0_), channel_id=1, source_target_pairs={{0,1},{1,0},{2,3},{3,2},{4,5},{5,4},{6,7},{7,6},{8,9},{9,8},{10,11... | collective-permute-start | bytes 884744 | tf_op jit(solution)/shard_map/ppermute | solution.py:23
  45.1 9.6 %collective-permute-start.7 = (bf16[1152,128]{1,0:T(8,128)(2,1)S(1)}, bf16[1152,128]{1,0:T(8,128)(2,1)S(1)}, u32[]{:S(2)}, u32[]{:S(2)}) collective-permute-start(bf16[1152,128]{1,0:T(8,128)(2,1)S(1)} %collective-permute-done.6.piece.refs_0_), channel_id=1, source_target_pairs={{0,1},{1,0},{2,3},{3,2},{4,5},{5,4},{6,7},{7,6},{8,9},{9,8},{10,11... | collective-permute-start | bytes 884744 | tf_op jit(solution)/shard_map/ppermute | solution.py:23
  45.1 7.5 %collective-permute-start.11 = (bf16[1160,128]{1,0:T(8,128)(2,1)S(1)}, bf16[1160,128]{1,0:T(8,128)(2,1)S(1)}, u32[]{:S(2)}, u32[]{:S(2)}) collective-permute-start(bf16[1160,128]{1,0:T(8,128)(2,1)S(1)} %collective-permute-done.3.marks.piece.refs_0_), channel_id=1, source_target_pairs={{0,1},{1,0},{2,3},{3,2},{4,5},{5,4},{6,7},{7,6},{8,9},{9,8},{10,11... | collective-permute-start | bytes 890888 | tf_op jit(solution)/shard_map/ppermute | solution.py:23
  47.6 12.7 %collective-permute-start.16 = (f32[2,3,128,128]{3,2,1,0:T(8,128)S(1)}, f32[2,3,128,128]{3,2,1,0:T(8,128)S(1)}, u32[]{:S(2)}, u32[]{:S(2)}) collective-permute-start(f32[2,3,128,128]{3,2,1,0:T(8,128)S(1)} %get-tuple-element.21.refs_3_), channel_id=1, source_target_pairs={{0,2},{2,0},{1,3},{3,1},{4,6},{6,4},{5,7},{7,5},{8,10},{10,8},{9,1... | collective-permute-start | bytes 1179656 | tf_op jit(solution)/shard_map/ppermute | solution.py:23
  50.3 14.2 %collective-permute-start.18 = (f32[1,3,128,128]{3,2,1,0:T(8,128)S(1)}, f32[1,3,128,128]{3,2,1,0:T(8,128)S(1)}, u32[]{:S(2)}, u32[]{:S(2)}) collective-permute-start(f32[1,3,128,128]{3,2,1,0:T(8,128)S(1)} %shard_map.87.refs_6_), channel_id=1, source_target_pairs={{0,2},{2,0},{1,3},{3,1},{4,6},{6,4},{5,7},{7,5},{8,10},{10,8},{9,1... | collective-permute-start | bytes 589832 | tf_op jit(solution)/shard_map/ppermute | solution.py:23
  52.6 16.1 %collective-permute-start.10 = (f32[1,3,128,128]{3,2,1,0:T(8,128)S(1)}, f32[1,3,128,128]{3,2,1,0:T(8,128)S(1)}, u32[]{:S(2)}, u32[]{:S(2)}) collective-permute-start(f32[1,3,128,128]{3,2,1,0:T(8,128)S(1)} %shard_map.80.refs_0_), channel_id=1, source_target_pairs={{0,2},{2,0},{1,3},{3,1},{4,6},{6,4},{5,7},{7,5},{8,10},{10,8},{9,1... | collective-permute-start | bytes 589832 | tf_op jit(solution)/shard_map/ppermute | solution.py:23
  54.7 18.2 %collective-permute-start.12 = (f32[1,3,128,128]{3,2,1,0:T(8,128)S(1)}, f32[1,3,128,128]{3,2,1,0:T(8,128)S(1)}, u32[]{:S(2)}, u32[]{:S(2)}) collective-permute-start(f32[1,3,128,128]{3,2,1,0:T(8,128)S(1)} %shard_map.83.refs_3_), channel_id=1, source_target_pairs={{0,2},{2,0},{1,3},{3,1},{4,6},{6,4},{5,7},{7,5},{8,10},{10,8},{9,1... | collective-permute-start | bytes 589832 | tf_op jit(solution)/shard_map/ppermute | solution.py:23
  56.5 20.2 %collective-permute-start.8 = (f32[1,3,128,128]{3,2,1,0:T(8,128)S(1)}, f32[1,3,128,128]{3,2,1,0:T(8,128)S(1)}, u32[]{:S(2)}, u32[]{:S(2)}) collective-permute-start(f32[1,3,128,128]{3,2,1,0:T(8,128)S(1)} %shard_map.77.refs_0_), channel_id=1, source_target_pairs={{0,2},{2,0},{1,3},{3,1},{4,6},{6,4},{5,7},{7,5},{8,10},{10,8},{9,1... | collective-permute-start | bytes 589832 | tf_op jit(solution)/shard_map/ppermute | solution.py:23
  73.0 3.7 %copy-start.3 = (bf16[384,768]{1,0:T(8,128)(2,1)S(1)}, bf16[384,768]{1,0:T(8,128)(2,1)}, u32[]{:S(2)}) copy-start(bf16[384,768]{1,0:T(8,128)(2,1)} %w_out.1) | copy-start | bytes 1769476
  77.6 2.1 %collective-permute-start.19 = (bf16[6,128,384]{2,1,0:T(8,128)(2,1)S(1)}, bf16[6,128,384]{2,1,0:T(8,128)(2,1)S(1)}, u32[]{:S(2)}, u32[]{:S(2)}) collective-permute-start(bf16[6,128,384]{2,1,0:T(8,128)(2,1)S(1)} %get-tuple-element.30), channel_id=1, source_target_pairs={{0,1},{1,0},{2,3},{3,2},{4,5},{5,4},{6,7},{7,6},{8,9},{9,8},{10,11... | collective-permute-start | bytes 1769480 | tf_op jit(solution)/shard_map/ppermute | solution.py:23

commit v5 on v4

--- a/solution.py
+++ b/solution.py
@@ -14,6 +14,8 @@
 PER_TILE = LANES // HEAD_DIM
 CHUNKS = 2
 MARK_ROWS = 8
+PIECE = 32
+PARTS = HEAD_DIM // PIECE
 MASKED = -1000000000.0
 VMEM_LIMIT = 24 * 1024 * 1024
 
@@ -127,7 +129,7 @@
     tiles = width // LANES
     flats = []
     for piece in pieces:
-        size = piece.shape[0] // tiles // HEAD_DIM * HEAD_DIM
+        size = piece.shape[0] // tiles // PIECE * PIECE
         flats.append(
             jnp.concatenate([piece[tile * size : (tile + 1) * size] for tile in range(tiles)], axis=1)
         )
@@ -175,6 +177,60 @@
     pieces, values = refs[:-1], refs[-1]
     flat = unpack(pieces, w_value.shape[0])
     spread(values, 0, dot(flat, w_value[...]).astype(jnp.bfloat16), 0, HEAD_DIM)
+
+
+def split_kernel(packed, *parts, tiles):
+    size = packed.shape[0] // tiles // PIECE * PIECE
+    count = len(parts)
+    for at, part in enumerate(parts):
+        for block in range(tiles * size // PIECE // count):
+            source = (block * count + at) * PIECE
+            part[block * PIECE : (block + 1) * PIECE] = packed[source : source + PIECE]
+    if packed.shape[0] > tiles * size:
+        parts[0][tiles * size // count :] = packed[tiles * size :]
+
+
+def tall_early_kernel(query, w_key, piece, logits, keys):
+    spread(keys, 0, dot(unpack([piece], w_key.shape[0]), w_key[...]).astype(jnp.bfloat16), 0, PIECE)
+    for tile in range(query.shape[0]):
+        logits[tile] = dot_nt(keys[0, tile], query[tile, :, : keys.shape[3]])
+
+
+def tall_late_kernel(query, w_key, marks, before, *refs, first, masked):
+    pieces, (logits, keys) = refs[:-2], refs[-2:]
+    flat = unpack(pieces, w_key.shape[0])
+    spread(keys, 0, dot(flat, w_key[...]).astype(jnp.bfloat16), 0, PIECE)
+    grid = logits.shape[1:]
+    cell = lax.broadcasted_iota(jnp.int32, grid, 0) % PIECE + first
+    here = cell == lax.broadcasted_iota(jnp.int32, grid, 1)
+    mask = jnp.broadcast_to(marks_of(marks)[:1], grid)
+    live = jnp.max(jnp.where(here, mask, 0.0), axis=1, keepdims=True) > 0
+    skip = query.shape[2] - keys.shape[3]
+    for tile in range(query.shape[0]):
+        total = before[tile] + dot_nt(keys[0, tile], query[tile, :, skip:])
+        logits[tile] = jnp.where(live, total, masked)
+
+
+def tall_values_kernel(w_value, *refs):
+    pieces, values = refs[:-1], refs[-1]
+    per_piece = len(pieces) // PARTS
+    for at in range(PARTS):
+        flat = unpack(pieces[at * per_piece : (at + 1) * per_piece], w_value.shape[0])
+        flat = dot(flat, w_value[...]).astype(jnp.bfloat16)
+        rows = flat.shape[0] // PIECE
+        heads = lane_head((PIECE, LANES))
+        for tile in range(flat.shape[1] // LANES):
+            for row in range(rows):
+                part = flat[row * PIECE : (row + 1) * PIECE, tile * LANES : (tile + 1) * LANES]
+                for h in range(PER_TILE):
+                    kept = jnp.where(heads == h, part, jnp.zeros_like(part))
+                    top = h * HEAD_DIM + at * PIECE
+                    values[0, tile, top : top + PIECE, row * LANES : (row + 1) * LANES] = kept
+
+
+def upright(parts):
+    rows = [part[h * PIECE : (h + 1) * PIECE] for h in range(PER_TILE) for part in parts]
+    return jnp.concatenate(rows, axis=0).T
 
 
 def own_kernel(*refs, cores, masked):
@@ -207,12 +263,16 @@
 
 def absorb(units, state, tile, rows):
     scores, mixed = [], []
-    for tiles, values in units:
-        for chunk in range(tiles[0].shape[0]):
-            total = tiles[0][chunk, tile]
-            for other in tiles[1:]:
-                total = total + other[chunk, tile]
-            scores.append(total)
+    for pieces, values in units:
+        whole_chunks = len(pieces) == 1
+        for chunk in range(values.shape[0]):
+            totals = []
+            for tiles in pieces:
+                total = tiles[0][chunk, tile] if whole_chunks else tiles[0][tile]
+                for other in tiles[1:]:
+                    total = total + (other[chunk, tile] if whole_chunks else other[tile])
+                totals.append(total)
+            scores.append(totals[0] if whole_chunks else upright(totals))
             mixed.append(values[chunk, tile])
     top = functools.reduce(jnp.maximum, scores)
     top = per_head(top, max_over)
@@ -232,9 +292,11 @@
 
 def read_units(refs, sizes):
     units, at = [], 0
-    for size in sizes:
-        units.append((refs[at : at + size], refs[at + size]))
-        at += size + 1
+    for parts, size in sizes:
+        pieces = [refs[at + n * size : at + (n + 1) * size] for n in range(parts)]
+        at += parts * size
+        units.append((pieces, refs[at]))
+        at += 1
     return units, refs[at:]
 
 
@@ -280,7 +342,7 @@
 def batches(blocks):
     every = tuple(range(CHUNKS))
     out = []
-    for step in range(1, blocks):
+    for step in range(1, blocks - 1):
         if step < blocks - 2:
             out.append((step, every))
         else:
@@ -341,23 +403,41 @@
         holders,
         [pltpu.VMEM((CHUNKS, tiles, depth, spans), bf16)],
     )
-    units = [(exchange(logits), values)]
+    units = [([exchange(logits)], values)]
 
     pieces, moved = {}, {}
+
+    def shared_rows(value):
+        return [value] + [ring(value, "head", j) for j in range(1, cores)]
+
+    fine = []
     for step in range(1, blocks):
+        if step == blocks - 1:
+            for k in range(CHUNKS):
+                size = moving[k].shape[0] // (PARTS * PIECE) * PIECE
+                rest = moving[k].shape[0] - PARTS * size
+                cut = call(
+                    functools.partial(split_kernel, tiles=width // LANES),
+                    [shape((size + (0 if n else rest), LANES), bf16) for n in range(PARTS)],
+                    [moving[k]],
+                    0,
+                )
+                fine += cut
+            fine = [ring(fine[q], "res") for q in range(len(fine))]
+            break
         moving = [ring(moving[k], "res") for k in range(CHUNKS)]
         moved[step] = moving[0]
         for k in range(CHUNKS):
-            pieces[step, k] = [moving[k]] + [ring(moving[k], "head", j) for j in range(1, cores)]
-
-    def kernel(function, outs, args, rows, both, scratch_rows):
+            pieces[step, k] = shared_rows(moving[k])
+
+    def kernel(function, outs, args, rows, both, scratch_rows, high=part):
         return call(
             function,
             outs,
             args,
             2 * rows * part * inner * (both * width + cells * PER_TILE),
             0,
-            [shape((1, tiles, depth, scratch_rows * LANES), bf16)] if scratch_rows else (),
+            [shape((1, tiles, PER_TILE * high, scratch_rows * LANES), bf16)] if scratch_rows else (),
         )
 
     for step, taken in batches(blocks):
@@ -368,29 +448,39 @@
             mine = sum([pieces[step, k] for k in taken], [])
             project = functools.partial(project_kernel, order=taken, masked=masked)
             logits, values = kernel(
-                project,
-                [logits_shape, values_shape],
-                [query, w_key, w_value] + mine,
-                rows * count,
-                2,
-                rows,
+                project, [logits_shape, values_shape], [query, w_key, w_value] + mine, rows * count, 2, rows
             )
-            units.append((exchange(logits), values))
+            units.append(([exchange(logits)], values))
             continue
         mine, marks = pieces[step, taken[0]], moved[step]
         early = kernel(early_kernel, logits_shape, [query, w_key, mine[0]], share, 1, share)
         late = functools.partial(late_kernel, chunk=taken[0], masked=masked)
-        logits = kernel(
-            late,
-            logits_shape,
-            [query, w_key, marks, early] + mine[1:],
-            rows - share,
-            1,
-            rows - share,
-        )
+        logits = kernel(late, logits_shape, [query, w_key, marks, early] + mine[1:], rows - share, 1, rows - share)
         shared = exchange(logits)
         values = kernel(values_kernel, values_shape, [w_value] + mine, rows, 1, 0)
-        units.append((shared, values))
+        units.append(([shared], values))
+
+    tall = []
+    for q, piece in enumerate(fine):
+        logits_shape = shape((tiles, PER_TILE * PIECE, cells), f32)
+        mine = shared_rows(piece)
+        early = kernel(tall_early_kernel, logits_shape, [query, w_key, piece], share / 2, 1, share, PIECE)
+        late = functools.partial(tall_late_kernel, first=q * PIECE, masked=masked)
+        logits = kernel(
+            late, logits_shape, [query, w_key, fine[0], early] + mine[1:], (rows - share) / 2, 1, rows - share, PIECE
+        )
+        tall.append((exchange(logits), mine))
+    for k in range(len(tall) // PARTS):
+        group = tall[k * PARTS : (k + 1) * PARTS]
+        values = kernel(
+            tall_values_kernel,
+            shape((1, tiles, depth, spans), bf16),
+            [w_value] + sum([mine for _, mine in group], []),
+            rows,
+            1,
+            0,
+        )
+        units.append(([shared for shared, _ in group], values))
 
     state = []
     state_shape = [
@@ -400,16 +490,19 @@
     ]
 
     def flatten(group):
-        return sum([list(u[0]) + [u[1]] for u in group], [])
+        return sum([sum([list(piece) for piece in u[0]], []) + [u[1]] for u in group], [])
 
     def work(group):
-        return sum(2 * u[0][0].size * spans for u in group)
+        return sum(2 * cells * u[1].size for u in group)
+
+    def sizes_of(group):
+        return [(len(u[0]), len(u[0][0])) for u in group]
 
     cuts = groups_of(len(units))
     for cut in cuts[:-1]:
         group = units[slice(*cut)]
         state = call(
-            functools.partial(absorb_kernel, sizes=[len(u[0]) for u in group], carried=bool(state)),
+            functools.partial(absorb_kernel, sizes=sizes_of(group), carried=bool(state)),
             state_shape,
             flatten(group) + list(state),
             work(group),
@@ -418,7 +511,7 @@
     columns = width // cores
     attended, sent = call(
         functools.partial(
-            finish_kernel, sizes=[len(u[0]) for u in group], carried=bool(state), cores=cores
+            finish_kernel, sizes=sizes_of(group), carried=bool(state), cores=cores
         ),
         [shape((rows, cells, inner), bf16), shape((rows, cells, columns), bf16)],
         flatten(group) + list(state) + [w_out],

time: 80.8 us -> 82.6 us (1.022)
  waiting for transfers between devices: 48.4 us -> 41.6 us
  starting transfers between devices: 14.9 us -> 21.3 us
  Pallas kernels: 16.1 us -> 18.3 us
    ppermute x20 -> x26, waiting for transfers between devices: 48.4 us -> 41.6 us  [ring(): lax.ppermute(value, axis, [(i, (i + by) % length) for i in range(length)])]
    ppermute x20 -> x26, starting transfers between devices: 14.9 us -> 21.3 us  [ring(): lax.ppermute(value, axis, [(i, (i + by) % length) for i in range(length)])]
    pallas_call x18 -> x24, Pallas kernels: 13.9 us -> 16.1 us  [call(): pl.pallas_call(kernel, out_shape=out_shape, in_specs=specs, out_specs=who...]
  transfers between devices with their start and end apart: 20 -> 26, of which waited for: 12 -> 12; matrix products, arithmetic and copies ran while one was open for 0% -> 0% of each run, Pallas kernels for 17% -> 19%
where the time goes in v5:
time: 82.6 us; the launch traced here: 82.4 us
  waiting for transfers between devices  41.6 us (50%)
  starting transfers between devices  21.3 us (26%)
  Pallas kernels  18.3 us (22%)
  other arithmetic  0.93 us (1%)
    ppermute x26, waiting for transfers between devices, ring(): lax.ppermute(value, axis, [(i, (i + by) % length) for i in range(length)])  41.6 us
    ppermute x26, starting transfers between devices, ring(): lax.ppermute(value, axis, [(i, (i + by) % length) for i in range(length)])  21.3 us
    pallas_call x24, Pallas kernels, call(): pl.pallas_call(kernel, out_shape=out_shape, in_specs=specs, out_specs=who...  16.1 us
    pallas_call x2, Pallas kernels, shards(): pl.pallas_call(functools.partial(pack_kernel, chunk=k, share=share), out_...  2.16 us
  transfers between devices with their start and end apart: 26, of which 12 were waited for; matrix products, arithmetic and copies ran while one was open for 0% of the time, Pallas kernels for 19%

profile of v5, /device:TPU:0, one launch (start us, length us, event | category | flops | bytes accessed | tf_op | source)
XLA Modules:
  0.0 82.4 jit_solution(14825559727115872097)
XLA Ops:
  0.0 1.1 %shard_map.76 = bf16[1152,128]{1,0:T(8,128)(2,1)S(1)} custom-call(bf16[6,128,768]{2,1,0:T(8,128)(2,1)} %tokens.3, s32[1,128]{1,0:T(1,128)} %bitcast.1), custom_call_target="tpu_custom_call" | custom-call | tf_op jit(solution)/shard_map/pallas_call | solution.py:371
  1.1 0.0 copy-start.6
  1.1 0.0 copy-start
  1.2 0.0 copy-start.1
  1.2 0.0 copy-start.4
  1.2 0.0 copy-start.5
  1.2 3.1 %collective-permute-start.4 = (bf16[1152,128]{1,0:T(8,128)(2,1)S(1)}, bf16[1152,128]{1,0:T(8,128)(2,1)S(1)}, u32[]{:S(2)}, u32[]{:S(2)}) collective-permute-start(bf16[1152,128]{1,0:T(8,128)(2,1)S(1)} %shard_map.76), channel_id=1, source_target_pairs={{0,4},{4,8},{8,12},{12,0},{1,5},{5,9},{9,13},{13,1},{2,6},{6,10},{... | collective-permute-start | bytes 884744 | tf_op jit(solution)/shard_map/ppermute | solution.py:25
  4.3 1.0 %shard_map.74 = bf16[1160,128]{1,0:T(8,128)(2,1)S(1)} custom-call(bf16[6,128,768]{2,1,0:T(8,128)(2,1)} %tokens.3, s32[1,128]{1,0:T(1,128)} %bitcast.2), custom_call_target="tpu_custom_call" | custom-call | tf_op jit(solution)/shard_map/pallas_call | solution.py:371
  5.3 1.6 %collective-permute-start.1 = (bf16[1160,128]{1,0:T(8,128)(2,1)S(1)}, bf16[1160,128]{1,0:T(8,128)(2,1)S(1)}, u32[]{:S(2)}, u32[]{:S(2)}) collective-permute-start(bf16[1160,128]{1,0:T(8,128)(2,1)S(1)} %shard_map.74), channel_id=1, source_target_pairs={{0,4},{4,8},{8,12},{12,0},{1,5},{5,9},{9,13},{13,1},{2,6},{6,10},{... | collective-permute-start | bytes 890888 | tf_op jit(solution)/shard_map/ppermute | solution.py:25
  7.0 7.2 %collective-permute-done.4.refs_5_ = bf16[1152,128]{1,0:T(8,128)(2,1)S(1)} collective-permute-done((bf16[1152,128]{1,0:T(8,128)(2,1)S(1)}, bf16[1152,128]{1,0:T(8,128)(2,1)S(1)}, u32[]{:S(2)}, u32[]{:S(2)}) %collective-permute-start.4) | collective-permute-done | bytes 294944 | tf_op jit(solution)/shard_map/ppermute | solution.py:25
  14.2 0.0 collective-permute-start.5
  14.2 6.4 %collective-permute-done.1.refs_3_ = bf16[1160,128]{1,0:T(8,128)(2,1)S(1)} collective-permute-done((bf16[1160,128]{1,0:T(8,128)(2,1)S(1)}, bf16[1160,128]{1,0:T(8,128)(2,1)S(1)}, u32[]{:S(2)}, u32[]{:S(2)}) %collective-permute-start.1) | collective-permute-done | bytes 296992 | tf_op jit(solution)/shard_map/ppermute | solution.py:25
  20.6 0.0 collective-permute-start.20
  20.6 0.5 collective-permute-start.21
  21.1 5.8 %collective-permute-done.5.packed.piece.refs_0_ = bf16[1152,128]{1,0:T(8,128)(2,1)S(1)} collective-permute-done((bf16[1152,128]{1,0:T(8,128)(2,1)S(1)}, bf16[1152,128]{1,0:T(8,128)(2,1)S(1)}, u32[]{:S(2)}, u32[]{:S(2)}) %collective-permute-start.5) | collective-permute-done | bytes 294944 | tf_op jit(solution)/shard_map/ppermute | solution.py:25
  26.9 0.1 collective-permute-start.9
  27.0 1.6 %collective-permute-start.6 = (bf16[576,128]{1,0:T(8,128)(2,1)S(1)}, bf16[576,128]{1,0:T(8,128)(2,1)S(1)}, u32[]{:S(2)}, u32[]{:S(2)}) collective-permute-start(bf16[576,128]{1,0:T(8,128)(2,1)S(1)} %get-tuple-element.24), channel_id=1, source_target_pairs={{0,4},{4,8},{8,12},{12,0},{1,5},{5,9},{9,13},{13,1},{2,6},{6,10},{... | collective-permute-start | bytes 442376 | tf_op jit(solution)/shard_map/ppermute | solution.py:25
  28.5 4.7 %collective-permute-done.2.packed.marks.piece.refs_0_ = bf16[1160,128]{1,0:T(8,128)(2,1)S(1)} collective-permute-done((bf16[1160,128]{1,0:T(8,128)(2,1)S(1)}, bf16[1160,128]{1,0:T(8,128)(2,1)S(1)}, u32[]{:S(2)}, u32[]{:S(2)}) %collective-permute-start.2) | collective-permute-done | bytes 296992 | tf_op jit(solution)/shard_map/ppermute | solution.py:25
  33.2 1.7 %collective-permute-start = (s32[6]{0:T(128)S(1)}, s32[6]{0:T(128)S(1)}, u32[]{:S(2)}, u32[]{:S(2)}) collective-permute-start(s32[6]{0:T(128)S(1)} %copy-done.6), channel_id=1, source_target_pairs={{0,2},{2,0},{1,3},{3,1},{4,6},{6,4},{5,7},{7,5},{8,10},{10,8},{9,1... | collective-permute-start | bytes 80 | tf_op jit(solution)/shard_map/ppermute | solution.py:25
  35.0 1.8 %collective-permute-done.refs_1_ = s32[6]{0:T(128)S(1)} collective-permute-done((s32[6]{0:T(128)S(1)}, s32[6]{0:T(128)S(1)}, u32[]{:S(2)}, u32[]{:S(2)}) %collective-permute-start) | collective-permute-done | bytes 56 | tf_op jit(solution)/shard_map/ppermute | solution.py:25
  36.8 0.0 collective-permute-start.12
  36.8 1.6 %collective-permute-start.16 = (bf16[576,128]{1,0:T(8,128)(2,1)S(1)}, bf16[576,128]{1,0:T(8,128)(2,1)S(1)}, u32[]{:S(2)}, u32[]{:S(2)}) collective-permute-start(bf16[576,128]{1,0:T(8,128)(2,1)S(1)} %get-tuple-element.26), channel_id=1, source_target_pairs={{0,4},{4,8},{8,12},{12,0},{1,5},{5,9},{9,13},{13,1},{2,6},{6,10},{... | collective-permute-start | bytes 442376 | tf_op jit(solution)/shard_map/ppermute | solution.py:25
  38.4 2.9 %shard_map.73 = (bf16[3,128,768]{2,1,0:T(8,128)(2,1)S(1)}, f32[2,3,128,128]{3,2,1,0:T(8,128)S(1)}, bf16[2,3,128,768]{3,2,1,0:T(8,128)(2,1)S(1)}) custom-call(s32[6]{0:T(128)S(1)} %copy-done.6, s32[6]{0:T(128)S(1)} %collective-permute-done.refs_1_, s32[1,128]{1,0:T(1,128)S(1)} %bitcast.3, bf16[6,128,768]{2,1,0:T(8,128)(2,1)S(1)} %copy-done.2, ...), custom_call_target="tpu_custom_call" | custom-call | flops 1509949440 | bytes 2949680 | tf_op jit(solution)/shard_map/pallas_call | solution.py:36
  41.4 1.6 %collective-permute-start.19 = (f32[2,3,128,128]{3,2,1,0:T(8,128)S(1)}, f32[2,3,128,128]{3,2,1,0:T(8,128)S(1)}, u32[]{:S(2)}, u32[]{:S(2)}) collective-permute-start(f32[2,3,128,128]{3,2,1,0:T(8,128)S(1)} %get-tuple-element.27.refs_0_), channel_id=1, source_target_pairs={{0,2},{2,0},{1,3},{3,1},{4,6},{6,4},{5,7},{7,5},{8,10},{10,8},{9,1... | collective-permute-start | bytes 1179656 | tf_op jit(solution)/shard_map/ppermute | solution.py:25
  42.9 1.9 %shard_map.91 = (f32[2,3,128,128]{3,2,1,0:T(8,128)S(1)}, bf16[2,3,128,768]{3,2,1,0:T(8,128)(2,1)S(1)}) custom-call(bf16[3,128,768]{2,1,0:T(8,128)(2,1)S(1)} %get-tuple-element.22.query.refs_0_, bf16[768,384]{1,0:T(8,128)(2,1)S(1)} %copy-done, bf16[768,384]{1,0:T(8,128)(2,1)S(1)} %copy-done.1, bf16[1160,128]{1,0:T(8,128)(2,1)S(1)} %collective-permute-done.1.refs_3_, ...), custom_call_target="tpu_custom_call" | custom-call | flops 1056964608 | bytes 2953216 | tf_op jit(solution)/shard_map/pallas_call | solution.py:36
  44.9 3.2 %collective-permute-done.16.piece.refs_2_ = bf16[576,128]{1,0:T(8,128)(2,1)S(1)} collective-permute-done((bf16[576,128]{1,0:T(8,128)(2,1)S(1)}, bf16[576,128]{1,0:T(8,128)(2,1)S(1)}, u32[]{:S(2)}, u32[]{:S(2)}) %collective-permute-start.16) | collective-permute-done | bytes 147488 | tf_op jit(solution)/shard_map/ppermute | solution.py:25
  48.1 1.7 %collective-permute-start.22 = (f32[2,3,128,128]{3,2,1,0:T(8,128)S(1)}, f32[2,3,128,128]{3,2,1,0:T(8,128)S(1)}, u32[]{:S(2)}, u32[]{:S(2)}) collective-permute-start(f32[2,3,128,128]{3,2,1,0:T(8,128)S(1)} %get-tuple-element.29.refs_3_), channel_id=1, source_target_pairs={{0,2},{2,0},{1,3},{3,1},{4,6},{6,4},{5,7},{7,5},{8,10},{10,8},{9,1... | collective-permute-start | bytes 1179656 | tf_op jit(solution)/shard_map/ppermute | solution.py:25
  49.8 0.5 collective-permute-start.7
  50.3 0.1 collective-permute-start.17
  50.4 0.6 shard_map.92.before
  50.9 0.6 shard_map.93.refs_6_
  51.5 0.4 collective-permute-start.24
  51.9 0.2 collective-permute-start.14
  52.1 0.6 shard_map.83.before
  52.7 0.5 shard_map.80.before
  53.2 0.6 shard_map.84.refs_0_
  53.8 1.7 %collective-permute-start.13 = (f32[1,3,128,128]{3,2,1,0:T(8,128)S(1)}, f32[1,3,128,128]{3,2,1,0:T(8,128)S(1)}, u32[]{:S(2)}, u32[]{:S(2)}) collective-permute-start(f32[1,3,128,128]{3,2,1,0:T(8,128)S(1)} %shard_map.84.refs_0_), channel_id=1, source_target_pairs={{0,2},{2,0},{1,3},{3,1},{4,6},{6,4},{5,7},{7,5},{8,10},{10,8},{9,1... | collective-permute-start | bytes 589832 | tf_op jit(solution)/shard_map/ppermute | solution.py:25
  55.5 0.5 shard_map.78.before
  56.0 0.5 shard_map.88.before
  56.5 0.5 shard_map.86.before
  56.9 0.5 shard_map.81.refs_2_
  57.4 0.5 shard_map.85.refs_2_
  57.9 0.5 shard_map.82.refs_4_
  58.4 0.5 shard_map.89.refs_5_
  58.9 0.4 collective-permute-start.18
  59.3 0.5 shard_map.87.refs_3_
  59.8 1.7 %collective-permute-start.15 = (f32[3,64,128]{2,1,0:T(8,128)S(1)}, f32[3,64,128]{2,1,0:T(8,128)S(1)}, u32[]{:S(2)}, u32[]{:S(2)}) collective-permute-start(f32[3,64,128]{2,1,0:T(8,128)S(1)} %shard_map.87.refs_3_), channel_id=1, source_target_pairs={{0,2},{2,0},{1,3},{3,1},{4,6},{6,4},{5,7},{7,5},{8,10},{10,8},{9,1... | collective-permute-start | bytes 294920 | tf_op jit(solution)/shard_map/ppermute | solution.py:25
  61.5 0.5 shard_map.79.refs_0_
  62.0 1.3 %collective-permute-start.11 = (f32[3,64,128]{2,1,0:T(8,128)S(1)}, f32[3,64,128]{2,1,0:T(8,128)S(1)}, u32[]{:S(2)}, u32[]{:S(2)}) collective-permute-start(f32[3,64,128]{2,1,0:T(8,128)S(1)} %shard_map.81.refs_2_), channel_id=1, source_target_pairs={{0,2},{2,0},{1,3},{3,1},{4,6},{6,4},{5,7},{7,5},{8,10},{10,8},{9,1... | collective-permute-start | bytes 294920 | tf_op jit(solution)/shard_map/ppermute | solution.py:25
  63.4 2.7 %collective-permute-done.24.refs_7_ = f32[1,3,128,128]{3,2,1,0:T(8,128)S(1)} collective-permute-done((f32[1,3,128,128]{3,2,1,0:T(8,128)S(1)}, f32[1,3,128,128]{3,2,1,0:T(8,128)S(1)}, u32[]{:S(2)}, u32[]{:S(2)}) %collective-permute-start.24) | collective-permute-done | bytes 196640 | tf_op jit(solution)/shard_map/ppermute | solution.py:25
  66.1 1.5 %collective-permute-start.8 = (f32[3,64,128]{2,1,0:T(8,128)S(1)}, f32[3,64,128]{2,1,0:T(8,128)S(1)}, u32[]{:S(2)}, u32[]{:S(2)}) collective-permute-start(f32[3,64,128]{2,1,0:T(8,128)S(1)} %shard_map.79.refs_0_), channel_id=1, source_target_pairs={{0,2},{2,0},{1,3},{3,1},{4,6},{6,4},{5,7},{7,5},{8,10},{10,8},{9,1... | collective-permute-start | bytes 294920 | tf_op jit(solution)/shard_map/ppermute | solution.py:25
  67.6 0.5 shard_map.94.refs_8_
  68.1 0.5 shard_map.90.refs_7_
  68.5 0.8 shard_map.95
  69.3 3.1 %collective-permute-done.18.refs_6_ = f32[3,64,128]{2,1,0:T(8,128)S(1)} collective-permute-done((f32[3,64,128]{2,1,0:T(8,128)S(1)}, f32[3,64,128]{2,1,0:T(8,128)S(1)}, u32[]{:S(2)}, u32[]{:S(2)}) %collective-permute-start.18) | collective-permute-done | bytes 98336 | tf_op jit(solution)/shard_map/ppermute | solution.py:25
  72.4 2.1 %collective-permute-done.15.refs_4_ = f32[3,64,128]{2,1,0:T(8,128)S(1)} collective-permute-done((f32[3,64,128]{2,1,0:T(8,128)S(1)}, f32[3,64,128]{2,1,0:T(8,128)S(1)}, u32[]{:S(2)}, u32[]{:S(2)}) %collective-permute-start.15) | collective-permute-done | bytes 98336 | tf_op jit(solution)/shard_map/ppermute | solution.py:25
  74.5 0.6 shard_map.96
  75.2 1.5 %collective-permute-done.11.refs_3_ = f32[3,64,128]{2,1,0:T(8,128)S(1)} collective-permute-done((f32[3,64,128]{2,1,0:T(8,128)S(1)}, f32[3,64,128]{2,1,0:T(8,128)S(1)}, u32[]{:S(2)}, u32[]{:S(2)}) %collective-permute-start.11) | collective-permute-done | bytes 98336 | tf_op jit(solution)/shard_map/ppermute | solution.py:25
  76.6 1.6 %collective-permute-done.8.refs_1_ = f32[3,64,128]{2,1,0:T(8,128)S(1)} collective-permute-done((f32[3,64,128]{2,1,0:T(8,128)S(1)}, f32[3,64,128]{2,1,0:T(8,128)S(1)}, u32[]{:S(2)}, u32[]{:S(2)}) %collective-permute-start.8) | collective-permute-done | bytes 98336 | tf_op jit(solution)/shard_map/ppermute | solution.py:25
  78.2 1.2 %shard_map.97 = (bf16[6,128,384]{2,1,0:T(8,128)(2,1)S(1)}, bf16[6,128,384]{2,1,0:T(8,128)(2,1)S(1)}) custom-call(f32[3,64,128]{2,1,0:T(8,128)S(1)} %shard_map.79.refs_0_, f32[3,64,128]{2,1,0:T(8,128)S(1)} %collective-permute-done.8.refs_1_, f32[3,64,128]{2,1,0:T(8,128)S(1)} %shard_map.81.refs_2_, f32[3,64,128]{2,1,0:T(8,128)S(1)} %collective-permute-done.11.refs_3_, ...), custom_call_target="tpu_custom_call" | custom-call | flops 301989888 | bytes 3145728 | tf_op jit(solution)/shard_map/pallas_call | solution.py:36
  79.4 0.1 collective-permute-start.25
  79.5 0.6 shard_map.98
  80.1 1.4 %collective-permute-done.25 = bf16[6,128,384]{2,1,0:T(8,128)(2,1)S(1)} collective-permute-done((bf16[6,128,384]{2,1,0:T(8,128)(2,1)S(1)}, bf16[6,128,384]{2,1,0:T(8,128)(2,1)S(1)}, u32[]{:S(2)}, u32[]{:S(2)}) %collective-permute-start.25) | collective-permute-done | bytes 589856 | tf_op jit(solution)/shard_map/ppermute | solution.py:25
  81.5 0.9 %add_convert_fusion = bf16[6,128,384]{2,1,0:T(8,128)(2,1)} fusion(f32[6,128,384]{2,1,0:T(8,128)S(1)} %shard_map.98, bf16[6,128,384]{2,1,0:T(8,128)(2,1)S(1)} %collective-permute-done.25), kind=kLoop, calls=%fused_computation | loop fusion | flops 884736 | bytes 2359296 | tf_op jit(solution)/shard_map/convert_element_type | solution.py:537
  (29 shorter events, 0.1 us)
Async XLA Ops:
  0.0 38.4 %copy-start.2 = (bf16[6,128,768]{2,1,0:T(8,128)(2,1)S(1)}, bf16[6,128,768]{2,1,0:T(8,128)(2,1)}, u32[]{:S(2)}) copy-start(bf16[6,128,768]{2,1,0:T(8,128)(2,1)} %tokens.3) | copy-start | bytes 3538948
  1.1 32.1 %copy-start.6 = (s32[6]{0:T(128)S(1)}, s32[6]{0:T(128)}, u32[]{:S(2)}) copy-start(s32[6]{0:T(128)} %refs_0_.1) | copy-start | bytes 76
  1.1 37.3 %copy-start = (bf16[768,384]{1,0:T(8,128)(2,1)S(1)}, bf16[768,384]{1,0:T(8,128)(2,1)}, u32[]{:S(2)}) copy-start(bf16[768,384]{1,0:T(8,128)(2,1)} %w_key.23) | copy-start | bytes 1769476
  1.2 37.3 %copy-start.1 = (bf16[768,384]{1,0:T(8,128)(2,1)S(1)}, bf16[768,384]{1,0:T(8,128)(2,1)}, u32[]{:S(2)}) copy-start(bf16[768,384]{1,0:T(8,128)(2,1)} %w_value.7) | copy-start | bytes 1769476
  1.2 37.3 %copy-start.4 = (s32[128]{0:T(128)S(1)}, s32[128]{0:T(128)}, u32[]{:S(2)}) copy-start(s32[128]{0:T(128)} %param.9) | copy-start | bytes 1540
  1.2 37.2 %copy-start.5 = (bf16[768,384]{1,0:T(8,128)(2,1)S(1)}, bf16[768,384]{1,0:T(8,128)(2,1)}, u32[]{:S(2)}) copy-start(bf16[768,384]{1,0:T(8,128)(2,1)} %refs_4_.1) | copy-start | bytes 1769476
  1.2 13.0 %collective-permute-start.4 = (bf16[1152,128]{1,0:T(8,128)(2,1)S(1)}, bf16[1152,128]{1,0:T(8,128)(2,1)S(1)}, u32[]{:S(2)}, u32[]{:S(2)}) collective-permute-start(bf16[1152,128]{1,0:T(8,128)(2,1)S(1)} %shard_map.76), channel_id=1, source_target_pairs={{0,4},{4,8},{8,12},{12,0},{1,5},{5,9},{9,13},{13,1},{2,6},{6,10},{... | collective-permute-start | bytes 884744 | tf_op jit(solution)/shard_map/ppermute | solution.py:25
  5.3 15.2 %collective-permute-start.1 = (bf16[1160,128]{1,0:T(8,128)(2,1)S(1)}, bf16[1160,128]{1,0:T(8,128)(2,1)S(1)}, u32[]{:S(2)}, u32[]{:S(2)}) collective-permute-start(bf16[1160,128]{1,0:T(8,128)(2,1)S(1)} %shard_map.74), channel_id=1, source_target_pairs={{0,4},{4,8},{8,12},{12,0},{1,5},{5,9},{9,13},{13,1},{2,6},{6,10},{... | collective-permute-start | bytes 890888 | tf_op jit(solution)/shard_map/ppermute | solution.py:25
  14.2 12.7 %collective-permute-start.5 = (bf16[1152,128]{1,0:T(8,128)(2,1)S(1)}, bf16[1152,128]{1,0:T(8,128)(2,1)S(1)}, u32[]{:S(2)}, u32[]{:S(2)}) collective-permute-start(bf16[1152,128]{1,0:T(8,128)(2,1)S(1)} %collective-permute-done.4.refs_5_), channel_id=1, source_target_pairs={{0,4},{4,8},{8,12},{12,0},{1,5},{5,9},{9,13},{13,1},{2,6},{6,10},{... | collective-permute-start | bytes 884744 | tf_op jit(solution)/shard_map/ppermute | solution.py:25
  20.5 12.7 %collective-permute-start.2 = (bf16[1160,128]{1,0:T(8,128)(2,1)S(1)}, bf16[1160,128]{1,0:T(8,128)(2,1)S(1)}, u32[]{:S(2)}, u32[]{:S(2)}) collective-permute-start(bf16[1160,128]{1,0:T(8,128)(2,1)S(1)} %collective-permute-done.1.refs_3_), channel_id=1, source_target_pairs={{0,4},{4,8},{8,12},{12,0},{1,5},{5,9},{9,13},{13,1},{2,6},{6,10},{... | collective-permute-start | bytes 890888 | tf_op jit(solution)/shard_map/ppermute | solution.py:25
  20.6 16.3 %collective-permute-start.20 = (bf16[1160,128]{1,0:T(8,128)(2,1)S(1)}, bf16[1160,128]{1,0:T(8,128)(2,1)S(1)}, u32[]{:S(2)}, u32[]{:S(2)}) collective-permute-start(bf16[1160,128]{1,0:T(8,128)(2,1)S(1)} %collective-permute-done.1.refs_3_), channel_id=1, source_target_pairs={{0,1},{1,0},{2,3},{3,2},{4,5},{5,4},{6,7},{7,6},{8,9},{9,8},{10,11... | collective-permute-start | bytes 890888 | tf_op jit(solution)/shard_map/ppermute | solution.py:25
  20.6 16.3 %collective-permute-start.21 = (bf16[1152,128]{1,0:T(8,128)(2,1)S(1)}, bf16[1152,128]{1,0:T(8,128)(2,1)S(1)}, u32[]{:S(2)}, u32[]{:S(2)}) collective-permute-start(bf16[1152,128]{1,0:T(8,128)(2,1)S(1)} %collective-permute-done.4.refs_5_), channel_id=1, source_target_pairs={{0,1},{1,0},{2,3},{3,2},{4,5},{5,4},{6,7},{7,6},{8,9},{9,8},{10,11... | collective-permute-start | bytes 884744 | tf_op jit(solution)/shard_map/ppermute | solution.py:25
  26.9 11.5 %collective-permute-start.9 = (bf16[576,128]{1,0:T(8,128)(2,1)S(1)}, bf16[576,128]{1,0:T(8,128)(2,1)S(1)}, u32[]{:S(2)}, u32[]{:S(2)}) collective-permute-start(bf16[576,128]{1,0:T(8,128)(2,1)S(1)} %get-tuple-element.25), channel_id=1, source_target_pairs={{0,4},{4,8},{8,12},{12,0},{1,5},{5,9},{9,13},{13,1},{2,6},{6,10},{... | collective-permute-start | bytes 442376 | tf_op jit(solution)/shard_map/ppermute | solution.py:25
  27.0 14.4 %collective-permute-start.6 = (bf16[576,128]{1,0:T(8,128)(2,1)S(1)}, bf16[576,128]{1,0:T(8,128)(2,1)S(1)}, u32[]{:S(2)}, u32[]{:S(2)}) collective-permute-start(bf16[576,128]{1,0:T(8,128)(2,1)S(1)} %get-tuple-element.24), channel_id=1, source_target_pairs={{0,4},{4,8},{8,12},{12,0},{1,5},{5,9},{9,13},{13,1},{2,6},{6,10},{... | collective-permute-start | bytes 442376 | tf_op jit(solution)/shard_map/ppermute | solution.py:25
  33.2 3.6 %collective-permute-start = (s32[6]{0:T(128)S(1)}, s32[6]{0:T(128)S(1)}, u32[]{:S(2)}, u32[]{:S(2)}) collective-permute-start(s32[6]{0:T(128)S(1)} %copy-done.6), channel_id=1, source_target_pairs={{0,2},{2,0},{1,3},{3,1},{4,6},{6,4},{5,7},{7,5},{8,10},{10,8},{9,1... | collective-permute-start | bytes 80 | tf_op jit(solution)/shard_map/ppermute | solution.py:25
  36.8 13.0 %collective-permute-start.12 = (bf16[1152,128]{1,0:T(8,128)(2,1)S(1)}, bf16[1152,128]{1,0:T(8,128)(2,1)S(1)}, u32[]{:S(2)}, u32[]{:S(2)}) collective-permute-start(bf16[1152,128]{1,0:T(8,128)(2,1)S(1)} %collective-permute-done.5.packed.piece.refs_0_), channel_id=1, source_target_pairs={{0,1},{1,0},{2,3},{3,2},{4,5},{5,4},{6,7},{7,6},{8,9},{9,8},{10,11... | collective-permute-start | bytes 884744 | tf_op jit(solution)/shard_map/ppermute | solution.py:25
  36.8 13.0 %collective-permute-start.3 = (bf16[584,128]{1,0:T(8,128)(2,1)S(1)}, bf16[584,128]{1,0:T(8,128)(2,1)S(1)}, u32[]{:S(2)}, u32[]{:S(2)}) collective-permute-start(bf16[584,128]{1,0:T(8,128)(2,1)S(1)} %get-tuple-element.23), channel_id=1, source_target_pairs={{0,4},{4,8},{8,12},{12,0},{1,5},{5,9},{9,13},{13,1},{2,6},{6,10},{... | collective-permute-start | bytes 448520 | tf_op jit(solution)/shard_map/ppermute | solution.py:25
  36.8 11.2 %collective-permute-start.16 = (bf16[576,128]{1,0:T(8,128)(2,1)S(1)}, bf16[576,128]{1,0:T(8,128)(2,1)S(1)}, u32[]{:S(2)}, u32[]{:S(2)}) collective-permute-start(bf16[576,128]{1,0:T(8,128)(2,1)S(1)} %get-tuple-element.26), channel_id=1, source_target_pairs={{0,4},{4,8},{8,12},{12,0},{1,5},{5,9},{9,13},{13,1},{2,6},{6,10},{... | collective-permute-start | bytes 442376 | tf_op jit(solution)/shard_map/ppermute | solution.py:25
  38.4 11.9 %collective-permute-start.23 = (bf16[1160,128]{1,0:T(8,128)(2,1)S(1)}, bf16[1160,128]{1,0:T(8,128)(2,1)S(1)}, u32[]{:S(2)}, u32[]{:S(2)}) collective-permute-start(bf16[1160,128]{1,0:T(8,128)(2,1)S(1)} %collective-permute-done.2.packed.marks.piece.refs_0_), channel_id=1, source_target_pairs={{0,1},{1,0},{2,3},{3,2},{4,5},{5,4},{6,7},{7,6},{8,9},{9,8},{10,11... | collective-permute-start | bytes 890888 | tf_op jit(solution)/shard_map/ppermute | solution.py:25
  41.4 18.4 %collective-permute-start.19 = (f32[2,3,128,128]{3,2,1,0:T(8,128)S(1)}, f32[2,3,128,128]{3,2,1,0:T(8,128)S(1)}, u32[]{:S(2)}, u32[]{:S(2)}) collective-permute-start(f32[2,3,128,128]{3,2,1,0:T(8,128)S(1)} %get-tuple-element.27.refs_0_), channel_id=1, source_target_pairs={{0,2},{2,0},{1,3},{3,1},{4,6},{6,4},{5,7},{7,5},{8,10},{10,8},{9,1... | collective-permute-start | bytes 1179656 | tf_op jit(solution)/shard_map/ppermute | solution.py:25
  48.1 14.0 %collective-permute-start.22 = (f32[2,3,128,128]{3,2,1,0:T(8,128)S(1)}, f32[2,3,128,128]{3,2,1,0:T(8,128)S(1)}, u32[]{:S(2)}, u32[]{:S(2)}) collective-permute-start(f32[2,3,128,128]{3,2,1,0:T(8,128)S(1)} %get-tuple-element.29.refs_3_), channel_id=1, source_target_pairs={{0,2},{2,0},{1,3},{3,1},{4,6},{6,4},{5,7},{7,5},{8,10},{10,8},{9,1... | collective-permute-start | bytes 1179656 | tf_op jit(solution)/shard_map/ppermute | solution.py:25
  49.8 1.7 %collective-permute-start.10 = (bf16[576,128]{1,0:T(8,128)(2,1)S(1)}, bf16[576,128]{1,0:T(8,128)(2,1)S(1)}, u32[]{:S(2)}, u32[]{:S(2)}) collective-permute-start(bf16[576,128]{1,0:T(8,128)(2,1)S(1)} %collective-permute-done.9.piece.refs_2_), channel_id=1, source_target_pairs={{0,1},{1,0},{2,3},{3,2},{4,5},{5,4},{6,7},{7,6},{8,9},{9,8},{10,11... | collective-permute-start | bytes 442376 | tf_op jit(solution)/shard_map/ppermute | solution.py:25
  49.8 2.1 %collective-permute-start.7 = (bf16[576,128]{1,0:T(8,128)(2,1)S(1)}, bf16[576,128]{1,0:T(8,128)(2,1)S(1)}, u32[]{:S(2)}, u32[]{:S(2)}) collective-permute-start(bf16[576,128]{1,0:T(8,128)(2,1)S(1)} %collective-permute-done.6.piece.refs_0_), channel_id=1, source_target_pairs={{0,1},{1,0},{2,3},{3,2},{4,5},{5,4},{6,7},{7,6},{8,9},{9,8},{10,11... | collective-permute-start | bytes 442376 | tf_op jit(solution)/shard_map/ppermute | solution.py:25
  50.3 3.4 %collective-permute-start.17 = (bf16[576,128]{1,0:T(8,128)(2,1)S(1)}, bf16[576,128]{1,0:T(8,128)(2,1)S(1)}, u32[]{:S(2)}, u32[]{:S(2)}) collective-permute-start(bf16[576,128]{1,0:T(8,128)(2,1)S(1)} %collective-permute-done.16.piece.refs_2_), channel_id=1, source_target_pairs={{0,1},{1,0},{2,3},{3,2},{4,5},{5,4},{6,7},{7,6},{8,9},{9,8},{10,11... | collective-permute-start | bytes 442376 | tf_op jit(solution)/shard_map/ppermute | solution.py:25
  51.5 14.6 %collective-permute-start.24 = (f32[1,3,128,128]{3,2,1,0:T(8,128)S(1)}, f32[1,3,128,128]{3,2,1,0:T(8,128)S(1)}, u32[]{:S(2)}, u32[]{:S(2)}) collective-permute-start(f32[1,3,128,128]{3,2,1,0:T(8,128)S(1)} %shard_map.93.refs_6_), channel_id=1, source_target_pairs={{0,2},{2,0},{1,3},{3,1},{4,6},{6,4},{5,7},{7,5},{8,10},{10,8},{9,1... | collective-permute-start | bytes 589832 | tf_op jit(solution)/shard_map/ppermute | solution.py:25
  51.9 7.0 %collective-permute-start.14 = (bf16[584,128]{1,0:T(8,128)(2,1)S(1)}, bf16[584,128]{1,0:T(8,128)(2,1)S(1)}, u32[]{:S(2)}, u32[]{:S(2)}) collective-permute-start(bf16[584,128]{1,0:T(8,128)(2,1)S(1)} %collective-permute-done.3.marks.piece.refs_0_), channel_id=1, source_target_pairs={{0,1},{1,0},{2,3},{3,2},{4,5},{5,4},{6,7},{7,6},{8,9},{9,8},{10,11... | collective-permute-start | bytes 448520 | tf_op jit(solution)/shard_map/ppermute | solution.py:25
  53.8 20.7 %collective-permute-start.13 = (f32[1,3,128,128]{3,2,1,0:T(8,128)S(1)}, f32[1,3,128,128]{3,2,1,0:T(8,128)S(1)}, u32[]{:S(2)}, u32[]{:S(2)}) collective-permute-start(f32[1,3,128,128]{3,2,1,0:T(8,128)S(1)} %shard_map.84.refs_0_), channel_id=1, source_target_pairs={{0,2},{2,0},{1,3},{3,1},{4,6},{6,4},{5,7},{7,5},{8,10},{10,8},{9,1... | collective-permute-start | bytes 589832 | tf_op jit(solution)/shard_map/ppermute | solution.py:25
  58.9 13.5 %collective-permute-start.18 = (f32[3,64,128]{2,1,0:T(8,128)S(1)}, f32[3,64,128]{2,1,0:T(8,128)S(1)}, u32[]{:S(2)}, u32[]{:S(2)}) collective-permute-start(f32[3,64,128]{2,1,0:T(8,128)S(1)} %shard_map.89.refs_5_), channel_id=1, source_target_pairs={{0,2},{2,0},{1,3},{3,1},{4,6},{6,4},{5,7},{7,5},{8,10},{10,8},{9,1... | collective-permute-start | bytes 294920 | tf_op jit(solution)/shard_map/ppermute | solution.py:25
  59.8 14.7 %collective-permute-start.15 = (f32[3,64,128]{2,1,0:T(8,128)S(1)}, f32[3,64,128]{2,1,0:T(8,128)S(1)}, u32[]{:S(2)}, u32[]{:S(2)}) collective-permute-start(f32[3,64,128]{2,1,0:T(8,128)S(1)} %shard_map.87.refs_3_), channel_id=1, source_target_pairs={{0,2},{2,0},{1,3},{3,1},{4,6},{6,4},{5,7},{7,5},{8,10},{10,8},{9,1... | collective-permute-start | bytes 294920 | tf_op jit(solution)/shard_map/ppermute | solution.py:25
  62.0 14.6 %collective-permute-start.11 = (f32[3,64,128]{2,1,0:T(8,128)S(1)}, f32[3,64,128]{2,1,0:T(8,128)S(1)}, u32[]{:S(2)}, u32[]{:S(2)}) collective-permute-start(f32[3,64,128]{2,1,0:T(8,128)S(1)} %shard_map.81.refs_2_), channel_id=1, source_target_pairs={{0,2},{2,0},{1,3},{3,1},{4,6},{6,4},{5,7},{7,5},{8,10},{10,8},{9,1... | collective-permute-start | bytes 294920 | tf_op jit(solution)/shard_map/ppermute | solution.py:25
  66.1 12.2 %collective-permute-start.8 = (f32[3,64,128]{2,1,0:T(8,128)S(1)}, f32[3,64,128]{2,1,0:T(8,128)S(1)}, u32[]{:S(2)}, u32[]{:S(2)}) collective-permute-start(f32[3,64,128]{2,1,0:T(8,128)S(1)} %shard_map.79.refs_0_), channel_id=1, source_target_pairs={{0,2},{2,0},{1,3},{3,1},{4,6},{6,4},{5,7},{7,5},{8,10},{10,8},{9,1... | collective-permute-start | bytes 294920 | tf_op jit(solution)/shard_map/ppermute | solution.py:25
  74.5 3.7 %copy-start.3 = (bf16[384,768]{1,0:T(8,128)(2,1)S(1)}, bf16[384,768]{1,0:T(8,128)(2,1)}, u32[]{:S(2)}) copy-start(bf16[384,768]{1,0:T(8,128)(2,1)} %w_out.1) | copy-start | bytes 1769476
  79.4 2.1 %collective-permute-start.25 = (bf16[6,128,384]{2,1,0:T(8,128)(2,1)S(1)}, bf16[6,128,384]{2,1,0:T(8,128)(2,1)S(1)}, u32[]{:S(2)}, u32[]{:S(2)}) collective-permute-start(bf16[6,128,384]{2,1,0:T(8,128)(2,1)S(1)} %get-tuple-element.38), channel_id=1, source_target_pairs={{0,1},{1,0},{2,3},{3,2},{4,5},{5,4},{6,7},{7,6},{8,9},{9,8},{10,11... | collective-permute-start | bytes 1769480 | tf_op jit(solution)/shard_map/ppermute | solution.py:25

commit v6 on v5

--- a/solution.py
+++ b/solution.py
@@ -180,14 +180,12 @@
 
 
 def split_kernel(packed, *parts, tiles):
-    size = packed.shape[0] // tiles // PIECE * PIECE
+    size = packed.shape[0] // tiles
     count = len(parts)
     for at, part in enumerate(parts):
         for block in range(tiles * size // PIECE // count):
             source = (block * count + at) * PIECE
             part[block * PIECE : (block + 1) * PIECE] = packed[source : source + PIECE]
-    if packed.shape[0] > tiles * size:
-        parts[0][tiles * size // count :] = packed[tiles * size :]
 
 
 def tall_early_kernel(query, w_key, piece, logits, keys):
@@ -342,11 +340,11 @@
 def batches(blocks):
     every = tuple(range(CHUNKS))
     out = []
-    for step in range(1, blocks - 1):
+    for step in range(1, blocks):
         if step < blocks - 2:
             out.append((step, every))
         else:
-            out += [(step, (k,)) for k in every]
+            out += [(step, (k,)) for k in every if (step, k) != (blocks - 1, CHUNKS - 1)]
     return out
 
 
@@ -410,24 +408,22 @@
     def shared_rows(value):
         return [value] + [ring(value, "head", j) for j in range(1, cores)]
 
+    last, tail = blocks - 1, CHUNKS - 1
     fine = []
     for step in range(1, blocks):
-        if step == blocks - 1:
-            for k in range(CHUNKS):
-                size = moving[k].shape[0] // (PARTS * PIECE) * PIECE
-                rest = moving[k].shape[0] - PARTS * size
-                cut = call(
-                    functools.partial(split_kernel, tiles=width // LANES),
-                    [shape((size + (0 if n else rest), LANES), bf16) for n in range(PARTS)],
-                    [moving[k]],
-                    0,
-                )
-                fine += cut
-            fine = [ring(fine[q], "res") for q in range(len(fine))]
-            break
-        moving = [ring(moving[k], "res") for k in range(CHUNKS)]
+        if step == last:
+            size = moving[tail].shape[0] // (PARTS * PIECE) * PIECE
+            fine = call(
+                functools.partial(split_kernel, tiles=width // LANES),
+                [shape((size, LANES), bf16) for _ in range(PARTS)],
+                [moving[tail]],
+                0,
+            )
+            fine = [ring(fine[n], "res") for n in range(PARTS)]
+        count = tail if step == last else CHUNKS
+        moving = [ring(moving[k], "res") for k in range(count)]
         moved[step] = moving[0]
-        for k in range(CHUNKS):
+        for k in range(count):
             pieces[step, k] = shared_rows(moving[k])
 
     def kernel(function, outs, args, rows, both, scratch_rows, high=part):
@@ -461,26 +457,31 @@
         units.append(([shared], values))
 
     tall = []
-    for q, piece in enumerate(fine):
+    for n, piece in enumerate(fine):
         logits_shape = shape((tiles, PER_TILE * PIECE, cells), f32)
         mine = shared_rows(piece)
         early = kernel(tall_early_kernel, logits_shape, [query, w_key, piece], share / 2, 1, share, PIECE)
-        late = functools.partial(tall_late_kernel, first=q * PIECE, masked=masked)
+        late = functools.partial(tall_late_kernel, first=tail * part + n * PIECE, masked=masked)
         logits = kernel(
-            late, logits_shape, [query, w_key, fine[0], early] + mine[1:], (rows - share) / 2, 1, rows - share, PIECE
+            late,
+            logits_shape,
+            [query, w_key, moved[last], early] + mine[1:],
+            (rows - share) / 2,
+            1,
+            rows - share,
+            PIECE,
         )
         tall.append((exchange(logits), mine))
-    for k in range(len(tall) // PARTS):
-        group = tall[k * PARTS : (k + 1) * PARTS]
+    if tall:
         values = kernel(
             tall_values_kernel,
             shape((1, tiles, depth, spans), bf16),
-            [w_value] + sum([mine for _, mine in group], []),
+            [w_value] + sum([mine for _, mine in tall], []),
             rows,
             1,
             0,
         )
-        units.append(([shared for shared, _ in group], values))
+        units.append(([shared for shared, _ in tall], values))
 
     state = []
     state_shape = [

time: 82.6 us -> 82.8 us (level)
  waiting for transfers between devices: 41.6 us -> 45.9 us
  starting transfers between devices: 21.3 us -> 18.3 us
  Pallas kernels: 18.3 us -> 17.2 us
    ppermute x26 -> x23, waiting for transfers between devices: 41.6 us -> 45.9 us  [ring(): lax.ppermute(value, axis, [(i, (i + by) % length) for i in range(length)])]
    ppermute x26 -> x23, starting transfers between devices: 21.3 us -> 18.3 us  [ring(): lax.ppermute(value, axis, [(i, (i + by) % length) for i in range(length)])]
    pallas_call x24 -> x21, Pallas kernels: 16.1 us -> 15 us  [call(): pl.pallas_call(kernel, out_shape=out_shape, in_specs=specs, out_specs=who...]
  transfers between devices with their start and end apart: 26 -> 23, of which waited for: 12 -> 14; matrix products, arithmetic and copies ran while one was open for 0% -> 0% of each run, Pallas kernels for 19% -> 18%
where the time goes in v6:
time: 82.8 us; the launch traced here: 82.6 us
  waiting for transfers between devices  45.9 us (55%)
  starting transfers between devices  18.3 us (22%)
  Pallas kernels  17.2 us (21%)
  other arithmetic  0.93 us (1%)
    ppermute x23, waiting for transfers between devices, ring(): lax.ppermute(value, axis, [(i, (i + by) % length) for i in range(length)])  45.9 us
    ppermute x23, starting transfers between devices, ring(): lax.ppermute(value, axis, [(i, (i + by) % length) for i in range(length)])  18.3 us
    pallas_call x21, Pallas kernels, call(): pl.pallas_call(kernel, out_shape=out_shape, in_specs=specs, out_specs=who...  15 us
    pallas_call x2, Pallas kernels, shards(): pl.pallas_call(functools.partial(pack_kernel, chunk=k, share=share), out_...  2.16 us
  transfers between devices with their start and end apart: 23, of which 14 were waited for; matrix products, arithmetic and copies ran while one was open for 0% of the time, Pallas kernels for 18%

profile of v6, /device:TPU:0, one launch (start us, length us, event | category | flops | bytes accessed | tf_op | source)
XLA Modules:
  0.0 82.6 jit_solution(10917164898389639643)
XLA Ops:
  0.0 1.1 %shard_map.74 = bf16[1160,128]{1,0:T(8,128)(2,1)S(1)} custom-call(bf16[6,128,768]{2,1,0:T(8,128)(2,1)} %tokens.3, s32[1,128]{1,0:T(1,128)} %bitcast.1), custom_call_target="tpu_custom_call" | custom-call | tf_op jit(solution)/shard_map/pallas_call | solution.py:369
  1.1 0.0 copy-start
  1.2 0.0 copy-start.1
  1.2 0.0 copy-start.4
  1.2 0.0 copy-start.5
  1.2 3.1 %collective-permute-start.1 = (bf16[1160,128]{1,0:T(8,128)(2,1)S(1)}, bf16[1160,128]{1,0:T(8,128)(2,1)S(1)}, u32[]{:S(2)}, u32[]{:S(2)}) collective-permute-start(bf16[1160,128]{1,0:T(8,128)(2,1)S(1)} %shard_map.74), channel_id=1, source_target_pairs={{0,4},{4,8},{8,12},{12,0},{1,5},{5,9},{9,13},{13,1},{2,6},{6,10},{... | collective-permute-start | bytes 890888 | tf_op jit(solution)/shard_map/ppermute | solution.py:25
  4.3 1.0 %shard_map.75 = bf16[1152,128]{1,0:T(8,128)(2,1)S(1)} custom-call(bf16[6,128,768]{2,1,0:T(8,128)(2,1)} %tokens.3, s32[1,128]{1,0:T(1,128)} %bitcast.2), custom_call_target="tpu_custom_call" | custom-call | tf_op jit(solution)/shard_map/pallas_call | solution.py:369
  5.3 1.6 %collective-permute-start.4 = (bf16[1152,128]{1,0:T(8,128)(2,1)S(1)}, bf16[1152,128]{1,0:T(8,128)(2,1)S(1)}, u32[]{:S(2)}, u32[]{:S(2)}) collective-permute-start(bf16[1152,128]{1,0:T(8,128)(2,1)S(1)} %shard_map.75), channel_id=1, source_target_pairs={{0,4},{4,8},{8,12},{12,0},{1,5},{5,9},{9,13},{13,1},{2,6},{6,10},{... | collective-permute-start | bytes 884744 | tf_op jit(solution)/shard_map/ppermute | solution.py:25
  7.0 7.3 %collective-permute-done.1.refs_3_ = bf16[1160,128]{1,0:T(8,128)(2,1)S(1)} collective-permute-done((bf16[1160,128]{1,0:T(8,128)(2,1)S(1)}, bf16[1160,128]{1,0:T(8,128)(2,1)S(1)}, u32[]{:S(2)}, u32[]{:S(2)}) %collective-permute-start.1) | collective-permute-done | bytes 296992 | tf_op jit(solution)/shard_map/ppermute | solution.py:25
  14.2 0.0 collective-permute-start.2
  14.2 6.3 %collective-permute-done.4.refs_5_ = bf16[1152,128]{1,0:T(8,128)(2,1)S(1)} collective-permute-done((bf16[1152,128]{1,0:T(8,128)(2,1)S(1)}, bf16[1152,128]{1,0:T(8,128)(2,1)S(1)}, u32[]{:S(2)}, u32[]{:S(2)}) %collective-permute-start.4) | collective-permute-done | bytes 294944 | tf_op jit(solution)/shard_map/ppermute | solution.py:25
  20.6 6.4 %collective-permute-done.2.marks.piece.refs_0_ = bf16[1160,128]{1,0:T(8,128)(2,1)S(1)} collective-permute-done((bf16[1160,128]{1,0:T(8,128)(2,1)S(1)}, bf16[1160,128]{1,0:T(8,128)(2,1)S(1)}, u32[]{:S(2)}, u32[]{:S(2)}) %collective-permute-start.2) | collective-permute-done | bytes 296992 | tf_op jit(solution)/shard_map/ppermute | solution.py:25
  26.9 1.7 %collective-permute-start = (s32[6]{0:T(128)S(1)}, s32[6]{0:T(128)S(1)}, u32[]{:S(2)}, u32[]{:S(2)}) collective-permute-start(s32[6]{0:T(128)S(1)} %copy-done.6), channel_id=1, source_target_pairs={{0,2},{2,0},{1,3},{3,1},{4,6},{6,4},{5,7},{7,5},{8,10},{10,8},{9,1... | collective-permute-start | bytes 80 | tf_op jit(solution)/shard_map/ppermute | solution.py:25
  28.6 4.6 %collective-permute-done.5.packed.piece.refs_0_ = bf16[1152,128]{1,0:T(8,128)(2,1)S(1)} collective-permute-done((bf16[1152,128]{1,0:T(8,128)(2,1)S(1)}, bf16[1152,128]{1,0:T(8,128)(2,1)S(1)}, u32[]{:S(2)}, u32[]{:S(2)}) %collective-permute-start.5) | collective-permute-done | bytes 294944 | tf_op jit(solution)/shard_map/ppermute | solution.py:25
  33.3 0.1 collective-permute-start.9
  33.3 1.6 %collective-permute-start.6 = (bf16[576,128]{1,0:T(8,128)(2,1)S(1)}, bf16[576,128]{1,0:T(8,128)(2,1)S(1)}, u32[]{:S(2)}, u32[]{:S(2)}) collective-permute-start(bf16[576,128]{1,0:T(8,128)(2,1)S(1)} %get-tuple-element.21), channel_id=1, source_target_pairs={{0,4},{4,8},{8,12},{12,0},{1,5},{5,9},{9,13},{13,1},{2,6},{6,10},{... | collective-permute-start | bytes 442376 | tf_op jit(solution)/shard_map/ppermute | solution.py:25
  34.9 0.0 collective-permute-done.18.refs_6_
  34.9 0.0 collective-permute-start.12
  34.9 0.0 collective-permute-done.17.refs_4_
  34.9 0.5 collective-permute-start.20
  35.4 2.9 %shard_map.73 = (bf16[3,128,768]{2,1,0:T(8,128)(2,1)S(1)}, f32[2,3,128,128]{3,2,1,0:T(8,128)S(1)}, bf16[2,3,128,768]{3,2,1,0:T(8,128)(2,1)S(1)}) custom-call(s32[6]{0:T(128)S(1)} %copy-done.6, s32[6]{0:T(128)S(1)} %collective-permute-done.refs_1_, s32[1,128]{1,0:T(1,128)S(1)} %bitcast.3, bf16[6,128,768]{2,1,0:T(8,128)(2,1)S(1)} %copy-done.2, ...), custom_call_target="tpu_custom_call" | custom-call | flops 1509949440 | bytes 2949680 | tf_op jit(solution)/shard_map/pallas_call | solution.py:36
  38.4 1.2 %collective-permute-done.3.marks.piece.refs_0_ = bf16[1160,128]{1,0:T(8,128)(2,1)S(1)} collective-permute-done((bf16[1160,128]{1,0:T(8,128)(2,1)S(1)}, bf16[1160,128]{1,0:T(8,128)(2,1)S(1)}, u32[]{:S(2)}, u32[]{:S(2)}) %collective-permute-start.3) | collective-permute-done | bytes 296992 | tf_op jit(solution)/shard_map/ppermute | solution.py:25
  39.6 0.0 collective-permute-start.14
  39.6 1.9 %shard_map.88 = (f32[2,3,128,128]{3,2,1,0:T(8,128)S(1)}, bf16[2,3,128,768]{3,2,1,0:T(8,128)(2,1)S(1)}) custom-call(bf16[3,128,768]{2,1,0:T(8,128)(2,1)S(1)} %get-tuple-element.20.query.refs_0_, bf16[768,384]{1,0:T(8,128)(2,1)S(1)} %copy-done, bf16[768,384]{1,0:T(8,128)(2,1)S(1)} %copy-done.1, bf16[1160,128]{1,0:T(8,128)(2,1)S(1)} %collective-permute-done.1.refs_3_, ...), custom_call_target="tpu_custom_call" | custom-call | flops 1056964608 | bytes 2953216 | tf_op jit(solution)/shard_map/pallas_call | solution.py:36
  41.5 1.2 %collective-permute-done.9.piece.refs_2_ = bf16[576,128]{1,0:T(8,128)(2,1)S(1)} collective-permute-done((bf16[576,128]{1,0:T(8,128)(2,1)S(1)}, bf16[576,128]{1,0:T(8,128)(2,1)S(1)}, u32[]{:S(2)}, u32[]{:S(2)}) %collective-permute-start.9) | collective-permute-done | bytes 147488 | tf_op jit(solution)/shard_map/ppermute | solution.py:25
  42.8 1.7 %collective-permute-start.16 = (f32[2,3,128,128]{3,2,1,0:T(8,128)S(1)}, f32[2,3,128,128]{3,2,1,0:T(8,128)S(1)}, u32[]{:S(2)}, u32[]{:S(2)}) collective-permute-start(f32[2,3,128,128]{3,2,1,0:T(8,128)S(1)} %get-tuple-element.23.refs_0_), channel_id=1, source_target_pairs={{0,2},{2,0},{1,3},{3,1},{4,6},{6,4},{5,7},{7,5},{8,10},{10,8},{9,1... | collective-permute-start | bytes 1179656 | tf_op jit(solution)/shard_map/ppermute | solution.py:25
  44.5 0.6 collective-permute-done.6.piece.refs_0_
  45.1 1.5 %collective-permute-start.19 = (f32[2,3,128,128]{3,2,1,0:T(8,128)S(1)}, f32[2,3,128,128]{3,2,1,0:T(8,128)S(1)}, u32[]{:S(2)}, u32[]{:S(2)}) collective-permute-start(f32[2,3,128,128]{3,2,1,0:T(8,128)S(1)} %get-tuple-element.25.refs_3_), channel_id=1, source_target_pairs={{0,2},{2,0},{1,3},{3,1},{4,6},{6,4},{5,7},{7,5},{8,10},{10,8},{9,1... | collective-permute-start | bytes 1179656 | tf_op jit(solution)/shard_map/ppermute | solution.py:25
  46.6 0.0 collective-permute-done.12.refs_0_.refs_1_
  46.6 0.0 collective-permute-start.10
  46.6 0.5 collective-permute-start.7
  47.1 0.6 shard_map.89.before
  47.6 0.6 shard_map.90.refs_6_
  48.2 0.6 collective-permute-start.21
  48.8 0.6 shard_map.82.before
  49.4 0.6 shard_map.83.refs_0_
  50.0 0.6 shard_map.85.before
  50.5 0.6 shard_map.86.refs_3_
  51.1 1.6 %collective-permute-start.13 = (f32[1,3,128,128]{3,2,1,0:T(8,128)S(1)}, f32[1,3,128,128]{3,2,1,0:T(8,128)S(1)}, u32[]{:S(2)}, u32[]{:S(2)}) collective-permute-start(f32[1,3,128,128]{3,2,1,0:T(8,128)S(1)} %shard_map.83.refs_0_), channel_id=1, source_target_pairs={{0,2},{2,0},{1,3},{3,1},{4,6},{6,4},{5,7},{7,5},{8,10},{10,8},{9,1... | collective-permute-start | bytes 589832 | tf_op jit(solution)/shard_map/ppermute | solution.py:25
  52.7 0.5 collective-permute-start.15
  53.2 0.5 shard_map.79.before
  53.7 0.5 shard_map.77.before
  54.2 0.5 shard_map.84.refs_2_
  54.7 0.5 shard_map.81.refs_4_
  55.1 0.5 shard_map.80.refs_2_
  55.6 0.5 shard_map.78.refs_0_
  56.1 0.0 collective-permute-done.16.refs_1_
  56.1 1.6 %collective-permute-start.11 = (f32[3,64,128]{2,1,0:T(8,128)S(1)}, f32[3,64,128]{2,1,0:T(8,128)S(1)}, u32[]{:S(2)}, u32[]{:S(2)}) collective-permute-start(f32[3,64,128]{2,1,0:T(8,128)S(1)} %shard_map.80.refs_2_), channel_id=1, source_target_pairs={{0,2},{2,0},{1,3},{3,1},{4,6},{6,4},{5,7},{7,5},{8,10},{10,8},{9,1... | collective-permute-start | bytes 294920 | tf_op jit(solution)/shard_map/ppermute | solution.py:25
  57.7 5.5 %collective-permute-done.19.refs_4_ = f32[2,3,128,128]{3,2,1,0:T(8,128)S(1)} collective-permute-done((f32[2,3,128,128]{3,2,1,0:T(8,128)S(1)}, f32[2,3,128,128]{3,2,1,0:T(8,128)S(1)}, u32[]{:S(2)}, u32[]{:S(2)}) %collective-permute-start.19) | collective-permute-done | bytes 393248 | tf_op jit(solution)/shard_map/ppermute | solution.py:25
  63.2 1.7 %collective-permute-start.8 = (f32[3,64,128]{2,1,0:T(8,128)S(1)}, f32[3,64,128]{2,1,0:T(8,128)S(1)}, u32[]{:S(2)}, u32[]{:S(2)}) collective-permute-start(f32[3,64,128]{2,1,0:T(8,128)S(1)} %shard_map.78.refs_0_), channel_id=1, source_target_pairs={{0,2},{2,0},{1,3},{3,1},{4,6},{6,4},{5,7},{7,5},{8,10},{10,8},{9,1... | collective-permute-start | bytes 294920 | tf_op jit(solution)/shard_map/ppermute | solution.py:25
  64.9 0.5 shard_map.91.refs_8_
  65.4 2.0 %collective-permute-done.21.refs_7_ = f32[1,3,128,128]{3,2,1,0:T(8,128)S(1)} collective-permute-done((f32[1,3,128,128]{3,2,1,0:T(8,128)S(1)}, f32[1,3,128,128]{3,2,1,0:T(8,128)S(1)}, u32[]{:S(2)}, u32[]{:S(2)}) %collective-permute-start.21) | collective-permute-done | bytes 196640 | tf_op jit(solution)/shard_map/ppermute | solution.py:25
  67.4 0.8 shard_map.92
  68.2 0.5 shard_map.87.refs_5_
  68.7 2.9 %collective-permute-done.13.refs_1_ = f32[1,3,128,128]{3,2,1,0:T(8,128)S(1)} collective-permute-done((f32[1,3,128,128]{3,2,1,0:T(8,128)S(1)}, f32[1,3,128,128]{3,2,1,0:T(8,128)S(1)}, u32[]{:S(2)}, u32[]{:S(2)}) %collective-permute-start.13) | collective-permute-done | bytes 196640 | tf_op jit(solution)/shard_map/ppermute | solution.py:25
  71.6 4.2 %collective-permute-done.15.refs_4_ = f32[1,3,128,128]{3,2,1,0:T(8,128)S(1)} collective-permute-done((f32[1,3,128,128]{3,2,1,0:T(8,128)S(1)}, f32[1,3,128,128]{3,2,1,0:T(8,128)S(1)}, u32[]{:S(2)}, u32[]{:S(2)}) %collective-permute-start.15) | collective-permute-done | bytes 196640 | tf_op jit(solution)/shard_map/ppermute | solution.py:25
  75.8 0.4 shard_map.93
  76.2 1.1 %collective-permute-done.11.refs_3_ = f32[3,64,128]{2,1,0:T(8,128)S(1)} collective-permute-done((f32[3,64,128]{2,1,0:T(8,128)S(1)}, f32[3,64,128]{2,1,0:T(8,128)S(1)}, u32[]{:S(2)}, u32[]{:S(2)}) %collective-permute-start.11) | collective-permute-done | bytes 98336 | tf_op jit(solution)/shard_map/ppermute | solution.py:25
  77.4 1.1 %collective-permute-done.8.refs_1_ = f32[3,64,128]{2,1,0:T(8,128)S(1)} collective-permute-done((f32[3,64,128]{2,1,0:T(8,128)S(1)}, f32[3,64,128]{2,1,0:T(8,128)S(1)}, u32[]{:S(2)}, u32[]{:S(2)}) %collective-permute-start.8) | collective-permute-done | bytes 98336 | tf_op jit(solution)/shard_map/ppermute | solution.py:25
  78.4 1.2 %shard_map.94 = (bf16[6,128,384]{2,1,0:T(8,128)(2,1)S(1)}, bf16[6,128,384]{2,1,0:T(8,128)(2,1)S(1)}) custom-call(f32[3,64,128]{2,1,0:T(8,128)S(1)} %shard_map.78.refs_0_, f32[3,64,128]{2,1,0:T(8,128)S(1)} %collective-permute-done.8.refs_1_, f32[3,64,128]{2,1,0:T(8,128)S(1)} %shard_map.80.refs_2_, f32[3,64,128]{2,1,0:T(8,128)S(1)} %collective-permute-done.11.refs_3_, ...), custom_call_target="tpu_custom_call" | custom-call | flops 301989888 | bytes 3145728 | tf_op jit(solution)/shard_map/pallas_call | solution.py:36
  79.6 0.1 collective-permute-start.22
  79.7 0.6 shard_map.95
  80.2 1.4 %collective-permute-done.22 = bf16[6,128,384]{2,1,0:T(8,128)(2,1)S(1)} collective-permute-done((bf16[6,128,384]{2,1,0:T(8,128)(2,1)S(1)}, bf16[6,128,384]{2,1,0:T(8,128)(2,1)S(1)}, u32[]{:S(2)}, u32[]{:S(2)}) %collective-permute-start.22) | collective-permute-done | bytes 589856 | tf_op jit(solution)/shard_map/ppermute | solution.py:25
  81.7 0.9 %add_convert_fusion = bf16[6,128,384]{2,1,0:T(8,128)(2,1)} fusion(f32[6,128,384]{2,1,0:T(8,128)S(1)} %shard_map.95, bf16[6,128,384]{2,1,0:T(8,128)(2,1)S(1)} %collective-permute-done.22), kind=kLoop, calls=%fused_computation | loop fusion | flops 884736 | bytes 2359296 | tf_op jit(solution)/shard_map/convert_element_type | solution.py:538
  (20 shorter events, 0.1 us)
Async XLA Ops:
  0.0 26.9 %copy-start.6 = (s32[6]{0:T(128)S(1)}, s32[6]{0:T(128)}, u32[]{:S(2)}) copy-start(s32[6]{0:T(128)} %refs_0_.1) | copy-start | bytes 76
  0.0 35.4 %copy-start.2 = (bf16[6,128,768]{2,1,0:T(8,128)(2,1)S(1)}, bf16[6,128,768]{2,1,0:T(8,128)(2,1)}, u32[]{:S(2)}) copy-start(bf16[6,128,768]{2,1,0:T(8,128)(2,1)} %tokens.3) | copy-start | bytes 3538948
  1.1 34.3 %copy-start = (bf16[768,384]{1,0:T(8,128)(2,1)S(1)}, bf16[768,384]{1,0:T(8,128)(2,1)}, u32[]{:S(2)}) copy-start(bf16[768,384]{1,0:T(8,128)(2,1)} %w_key.19) | copy-start | bytes 1769476
  1.2 34.3 %copy-start.1 = (bf16[768,384]{1,0:T(8,128)(2,1)S(1)}, bf16[768,384]{1,0:T(8,128)(2,1)}, u32[]{:S(2)}) copy-start(bf16[768,384]{1,0:T(8,128)(2,1)} %w_value.7) | copy-start | bytes 1769476
  1.2 34.2 %copy-start.4 = (s32[128]{0:T(128)S(1)}, s32[128]{0:T(128)}, u32[]{:S(2)}) copy-start(s32[128]{0:T(128)} %param.9) | copy-start | bytes 1540
  1.2 34.2 %copy-start.5 = (bf16[768,384]{1,0:T(8,128)(2,1)S(1)}, bf16[768,384]{1,0:T(8,128)(2,1)}, u32[]{:S(2)}) copy-start(bf16[768,384]{1,0:T(8,128)(2,1)} %refs_4_.1) | copy-start | bytes 1769476
  1.2 13.0 %collective-permute-start.1 = (bf16[1160,128]{1,0:T(8,128)(2,1)S(1)}, bf16[1160,128]{1,0:T(8,128)(2,1)S(1)}, u32[]{:S(2)}, u32[]{:S(2)}) collective-permute-start(bf16[1160,128]{1,0:T(8,128)(2,1)S(1)} %shard_map.74), channel_id=1, source_target_pairs={{0,4},{4,8},{8,12},{12,0},{1,5},{5,9},{9,13},{13,1},{2,6},{6,10},{... | collective-permute-start | bytes 890888 | tf_op jit(solution)/shard_map/ppermute | solution.py:25
  5.3 15.2 %collective-permute-start.4 = (bf16[1152,128]{1,0:T(8,128)(2,1)S(1)}, bf16[1152,128]{1,0:T(8,128)(2,1)S(1)}, u32[]{:S(2)}, u32[]{:S(2)}) collective-permute-start(bf16[1152,128]{1,0:T(8,128)(2,1)S(1)} %shard_map.75), channel_id=1, source_target_pairs={{0,4},{4,8},{8,12},{12,0},{1,5},{5,9},{9,13},{13,1},{2,6},{6,10},{... | collective-permute-start | bytes 884744 | tf_op jit(solution)/shard_map/ppermute | solution.py:25
  14.2 12.7 %collective-permute-start.2 = (bf16[1160,128]{1,0:T(8,128)(2,1)S(1)}, bf16[1160,128]{1,0:T(8,128)(2,1)S(1)}, u32[]{:S(2)}, u32[]{:S(2)}) collective-permute-start(bf16[1160,128]{1,0:T(8,128)(2,1)S(1)} %collective-permute-done.1.refs_3_), channel_id=1, source_target_pairs={{0,4},{4,8},{8,12},{12,0},{1,5},{5,9},{9,13},{13,1},{2,6},{6,10},{... | collective-permute-start | bytes 890888 | tf_op jit(solution)/shard_map/ppermute | solution.py:25
  14.2 20.7 %collective-permute-start.17 = (bf16[1160,128]{1,0:T(8,128)(2,1)S(1)}, bf16[1160,128]{1,0:T(8,128)(2,1)S(1)}, u32[]{:S(2)}, u32[]{:S(2)}) collective-permute-start(bf16[1160,128]{1,0:T(8,128)(2,1)S(1)} %collective-permute-done.1.refs_3_), channel_id=1, source_target_pairs={{0,1},{1,0},{2,3},{3,2},{4,5},{5,4},{6,7},{7,6},{8,9},{9,8},{10,11... | collective-permute-start | bytes 890888 | tf_op jit(solution)/shard_map/ppermute | solution.py:25
  20.5 12.7 %collective-permute-start.5 = (bf16[1152,128]{1,0:T(8,128)(2,1)S(1)}, bf16[1152,128]{1,0:T(8,128)(2,1)S(1)}, u32[]{:S(2)}, u32[]{:S(2)}) collective-permute-start(bf16[1152,128]{1,0:T(8,128)(2,1)S(1)} %collective-permute-done.4.refs_5_), channel_id=1, source_target_pairs={{0,4},{4,8},{8,12},{12,0},{1,5},{5,9},{9,13},{13,1},{2,6},{6,10},{... | collective-permute-start | bytes 884744 | tf_op jit(solution)/shard_map/ppermute | solution.py:25
  20.5 14.3 %collective-permute-start.18 = (bf16[1152,128]{1,0:T(8,128)(2,1)S(1)}, bf16[1152,128]{1,0:T(8,128)(2,1)S(1)}, u32[]{:S(2)}, u32[]{:S(2)}) collective-permute-start(bf16[1152,128]{1,0:T(8,128)(2,1)S(1)} %collective-permute-done.4.refs_5_), channel_id=1, source_target_pairs={{0,1},{1,0},{2,3},{3,2},{4,5},{5,4},{6,7},{7,6},{8,9},{9,8},{10,11... | collective-permute-start | bytes 884744 | tf_op jit(solution)/shard_map/ppermute | solution.py:25
  26.9 12.7 %collective-permute-start.3 = (bf16[1160,128]{1,0:T(8,128)(2,1)S(1)}, bf16[1160,128]{1,0:T(8,128)(2,1)S(1)}, u32[]{:S(2)}, u32[]{:S(2)}) collective-permute-start(bf16[1160,128]{1,0:T(8,128)(2,1)S(1)} %collective-permute-done.2.marks.piece.refs_0_), channel_id=1, source_target_pairs={{0,4},{4,8},{8,12},{12,0},{1,5},{5,9},{9,13},{13,1},{2,6},{6,10},{... | collective-permute-start | bytes 890888 | tf_op jit(solution)/shard_map/ppermute | solution.py:25
  26.9 6.4 %collective-permute-start = (s32[6]{0:T(128)S(1)}, s32[6]{0:T(128)S(1)}, u32[]{:S(2)}, u32[]{:S(2)}) collective-permute-start(s32[6]{0:T(128)S(1)} %copy-done.6), channel_id=1, source_target_pairs={{0,2},{2,0},{1,3},{3,1},{4,6},{6,4},{5,7},{7,5},{8,10},{10,8},{9,1... | collective-permute-start | bytes 80 | tf_op jit(solution)/shard_map/ppermute | solution.py:25
  33.3 9.5 %collective-permute-start.9 = (bf16[576,128]{1,0:T(8,128)(2,1)S(1)}, bf16[576,128]{1,0:T(8,128)(2,1)S(1)}, u32[]{:S(2)}, u32[]{:S(2)}) collective-permute-start(bf16[576,128]{1,0:T(8,128)(2,1)S(1)} %get-tuple-element.22), channel_id=1, source_target_pairs={{0,4},{4,8},{8,12},{12,0},{1,5},{5,9},{9,13},{13,1},{2,6},{6,10},{... | collective-permute-start | bytes 442376 | tf_op jit(solution)/shard_map/ppermute | solution.py:25
  33.3 11.7 %collective-permute-start.6 = (bf16[576,128]{1,0:T(8,128)(2,1)S(1)}, bf16[576,128]{1,0:T(8,128)(2,1)S(1)}, u32[]{:S(2)}, u32[]{:S(2)}) collective-permute-start(bf16[576,128]{1,0:T(8,128)(2,1)S(1)} %get-tuple-element.21), channel_id=1, source_target_pairs={{0,4},{4,8},{8,12},{12,0},{1,5},{5,9},{9,13},{13,1},{2,6},{6,10},{... | collective-permute-start | bytes 442376 | tf_op jit(solution)/shard_map/ppermute | solution.py:25
  34.9 11.7 %collective-permute-start.12 = (bf16[1152,128]{1,0:T(8,128)(2,1)S(1)}, bf16[1152,128]{1,0:T(8,128)(2,1)S(1)}, u32[]{:S(2)}, u32[]{:S(2)}) collective-permute-start(bf16[1152,128]{1,0:T(8,128)(2,1)S(1)} %collective-permute-done.5.packed.piece.refs_0_), channel_id=1, source_target_pairs={{0,1},{1,0},{2,3},{3,2},{4,5},{5,4},{6,7},{7,6},{8,9},{9,8},{10,11... | collective-permute-start | bytes 884744 | tf_op jit(solution)/shard_map/ppermute | solution.py:25
  34.9 11.7 %collective-permute-start.20 = (bf16[1160,128]{1,0:T(8,128)(2,1)S(1)}, bf16[1160,128]{1,0:T(8,128)(2,1)S(1)}, u32[]{:S(2)}, u32[]{:S(2)}) collective-permute-start(bf16[1160,128]{1,0:T(8,128)(2,1)S(1)} %collective-permute-done.2.marks.piece.refs_0_), channel_id=1, source_target_pairs={{0,1},{1,0},{2,3},{3,2},{4,5},{5,4},{6,7},{7,6},{8,9},{9,8},{10,11... | collective-permute-start | bytes 890888 | tf_op jit(solution)/shard_map/ppermute | solution.py:25
  39.6 8.6 %collective-permute-start.14 = (bf16[1160,128]{1,0:T(8,128)(2,1)S(1)}, bf16[1160,128]{1,0:T(8,128)(2,1)S(1)}, u32[]{:S(2)}, u32[]{:S(2)}) collective-permute-start(bf16[1160,128]{1,0:T(8,128)(2,1)S(1)} %collective-permute-done.3.marks.piece.refs_0_), channel_id=1, source_target_pairs={{0,1},{1,0},{2,3},{3,2},{4,5},{5,4},{6,7},{7,6},{8,9},{9,8},{10,11... | collective-permute-start | bytes 890888 | tf_op jit(solution)/shard_map/ppermute | solution.py:25
  42.8 13.4 %collective-permute-start.16 = (f32[2,3,128,128]{3,2,1,0:T(8,128)S(1)}, f32[2,3,128,128]{3,2,1,0:T(8,128)S(1)}, u32[]{:S(2)}, u32[]{:S(2)}) collective-permute-start(f32[2,3,128,128]{3,2,1,0:T(8,128)S(1)} %get-tuple-element.23.refs_0_), channel_id=1, source_target_pairs={{0,2},{2,0},{1,3},{3,1},{4,6},{6,4},{5,7},{7,5},{8,10},{10,8},{9,1... | collective-permute-start | bytes 1179656 | tf_op jit(solution)/shard_map/ppermute | solution.py:25
  45.1 18.1 %collective-permute-start.19 = (f32[2,3,128,128]{3,2,1,0:T(8,128)S(1)}, f32[2,3,128,128]{3,2,1,0:T(8,128)S(1)}, u32[]{:S(2)}, u32[]{:S(2)}) collective-permute-start(f32[2,3,128,128]{3,2,1,0:T(8,128)S(1)} %get-tuple-element.25.refs_3_), channel_id=1, source_target_pairs={{0,2},{2,0},{1,3},{3,1},{4,6},{6,4},{5,7},{7,5},{8,10},{10,8},{9,1... | collective-permute-start | bytes 1179656 | tf_op jit(solution)/shard_map/ppermute | solution.py:25
  46.6 4.5 %collective-permute-start.10 = (bf16[576,128]{1,0:T(8,128)(2,1)S(1)}, bf16[576,128]{1,0:T(8,128)(2,1)S(1)}, u32[]{:S(2)}, u32[]{:S(2)}) collective-permute-start(bf16[576,128]{1,0:T(8,128)(2,1)S(1)} %collective-permute-done.9.piece.refs_2_), channel_id=1, source_target_pairs={{0,1},{1,0},{2,3},{3,2},{4,5},{5,4},{6,7},{7,6},{8,9},{9,8},{10,11... | collective-permute-start | bytes 442376 | tf_op jit(solution)/shard_map/ppermute | solution.py:25
  46.6 6.1 %collective-permute-start.7 = (bf16[576,128]{1,0:T(8,128)(2,1)S(1)}, bf16[576,128]{1,0:T(8,128)(2,1)S(1)}, u32[]{:S(2)}, u32[]{:S(2)}) collective-permute-start(bf16[576,128]{1,0:T(8,128)(2,1)S(1)} %collective-permute-done.6.piece.refs_0_), channel_id=1, source_target_pairs={{0,1},{1,0},{2,3},{3,2},{4,5},{5,4},{6,7},{7,6},{8,9},{9,8},{10,11... | collective-permute-start | bytes 442376 | tf_op jit(solution)/shard_map/ppermute | solution.py:25
  48.2 19.2 %collective-permute-start.21 = (f32[1,3,128,128]{3,2,1,0:T(8,128)S(1)}, f32[1,3,128,128]{3,2,1,0:T(8,128)S(1)}, u32[]{:S(2)}, u32[]{:S(2)}) collective-permute-start(f32[1,3,128,128]{3,2,1,0:T(8,128)S(1)} %shard_map.90.refs_6_), channel_id=1, source_target_pairs={{0,2},{2,0},{1,3},{3,1},{4,6},{6,4},{5,7},{7,5},{8,10},{10,8},{9,1... | collective-permute-start | bytes 589832 | tf_op jit(solution)/shard_map/ppermute | solution.py:25
  51.1 20.5 %collective-permute-start.13 = (f32[1,3,128,128]{3,2,1,0:T(8,128)S(1)}, f32[1,3,128,128]{3,2,1,0:T(8,128)S(1)}, u32[]{:S(2)}, u32[]{:S(2)}) collective-permute-start(f32[1,3,128,128]{3,2,1,0:T(8,128)S(1)} %shard_map.83.refs_0_), channel_id=1, source_target_pairs={{0,2},{2,0},{1,3},{3,1},{4,6},{6,4},{5,7},{7,5},{8,10},{10,8},{9,1... | collective-permute-start | bytes 589832 | tf_op jit(solution)/shard_map/ppermute | solution.py:25
  52.7 23.1 %collective-permute-start.15 = (f32[1,3,128,128]{3,2,1,0:T(8,128)S(1)}, f32[1,3,128,128]{3,2,1,0:T(8,128)S(1)}, u32[]{:S(2)}, u32[]{:S(2)}) collective-permute-start(f32[1,3,128,128]{3,2,1,0:T(8,128)S(1)} %shard_map.86.refs_3_), channel_id=1, source_target_pairs={{0,2},{2,0},{1,3},{3,1},{4,6},{6,4},{5,7},{7,5},{8,10},{10,8},{9,1... | collective-permute-start | bytes 589832 | tf_op jit(solution)/shard_map/ppermute | solution.py:25
  56.1 21.3 %collective-permute-start.11 = (f32[3,64,128]{2,1,0:T(8,128)S(1)}, f32[3,64,128]{2,1,0:T(8,128)S(1)}, u32[]{:S(2)}, u32[]{:S(2)}) collective-permute-start(f32[3,64,128]{2,1,0:T(8,128)S(1)} %shard_map.80.refs_2_), channel_id=1, source_target_pairs={{0,2},{2,0},{1,3},{3,1},{4,6},{6,4},{5,7},{7,5},{8,10},{10,8},{9,1... | collective-permute-start | bytes 294920 | tf_op jit(solution)/shard_map/ppermute | solution.py:25
  63.2 15.3 %collective-permute-start.8 = (f32[3,64,128]{2,1,0:T(8,128)S(1)}, f32[3,64,128]{2,1,0:T(8,128)S(1)}, u32[]{:S(2)}, u32[]{:S(2)}) collective-permute-start(f32[3,64,128]{2,1,0:T(8,128)S(1)} %shard_map.78.refs_0_), channel_id=1, source_target_pairs={{0,2},{2,0},{1,3},{3,1},{4,6},{6,4},{5,7},{7,5},{8,10},{10,8},{9,1... | collective-permute-start | bytes 294920 | tf_op jit(solution)/shard_map/ppermute | solution.py:25
  75.8 2.6 %copy-start.3 = (bf16[384,768]{1,0:T(8,128)(2,1)S(1)}, bf16[384,768]{1,0:T(8,128)(2,1)}, u32[]{:S(2)}) copy-start(bf16[384,768]{1,0:T(8,128)(2,1)} %w_out.1) | copy-start | bytes 1769476
  79.6 2.1 %collective-permute-start.22 = (bf16[6,128,384]{2,1,0:T(8,128)(2,1)S(1)}, bf16[6,128,384]{2,1,0:T(8,128)(2,1)S(1)}, u32[]{:S(2)}, u32[]{:S(2)}) collective-permute-start(bf16[6,128,384]{2,1,0:T(8,128)(2,1)S(1)} %get-tuple-element.34), channel_id=1, source_target_pairs={{0,1},{1,0},{2,3},{3,2},{4,5},{5,4},{6,7},{7,6},{8,9},{9,8},{10,11... | collective-permute-start | bytes 1769480 | tf_op jit(solution)/shard_map/ppermute | solution.py:25

commit v7 on v6

--- a/solution.py
+++ b/solution.py
@@ -307,34 +307,48 @@
         top[tile], denom[tile], accum[tile] = absorb(units, state, tile, rows)
 
 
-def columns_of(w_out, ahead, cores):
+def columns_kernel(w_out, *targets, cores):
     columns = w_out.shape[1] // cores
-    at = lax.rem(lax.axis_index("head") + ahead, cores) * columns
-    return w_out[:, pl.ds(pl.multiple_of(at, LANES), columns)]
-
-
-def finish_kernel(*refs, sizes, carried, cores):
+    for ahead, target in enumerate(targets):
+        at = lax.rem(lax.axis_index("head") + ahead, cores) * columns
+        target[...] = w_out[:, pl.ds(pl.multiple_of(at, LANES), columns)]
+
+
+def finish_kernel(*refs, sizes, carried, cores, tile):
     units, refs = read_units(refs, sizes)
     state = refs[:3] if carried else None
-    w_out, attended, sent = refs[-3:]
-    rows, _, _ = attended.shape
-    for tile in range(attended.shape[2] // LANES):
-        _, denom, accum = absorb(units, state, tile, rows)
-        denom = per_head(denom, sum_over)
-        for row in range(rows):
-            part = accum[:, row * LANES : (row + 1) * LANES] / denom
-            attended[row, :, tile * LANES : (tile + 1) * LANES] = part.astype(jnp.bfloat16)
-    write_output(attended, columns_of(w_out, 1 % cores, cores), sent, cores)
-
-
-def write_output(attended, w, target, cores):
+    attended = refs[-1]
     rows = attended.shape[0]
+    _, denom, accum = absorb(units, state, tile, rows)
+    denom = per_head(denom, sum_over)
     for row in range(rows):
-        target[own_row(row, rows // cores, cores)] = dot(attended[row], w).astype(target.dtype)
-
-
-def output_kernel(attended, w_out, kept, *, ahead, cores):
-    write_output(attended, columns_of(w_out, ahead, cores), kept, cores)
+        part = accum[:, row * LANES : (row + 1) * LANES] / denom
+        attended[own_row(row, rows // cores, cores)] = part.astype(jnp.bfloat16)
+
+
+def product(tiles, w, row):
+    return dot(jnp.concatenate([tile[row] for tile in tiles], axis=1), w[...])
+
+
+def local_kernel(w, *refs):
+    tiles, kept = refs[:-1], refs[-1]
+    for row in range(kept.shape[0]):
+        kept[row] = product(tiles, w, row)
+
+
+def output_kernel(kept, *refs, tiles):
+    parts, (out, staged, done) = refs[:-3], refs[-3:]
+    groups = [parts[at : at + tiles + 1] for at in range(0, len(parts), tiles + 1)]
+    copies = []
+    for row in range(kept.shape[0]):
+        total = kept[row]
+        for group in groups:
+            total = total + product(group[1:], group[0], row)
+        staged[row] = total.astype(jnp.bfloat16)
+        copies.append(pltpu.make_async_copy(staged.at[row], out.at[row], done.at[row]))
+        copies[-1].start()
+    for copy in copies:
+        copy.wait()
 
 
 def batches(blocks):
@@ -380,6 +394,17 @@
         )(pltpu.with_memory_space_constraint(tokens, pltpu.HBM), pltpu.with_memory_space_constraint(key_mask, pltpu.HBM))
         for k in range(CHUNKS)
     ]
+    moving[0], tokens, w_query, w_key, w_value, w_out = lax.optimization_barrier(
+        (moving[0], tokens, w_query, w_key, w_value, w_out)
+    )
+    columns = width // cores
+    w_parts = call(
+        functools.partial(columns_kernel, cores=cores),
+        [shape((inner, columns), bf16) for _ in range(cores)],
+        [w_out],
+        0,
+    )
+    w_parts = [w_parts[0]] + [ring(w_parts[k], "head", k) for k in range(1, cores)]
     counts = [weights]
     for k in range(1, holders):
         counts.append(ring(weights, "seq", k))
@@ -509,33 +534,28 @@
             work(group),
         )
     group = units[slice(*cuts[-1])]
-    columns = width // cores
-    attended, sent = call(
-        functools.partial(
-            finish_kernel, sizes=sizes_of(group), carried=bool(state), cores=cores
-        ),
-        [shape((rows, cells, inner), bf16), shape((rows, cells, columns), bf16)],
-        flatten(group) + list(state) + [w_out],
-        work(group) + 2 * rows * cells * inner * columns,
+    attended, received = [], [[] for _ in range(1, cores)]
+    for tile in range(tiles):
+        finish = functools.partial(
+            finish_kernel, sizes=sizes_of(group), carried=bool(state), cores=cores, tile=tile
+        )
+        attended.append(
+            call(finish, shape((rows, cells, LANES), bf16), flatten(group) + list(state), work(group) / tiles)
+        )
+        for k in range(1, cores):
+            received[k - 1].append(ring(attended[tile], "head", k))
+    kept = call(
+        local_kernel, shape((rows, cells, columns), f32), [w_parts[0]] + attended, 2 * rows * cells * inner * columns
     )
-
-    def output(k):
-        return call(
-            functools.partial(output_kernel, ahead=k, cores=cores),
-            shape((rows, cells, columns), f32),
-            [attended, w_out],
-            2 * rows * cells * inner * columns,
-        )
-
-    if cores == 1:
-        return sent
-    received = [ring(sent, "head")]
-    for k in range(2, cores):
-        received.append(ring(output(k).astype(bf16), "head", k))
-    result = output(0)
-    for value in received:
-        result = result + value.astype(f32)
-    return result.astype(bf16)
+    others = sum([[w] + group for w, group in zip(w_parts[1:], received)], [])
+    return pl.pallas_call(
+        functools.partial(output_kernel, tiles=tiles),
+        out_shape=pltpu.HBM((rows, cells, columns), bf16),
+        in_specs=whole(1 + len(others)),
+        out_specs=hbm,
+        scratch_shapes=[shape((rows, cells, columns), bf16), pltpu.SemaphoreType.DMA((rows,))],
+        compiler_params=pltpu.CompilerParams(vmem_limit_bytes=VMEM_LIMIT),
+    )(kept, *others)
 
 
 def groups_of(count):
@@ -554,4 +574,8 @@
     )
     out_specs = P(("grp", "seq"), "res", "head")
 
-    return jax.shard_map(shards, mesh=mesh, in_specs=in_specs, out_specs=out_specs, check_vma=False)
+    def placed(*args):
+        step = jax.shard_map(shards, mesh=mesh, in_specs=in_specs, out_specs=out_specs, check_vma=False)
+        return step(*args)
+
+    return placed

time: 82.8 us -> 90.1 us (1.088)
  waiting for transfers between devices: 45.9 us -> 55.4 us
  starting transfers between devices: 18.3 us -> 15.4 us
  Pallas kernels: 17.2 us -> 18.3 us
  other arithmetic: 0.93 us -> 0 us
    ppermute x23 -> x26, waiting for transfers between devices: 45.9 us -> 55.4 us  [ring(): lax.ppermute(value, axis, [(i, (i + by) % length) for i in range(length)])]
    ppermute x23 -> x26, starting transfers between devices: 18.3 us -> 15.4 us  [ring(): lax.ppermute(value, axis, [(i, (i + by) % length) for i in range(length)])]
    pallas_call x0 -> x1, Pallas kernels: none -> 1.24 us  [shards(): pl.pallas_call(functools.partial(output_kernel, tiles=tiles), out_shape=p...]
    convert_element_type x1 -> x0, other arithmetic: 0.93 us -> none  [shards(): return result.astype(bf16)]
    pallas_call x21 -> x24, Pallas kernels: 15 us -> 14.9 us  [call(): pl.pallas_call(kernel, out_shape=out_shape, in_specs=specs, out_specs=who...]
  transfers between devices with their start and end apart: 23 -> 26, of which waited for: 14 -> 13; matrix products, arithmetic and copies ran while one was open for 0% -> 0% of each run, Pallas kernels for 18% -> 18%
where the time goes in v7:
time: 90.1 us; the launch traced here: 89.5 us
  waiting for transfers between devices  55.4 us (61%)
  Pallas kernels  18.3 us (20%)
  starting transfers between devices  15.4 us (17%)
    ppermute x26, waiting for transfers between devices, ring(): lax.ppermute(value, axis, [(i, (i + by) % length) for i in range(length)])  55.4 us
    ppermute x26, starting transfers between devices, ring(): lax.ppermute(value, axis, [(i, (i + by) % length) for i in range(length)])  15.4 us
    pallas_call x24, Pallas kernels, call(): pl.pallas_call(kernel, out_shape=out_shape, in_specs=specs, out_specs=who...  14.9 us
    pallas_call x2, Pallas kernels, shards(): pl.pallas_call(functools.partial(pack_kernel, chunk=k, share=share), out_...  2.16 us
  transfers between devices with their start and end apart: 26, of which 13 were waited for; matrix products, arithmetic and copies ran while one was open for 0% of the time, Pallas kernels for 18%

profile of v7, /device:TPU:0, one launch (start us, length us, event | category | flops | bytes accessed | tf_op | source)
XLA Modules:
  0.0 89.5 jit_solution(11553081471012459487)
XLA Ops:
  0.0 1.1 %shard_map.73 = bf16[1160,128]{1,0:T(8,128)(2,1)S(1)} custom-call(bf16[6,128,768]{2,1,0:T(8,128)(2,1)} %tokens.3, s32[1,128]{1,0:T(1,128)} %bitcast.1), custom_call_target="tpu_custom_call" | custom-call | tf_op jit(solution)/shard_map/pallas_call | solution.py:383
  1.1 0.0 copy-start
  1.2 0.0 copy-start.1
  1.2 0.0 copy-start.4
  1.2 3.1 %collective-permute-start.1 = (bf16[1160,128]{1,0:T(8,128)(2,1)S(1)}, bf16[1160,128]{1,0:T(8,128)(2,1)S(1)}, u32[]{:S(2)}, u32[]{:S(2)}) collective-permute-start(bf16[1160,128]{1,0:T(8,128)(2,1)S(1)} %shard_map.73), channel_id=1, source_target_pairs={{0,4},{4,8},{8,12},{12,0},{1,5},{5,9},{9,13},{13,1},{2,6},{6,10},{... | collective-permute-start | bytes 890888 | tf_op jit(solution)/shard_map/ppermute | solution.py:25
  4.3 9.1 %collective-permute-done.1.refs_3_ = bf16[1160,128]{1,0:T(8,128)(2,1)S(1)} collective-permute-done((bf16[1160,128]{1,0:T(8,128)(2,1)S(1)}, bf16[1160,128]{1,0:T(8,128)(2,1)S(1)}, u32[]{:S(2)}, u32[]{:S(2)}) %collective-permute-start.1) | collective-permute-done | bytes 296992 | tf_op jit(solution)/shard_map/ppermute | solution.py:25
  13.4 1.0 %shard_map.76 = bf16[1152,128]{1,0:T(8,128)(2,1)S(1)} custom-call(bf16[6,128,768]{2,1,0:T(8,128)(2,1)} %tokens.3, s32[1,128]{1,0:T(1,128)} %bitcast.2), custom_call_target="tpu_custom_call" | custom-call | tf_op jit(solution)/shard_map/pallas_call | solution.py:383
  14.4 1.3 %collective-permute-start.4 = (bf16[1152,128]{1,0:T(8,128)(2,1)S(1)}, bf16[1152,128]{1,0:T(8,128)(2,1)S(1)}, u32[]{:S(2)}, u32[]{:S(2)}) collective-permute-start(bf16[1152,128]{1,0:T(8,128)(2,1)S(1)} %shard_map.76), channel_id=1, source_target_pairs={{0,4},{4,8},{8,12},{12,0},{1,5},{5,9},{9,13},{13,1},{2,6},{6,10},{... | collective-permute-start | bytes 884744 | tf_op jit(solution)/shard_map/ppermute | solution.py:25
  15.8 9.3 %collective-permute-done.2.marks.piece.refs_0_ = bf16[1160,128]{1,0:T(8,128)(2,1)S(1)} collective-permute-done((bf16[1160,128]{1,0:T(8,128)(2,1)S(1)}, bf16[1160,128]{1,0:T(8,128)(2,1)S(1)}, u32[]{:S(2)}, u32[]{:S(2)}) %collective-permute-start.2) | collective-permute-done | bytes 296992 | tf_op jit(solution)/shard_map/ppermute | solution.py:25
  25.1 6.3 %collective-permute-done.4.refs_5_ = bf16[1152,128]{1,0:T(8,128)(2,1)S(1)} collective-permute-done((bf16[1152,128]{1,0:T(8,128)(2,1)S(1)}, bf16[1152,128]{1,0:T(8,128)(2,1)S(1)}, u32[]{:S(2)}, u32[]{:S(2)}) %collective-permute-start.4) | collective-permute-done | bytes 294944 | tf_op jit(solution)/shard_map/ppermute | solution.py:25
  31.4 1.6 %collective-permute-start = (s32[6]{0:T(128)S(1)}, s32[6]{0:T(128)S(1)}, u32[]{:S(2)}, u32[]{:S(2)}) collective-permute-start(s32[6]{0:T(128)S(1)} %copy-done.6), channel_id=1, source_target_pairs={{0,2},{2,0},{1,3},{3,1},{4,6},{6,4},{5,7},{7,5},{8,10},{10,8},{9,1... | collective-permute-start | bytes 80 | tf_op jit(solution)/shard_map/ppermute | solution.py:25
  33.0 9.4 %collective-permute-done.5.packed.piece.refs_0_ = bf16[1152,128]{1,0:T(8,128)(2,1)S(1)} collective-permute-done((bf16[1152,128]{1,0:T(8,128)(2,1)S(1)}, bf16[1152,128]{1,0:T(8,128)(2,1)S(1)}, u32[]{:S(2)}, u32[]{:S(2)}) %collective-permute-start.5) | collective-permute-done | bytes 294944 | tf_op jit(solution)/shard_map/ppermute | solution.py:25
  42.4 0.1 collective-permute-start.9
  42.5 0.1 collective-permute-start.6
  42.6 0.1 collective-permute-start.12
  42.7 0.5 collective-permute-start.20
  43.2 0.1 collective-permute-start.14
  43.3 2.9 %shard_map.75 = (bf16[3,128,768]{2,1,0:T(8,128)(2,1)S(1)}, f32[2,3,128,128]{3,2,1,0:T(8,128)S(1)}, bf16[2,3,128,768]{3,2,1,0:T(8,128)(2,1)S(1)}) custom-call(s32[6]{0:T(128)S(1)} %copy-done.6, s32[6]{0:T(128)S(1)} %collective-permute-done.refs_1_, s32[1,128]{1,0:T(1,128)S(1)} %bitcast.3, bf16[6,128,768]{2,1,0:T(8,128)(2,1)S(1)} %copy-done.2, ...), custom_call_target="tpu_custom_call" | custom-call | flops 1509949440 | bytes 2949680 | tf_op jit(solution)/shard_map/pallas_call | solution.py:36
  46.2 1.9 %shard_map.89 = (f32[2,3,128,128]{3,2,1,0:T(8,128)S(1)}, bf16[2,3,128,768]{3,2,1,0:T(8,128)(2,1)S(1)}) custom-call(bf16[3,128,768]{2,1,0:T(8,128)(2,1)S(1)} %get-tuple-element.32.query.refs_0_, bf16[768,384]{1,0:T(8,128)(2,1)S(1)} %copy-done, bf16[768,384]{1,0:T(8,128)(2,1)S(1)} %copy-done.1, bf16[1160,128]{1,0:T(8,128)(2,1)S(1)} %collective-permute-done.1.refs_3_, ...), custom_call_target="tpu_custom_call" | custom-call | flops 1056964608 | bytes 2953216 | tf_op jit(solution)/shard_map/pallas_call | solution.py:36
  48.1 1.9 %collective-permute-done.9.piece.refs_2_ = bf16[576,128]{1,0:T(8,128)(2,1)S(1)} collective-permute-done((bf16[576,128]{1,0:T(8,128)(2,1)S(1)}, bf16[576,128]{1,0:T(8,128)(2,1)S(1)}, u32[]{:S(2)}, u32[]{:S(2)}) %collective-permute-start.9) | collective-permute-done | bytes 147488 | tf_op jit(solution)/shard_map/ppermute | solution.py:25
  50.0 1.1 %collective-permute-start.16 = (f32[2,3,128,128]{3,2,1,0:T(8,128)S(1)}, f32[2,3,128,128]{3,2,1,0:T(8,128)S(1)}, u32[]{:S(2)}, u32[]{:S(2)}) collective-permute-start(f32[2,3,128,128]{3,2,1,0:T(8,128)S(1)} %get-tuple-element.36.refs_0_), channel_id=1, source_target_pairs={{0,2},{2,0},{1,3},{3,1},{4,6},{6,4},{5,7},{7,5},{8,10},{10,8},{9,1... | collective-permute-start | bytes 1179656 | tf_op jit(solution)/shard_map/ppermute | solution.py:25
  51.1 0.5 collective-permute-done.6.piece.refs_0_
  51.6 1.1 %collective-permute-start.19 = (f32[2,3,128,128]{3,2,1,0:T(8,128)S(1)}, f32[2,3,128,128]{3,2,1,0:T(8,128)S(1)}, u32[]{:S(2)}, u32[]{:S(2)}) collective-permute-start(f32[2,3,128,128]{3,2,1,0:T(8,128)S(1)} %get-tuple-element.38.refs_3_), channel_id=1, source_target_pairs={{0,2},{2,0},{1,3},{3,1},{4,6},{6,4},{5,7},{7,5},{8,10},{10,8},{9,1... | collective-permute-start | bytes 1179656 | tf_op jit(solution)/shard_map/ppermute | solution.py:25
  52.6 0.5 collective-permute-start.7
  53.2 0.6 shard_map.90.before
  53.7 0.6 shard_map.91.refs_6_
  54.3 1.0 %collective-permute-start.21 = (f32[1,3,128,128]{3,2,1,0:T(8,128)S(1)}, f32[1,3,128,128]{3,2,1,0:T(8,128)S(1)}, u32[]{:S(2)}, u32[]{:S(2)}) collective-permute-start(f32[1,3,128,128]{3,2,1,0:T(8,128)S(1)} %shard_map.91.refs_6_), channel_id=1, source_target_pairs={{0,2},{2,0},{1,3},{3,1},{4,6},{6,4},{5,7},{7,5},{8,10},{10,8},{9,1... | collective-permute-start | bytes 589832 | tf_op jit(solution)/shard_map/ppermute | solution.py:25
  55.3 0.6 shard_map.83.before
  55.9 0.6 shard_map.84.refs_0_
  56.5 0.6 shard_map.86.before
  57.0 0.0 copy-start.3
  57.1 0.6 shard_map.87.refs_3_
  57.6 1.1 %collective-permute-start.13 = (f32[1,3,128,128]{3,2,1,0:T(8,128)S(1)}, f32[1,3,128,128]{3,2,1,0:T(8,128)S(1)}, u32[]{:S(2)}, u32[]{:S(2)}) collective-permute-start(f32[1,3,128,128]{3,2,1,0:T(8,128)S(1)} %shard_map.84.refs_0_), channel_id=1, source_target_pairs={{0,2},{2,0},{1,3},{3,1},{4,6},{6,4},{5,7},{7,5},{8,10},{10,8},{9,1... | collective-permute-start | bytes 589832 | tf_op jit(solution)/shard_map/ppermute | solution.py:25
  58.8 1.0 %collective-permute-start.15 = (f32[1,3,128,128]{3,2,1,0:T(8,128)S(1)}, f32[1,3,128,128]{3,2,1,0:T(8,128)S(1)}, u32[]{:S(2)}, u32[]{:S(2)}) collective-permute-start(f32[1,3,128,128]{3,2,1,0:T(8,128)S(1)} %shard_map.87.refs_3_), channel_id=1, source_target_pairs={{0,2},{2,0},{1,3},{3,1},{4,6},{6,4},{5,7},{7,5},{8,10},{10,8},{9,1... | collective-permute-start | bytes 589832 | tf_op jit(solution)/shard_map/ppermute | solution.py:25
  59.7 0.1 shard_map.74
  59.8 0.5 shard_map.80.before
  60.3 0.5 shard_map.78.before
  60.8 0.5 shard_map.85.refs_2_
  61.2 0.5 shard_map.82.refs_4_
  61.7 0.5 shard_map.81.refs_2_
  62.2 0.5 shard_map.79.refs_0_
  62.7 0.1 collective-permute-start.22
  62.8 7.6 %collective-permute-done.19.refs_4_ = f32[2,3,128,128]{3,2,1,0:T(8,128)S(1)} collective-permute-done((f32[2,3,128,128]{3,2,1,0:T(8,128)S(1)}, f32[2,3,128,128]{3,2,1,0:T(8,128)S(1)}, u32[]{:S(2)}, u32[]{:S(2)}) %collective-permute-start.19) | collective-permute-done | bytes 393248 | tf_op jit(solution)/shard_map/ppermute | solution.py:25
  70.4 1.1 %collective-permute-start.11 = (f32[3,64,128]{2,1,0:T(8,128)S(1)}, f32[3,64,128]{2,1,0:T(8,128)S(1)}, u32[]{:S(2)}, u32[]{:S(2)}) collective-permute-start(f32[3,64,128]{2,1,0:T(8,128)S(1)} %shard_map.81.refs_2_), channel_id=1, source_target_pairs={{0,2},{2,0},{1,3},{3,1},{4,6},{6,4},{5,7},{7,5},{8,10},{10,8},{9,1... | collective-permute-start | bytes 294920 | tf_op jit(solution)/shard_map/ppermute | solution.py:25
  71.5 3.2 %collective-permute-done.21.refs_7_ = f32[1,3,128,128]{3,2,1,0:T(8,128)S(1)} collective-permute-done((f32[1,3,128,128]{3,2,1,0:T(8,128)S(1)}, f32[1,3,128,128]{3,2,1,0:T(8,128)S(1)}, u32[]{:S(2)}, u32[]{:S(2)}) %collective-permute-start.21) | collective-permute-done | bytes 196640 | tf_op jit(solution)/shard_map/ppermute | solution.py:25
  74.6 1.1 %collective-permute-start.8 = (f32[3,64,128]{2,1,0:T(8,128)S(1)}, f32[3,64,128]{2,1,0:T(8,128)S(1)}, u32[]{:S(2)}, u32[]{:S(2)}) collective-permute-start(f32[3,64,128]{2,1,0:T(8,128)S(1)} %shard_map.79.refs_0_), channel_id=1, source_target_pairs={{0,2},{2,0},{1,3},{3,1},{4,6},{6,4},{5,7},{7,5},{8,10},{10,8},{9,1... | collective-permute-start | bytes 294920 | tf_op jit(solution)/shard_map/ppermute | solution.py:25
  75.7 0.5 shard_map.92.refs_8_
  76.2 0.7 shard_map.93
  76.9 0.5 shard_map.88.refs_5_
  77.4 1.4 %collective-permute-done.13.refs_1_ = f32[1,3,128,128]{3,2,1,0:T(8,128)S(1)} collective-permute-done((f32[1,3,128,128]{3,2,1,0:T(8,128)S(1)}, f32[1,3,128,128]{3,2,1,0:T(8,128)S(1)}, u32[]{:S(2)}, u32[]{:S(2)}) %collective-permute-start.13) | collective-permute-done | bytes 196640 | tf_op jit(solution)/shard_map/ppermute | solution.py:25
  78.8 4.0 %collective-permute-done.15.refs_4_ = f32[1,3,128,128]{3,2,1,0:T(8,128)S(1)} collective-permute-done((f32[1,3,128,128]{3,2,1,0:T(8,128)S(1)}, f32[1,3,128,128]{3,2,1,0:T(8,128)S(1)}, u32[]{:S(2)}, u32[]{:S(2)}) %collective-permute-start.15) | collective-permute-done | bytes 196640 | tf_op jit(solution)/shard_map/ppermute | solution.py:25
  82.9 0.4 shard_map.94
  83.3 0.6 collective-permute-done.11.refs_3_
  83.9 1.1 %collective-permute-done.8.refs_1_ = f32[3,64,128]{2,1,0:T(8,128)S(1)} collective-permute-done((f32[3,64,128]{2,1,0:T(8,128)S(1)}, f32[3,64,128]{2,1,0:T(8,128)S(1)}, u32[]{:S(2)}, u32[]{:S(2)}) %collective-permute-start.8) | collective-permute-done | bytes 98336 | tf_op jit(solution)/shard_map/ppermute | solution.py:25
  85.0 0.4 shard_map.97.refs_2_
  85.3 0.1 collective-permute-start.25
  85.4 0.4 shard_map.96.refs_1_
  85.8 0.6 collective-permute-start.24
  86.3 0.4 shard_map.95.refs_0_
  86.7 0.1 collective-permute-start.23
  86.8 0.5 shard_map.98.kept
  87.4 0.0 collective-permute-done.24.refs_2_
  87.4 0.8 collective-permute-done.23.refs_1_
  88.2 1.2 %shard_map.99 = bf16[6,128,384]{2,1,0:T(8,128)(2,1)} custom-call(f32[6,128,384]{2,1,0:T(8,128)S(1)} %shard_map.98.kept, bf16[384,384]{1,0:T(8,128)(2,1)S(1)} %collective-permute-done.22.refs_0_, bf16[6,128,128]{2,1,0:T(8,128)(2,1)S(1)} %collective-permute-done.23.refs_1_, bf16[6,128,128]{2,1,0:T(8,128)(2,1)S(1)} %collective-permute-done.24.refs_2_, ...), custom_call_target="tpu_custom_call" | custom-call | tf_op jit(solution)/shard_map/pallas_call | solution.py:551
  (29 shorter events, 0.1 us)
Async XLA Ops:
  0.0 31.4 %copy-start.6 = (s32[6]{0:T(128)S(1)}, s32[6]{0:T(128)}, u32[]{:S(2)}) copy-start(s32[6]{0:T(128)} %refs_0_.1) | copy-start | bytes 76
  0.0 43.2 %copy-start.2 = (bf16[6,128,768]{2,1,0:T(8,128)(2,1)S(1)}, bf16[6,128,768]{2,1,0:T(8,128)(2,1)}, u32[]{:S(2)}) copy-start(bf16[6,128,768]{2,1,0:T(8,128)(2,1)} %tokens.3) | copy-start | bytes 3538948
  1.1 42.1 %copy-start = (bf16[768,384]{1,0:T(8,128)(2,1)S(1)}, bf16[768,384]{1,0:T(8,128)(2,1)}, u32[]{:S(2)}) copy-start(bf16[768,384]{1,0:T(8,128)(2,1)} %w_key.9) | copy-start | bytes 1769476
  1.2 42.1 %copy-start.1 = (bf16[768,384]{1,0:T(8,128)(2,1)S(1)}, bf16[768,384]{1,0:T(8,128)(2,1)}, u32[]{:S(2)}) copy-start(bf16[768,384]{1,0:T(8,128)(2,1)} %w_value.3) | copy-start | bytes 1769476
  1.2 42.1 %copy-start.4 = (s32[128]{0:T(128)S(1)}, s32[128]{0:T(128)}, u32[]{:S(2)}) copy-start(s32[128]{0:T(128)} %param.9) | copy-start | bytes 1540
  1.2 42.1 %copy-start.5 = (bf16[768,384]{1,0:T(8,128)(2,1)S(1)}, bf16[768,384]{1,0:T(8,128)(2,1)}, u32[]{:S(2)}) copy-start(bf16[768,384]{1,0:T(8,128)(2,1)} %refs_4_) | copy-start | bytes 1769476
  1.2 12.2 %collective-permute-start.1 = (bf16[1160,128]{1,0:T(8,128)(2,1)S(1)}, bf16[1160,128]{1,0:T(8,128)(2,1)S(1)}, u32[]{:S(2)}, u32[]{:S(2)}) collective-permute-start(bf16[1160,128]{1,0:T(8,128)(2,1)S(1)} %shard_map.73), channel_id=1, source_target_pairs={{0,4},{4,8},{8,12},{12,0},{1,5},{5,9},{9,13},{13,1},{2,6},{6,10},{... | collective-permute-start | bytes 890888 | tf_op jit(solution)/shard_map/ppermute | solution.py:25
  13.4 11.7 %collective-permute-start.2 = (bf16[1160,128]{1,0:T(8,128)(2,1)S(1)}, bf16[1160,128]{1,0:T(8,128)(2,1)S(1)}, u32[]{:S(2)}, u32[]{:S(2)}) collective-permute-start(bf16[1160,128]{1,0:T(8,128)(2,1)S(1)} %collective-permute-done.1.refs_3_), channel_id=1, source_target_pairs={{0,4},{4,8},{8,12},{12,0},{1,5},{5,9},{9,13},{13,1},{2,6},{6,10},{... | collective-permute-start | bytes 890888 | tf_op jit(solution)/shard_map/ppermute | solution.py:25
  14.4 17.0 %collective-permute-start.4 = (bf16[1152,128]{1,0:T(8,128)(2,1)S(1)}, bf16[1152,128]{1,0:T(8,128)(2,1)S(1)}, u32[]{:S(2)}, u32[]{:S(2)}) collective-permute-start(bf16[1152,128]{1,0:T(8,128)(2,1)S(1)} %shard_map.76), channel_id=1, source_target_pairs={{0,4},{4,8},{8,12},{12,0},{1,5},{5,9},{9,13},{13,1},{2,6},{6,10},{... | collective-permute-start | bytes 884744 | tf_op jit(solution)/shard_map/ppermute | solution.py:25
  15.8 26.9 %collective-permute-start.17 = (bf16[1160,128]{1,0:T(8,128)(2,1)S(1)}, bf16[1160,128]{1,0:T(8,128)(2,1)S(1)}, u32[]{:S(2)}, u32[]{:S(2)}) collective-permute-start(bf16[1160,128]{1,0:T(8,128)(2,1)S(1)} %collective-permute-done.1.refs_3_), channel_id=1, source_target_pairs={{0,1},{1,0},{2,3},{3,2},{4,5},{5,4},{6,7},{7,6},{8,9},{9,8},{10,11... | collective-permute-start | bytes 890888 | tf_op jit(solution)/shard_map/ppermute | solution.py:25
  25.1 18.1 %collective-permute-start.3 = (bf16[1160,128]{1,0:T(8,128)(2,1)S(1)}, bf16[1160,128]{1,0:T(8,128)(2,1)S(1)}, u32[]{:S(2)}, u32[]{:S(2)}) collective-permute-start(bf16[1160,128]{1,0:T(8,128)(2,1)S(1)} %collective-permute-done.2.marks.piece.refs_0_), channel_id=1, source_target_pairs={{0,4},{4,8},{8,12},{12,0},{1,5},{5,9},{9,13},{13,1},{2,6},{6,10},{... | collective-permute-start | bytes 890888 | tf_op jit(solution)/shard_map/ppermute | solution.py:25
  31.4 11.0 %collective-permute-start.5 = (bf16[1152,128]{1,0:T(8,128)(2,1)S(1)}, bf16[1152,128]{1,0:T(8,128)(2,1)S(1)}, u32[]{:S(2)}, u32[]{:S(2)}) collective-permute-start(bf16[1152,128]{1,0:T(8,128)(2,1)S(1)} %collective-permute-done.4.refs_5_), channel_id=1, source_target_pairs={{0,4},{4,8},{8,12},{12,0},{1,5},{5,9},{9,13},{13,1},{2,6},{6,10},{... | collective-permute-start | bytes 884744 | tf_op jit(solution)/shard_map/ppermute | solution.py:25
  31.4 11.1 %collective-permute-start.18 = (bf16[1152,128]{1,0:T(8,128)(2,1)S(1)}, bf16[1152,128]{1,0:T(8,128)(2,1)S(1)}, u32[]{:S(2)}, u32[]{:S(2)}) collective-permute-start(bf16[1152,128]{1,0:T(8,128)(2,1)S(1)} %collective-permute-done.4.refs_5_), channel_id=1, source_target_pairs={{0,1},{1,0},{2,3},{3,2},{4,5},{5,4},{6,7},{7,6},{8,9},{9,8},{10,11... | collective-permute-start | bytes 884744 | tf_op jit(solution)/shard_map/ppermute | solution.py:25
  31.4 11.1 %collective-permute-start = (s32[6]{0:T(128)S(1)}, s32[6]{0:T(128)S(1)}, u32[]{:S(2)}, u32[]{:S(2)}) collective-permute-start(s32[6]{0:T(128)S(1)} %copy-done.6), channel_id=1, source_target_pairs={{0,2},{2,0},{1,3},{3,1},{4,6},{6,4},{5,7},{7,5},{8,10},{10,8},{9,1... | collective-permute-start | bytes 80 | tf_op jit(solution)/shard_map/ppermute | solution.py:25
  42.4 7.6 %collective-permute-start.9 = (bf16[576,128]{1,0:T(8,128)(2,1)S(1)}, bf16[576,128]{1,0:T(8,128)(2,1)S(1)}, u32[]{:S(2)}, u32[]{:S(2)}) collective-permute-start(bf16[576,128]{1,0:T(8,128)(2,1)S(1)} %get-tuple-element.35), channel_id=1, source_target_pairs={{0,4},{4,8},{8,12},{12,0},{1,5},{5,9},{9,13},{13,1},{2,6},{6,10},{... | collective-permute-start | bytes 442376 | tf_op jit(solution)/shard_map/ppermute | solution.py:25
  42.5 9.1 %collective-permute-start.6 = (bf16[576,128]{1,0:T(8,128)(2,1)S(1)}, bf16[576,128]{1,0:T(8,128)(2,1)S(1)}, u32[]{:S(2)}, u32[]{:S(2)}) collective-permute-start(bf16[576,128]{1,0:T(8,128)(2,1)S(1)} %get-tuple-element.34), channel_id=1, source_target_pairs={{0,4},{4,8},{8,12},{12,0},{1,5},{5,9},{9,13},{13,1},{2,6},{6,10},{... | collective-permute-start | bytes 442376 | tf_op jit(solution)/shard_map/ppermute | solution.py:25
  42.6 10.1 %collective-permute-start.12 = (bf16[1152,128]{1,0:T(8,128)(2,1)S(1)}, bf16[1152,128]{1,0:T(8,128)(2,1)S(1)}, u32[]{:S(2)}, u32[]{:S(2)}) collective-permute-start(bf16[1152,128]{1,0:T(8,128)(2,1)S(1)} %collective-permute-done.5.packed.piece.refs_0_), channel_id=1, source_target_pairs={{0,1},{1,0},{2,3},{3,2},{4,5},{5,4},{6,7},{7,6},{8,9},{9,8},{10,11... | collective-permute-start | bytes 884744 | tf_op jit(solution)/shard_map/ppermute | solution.py:25
  42.7 10.0 %collective-permute-start.20 = (bf16[1160,128]{1,0:T(8,128)(2,1)S(1)}, bf16[1160,128]{1,0:T(8,128)(2,1)S(1)}, u32[]{:S(2)}, u32[]{:S(2)}) collective-permute-start(bf16[1160,128]{1,0:T(8,128)(2,1)S(1)} %collective-permute-done.2.marks.piece.refs_0_), channel_id=1, source_target_pairs={{0,1},{1,0},{2,3},{3,2},{4,5},{5,4},{6,7},{7,6},{8,9},{9,8},{10,11... | collective-permute-start | bytes 890888 | tf_op jit(solution)/shard_map/ppermute | solution.py:25
  43.2 11.1 %collective-permute-start.14 = (bf16[1160,128]{1,0:T(8,128)(2,1)S(1)}, bf16[1160,128]{1,0:T(8,128)(2,1)S(1)}, u32[]{:S(2)}, u32[]{:S(2)}) collective-permute-start(bf16[1160,128]{1,0:T(8,128)(2,1)S(1)} %collective-permute-done.3.marks.piece.refs_0_), channel_id=1, source_target_pairs={{0,1},{1,0},{2,3},{3,2},{4,5},{5,4},{6,7},{7,6},{8,9},{9,8},{10,11... | collective-permute-start | bytes 890888 | tf_op jit(solution)/shard_map/ppermute | solution.py:25
  50.0 12.7 %collective-permute-start.16 = (f32[2,3,128,128]{3,2,1,0:T(8,128)S(1)}, f32[2,3,128,128]{3,2,1,0:T(8,128)S(1)}, u32[]{:S(2)}, u32[]{:S(2)}) collective-permute-start(f32[2,3,128,128]{3,2,1,0:T(8,128)S(1)} %get-tuple-element.36.refs_0_), channel_id=1, source_target_pairs={{0,2},{2,0},{1,3},{3,1},{4,6},{6,4},{5,7},{7,5},{8,10},{10,8},{9,1... | collective-permute-start | bytes 1179656 | tf_op jit(solution)/shard_map/ppermute | solution.py:25
  51.6 18.8 %collective-permute-start.19 = (f32[2,3,128,128]{3,2,1,0:T(8,128)S(1)}, f32[2,3,128,128]{3,2,1,0:T(8,128)S(1)}, u32[]{:S(2)}, u32[]{:S(2)}) collective-permute-start(f32[2,3,128,128]{3,2,1,0:T(8,128)S(1)} %get-tuple-element.38.refs_3_), channel_id=1, source_target_pairs={{0,2},{2,0},{1,3},{3,1},{4,6},{6,4},{5,7},{7,5},{8,10},{10,8},{9,1... | collective-permute-start | bytes 1179656 | tf_op jit(solution)/shard_map/ppermute | solution.py:25
  52.6 5.0 %collective-permute-start.10 = (bf16[576,128]{1,0:T(8,128)(2,1)S(1)}, bf16[576,128]{1,0:T(8,128)(2,1)S(1)}, u32[]{:S(2)}, u32[]{:S(2)}) collective-permute-start(bf16[576,128]{1,0:T(8,128)(2,1)S(1)} %collective-permute-done.9.piece.refs_2_), channel_id=1, source_target_pairs={{0,1},{1,0},{2,3},{3,2},{4,5},{5,4},{6,7},{7,6},{8,9},{9,8},{10,11... | collective-permute-start | bytes 442376 | tf_op jit(solution)/shard_map/ppermute | solution.py:25
  52.6 6.1 %collective-permute-start.7 = (bf16[576,128]{1,0:T(8,128)(2,1)S(1)}, bf16[576,128]{1,0:T(8,128)(2,1)S(1)}, u32[]{:S(2)}, u32[]{:S(2)}) collective-permute-start(bf16[576,128]{1,0:T(8,128)(2,1)S(1)} %collective-permute-done.6.piece.refs_0_), channel_id=1, source_target_pairs={{0,1},{1,0},{2,3},{3,2},{4,5},{5,4},{6,7},{7,6},{8,9},{9,8},{10,11... | collective-permute-start | bytes 442376 | tf_op jit(solution)/shard_map/ppermute | solution.py:25
  54.3 20.3 %collective-permute-start.21 = (f32[1,3,128,128]{3,2,1,0:T(8,128)S(1)}, f32[1,3,128,128]{3,2,1,0:T(8,128)S(1)}, u32[]{:S(2)}, u32[]{:S(2)}) collective-permute-start(f32[1,3,128,128]{3,2,1,0:T(8,128)S(1)} %shard_map.91.refs_6_), channel_id=1, source_target_pairs={{0,2},{2,0},{1,3},{3,1},{4,6},{6,4},{5,7},{7,5},{8,10},{10,8},{9,1... | collective-permute-start | bytes 589832 | tf_op jit(solution)/shard_map/ppermute | solution.py:25
  57.0 2.7 %copy-start.3 = (bf16[384,768]{1,0:T(8,128)(2,1)S(1)}, bf16[384,768]{1,0:T(8,128)(2,1)}, u32[]{:S(2)}) copy-start(bf16[384,768]{1,0:T(8,128)(2,1)} %w_out) | copy-start | bytes 1769476
  57.6 21.2 %collective-permute-start.13 = (f32[1,3,128,128]{3,2,1,0:T(8,128)S(1)}, f32[1,3,128,128]{3,2,1,0:T(8,128)S(1)}, u32[]{:S(2)}, u32[]{:S(2)}) collective-permute-start(f32[1,3,128,128]{3,2,1,0:T(8,128)S(1)} %shard_map.84.refs_0_), channel_id=1, source_target_pairs={{0,2},{2,0},{1,3},{3,1},{4,6},{6,4},{5,7},{7,5},{8,10},{10,8},{9,1... | collective-permute-start | bytes 589832 | tf_op jit(solution)/shard_map/ppermute | solution.py:25
  58.8 24.1 %collective-permute-start.15 = (f32[1,3,128,128]{3,2,1,0:T(8,128)S(1)}, f32[1,3,128,128]{3,2,1,0:T(8,128)S(1)}, u32[]{:S(2)}, u32[]{:S(2)}) collective-permute-start(f32[1,3,128,128]{3,2,1,0:T(8,128)S(1)} %shard_map.87.refs_3_), channel_id=1, source_target_pairs={{0,2},{2,0},{1,3},{3,1},{4,6},{6,4},{5,7},{7,5},{8,10},{10,8},{9,1... | collective-permute-start | bytes 589832 | tf_op jit(solution)/shard_map/ppermute | solution.py:25
  62.7 24.6 %collective-permute-start.22 = (bf16[384,384]{1,0:T(8,128)(2,1)S(1)}, bf16[384,384]{1,0:T(8,128)(2,1)S(1)}, u32[]{:S(2)}, u32[]{:S(2)}) collective-permute-start(bf16[384,384]{1,0:T(8,128)(2,1)S(1)} %get-tuple-element.46), channel_id=1, source_target_pairs={{0,1},{1,0},{2,3},{3,2},{4,5},{5,4},{6,7},{7,6},{8,9},{9,8},{10,11... | collective-permute-start | bytes 884744 | tf_op jit(solution)/shard_map/ppermute | solution.py:25
  70.4 13.5 %collective-permute-start.11 = (f32[3,64,128]{2,1,0:T(8,128)S(1)}, f32[3,64,128]{2,1,0:T(8,128)S(1)}, u32[]{:S(2)}, u32[]{:S(2)}) collective-permute-start(f32[3,64,128]{2,1,0:T(8,128)S(1)} %shard_map.81.refs_2_), channel_id=1, source_target_pairs={{0,2},{2,0},{1,3},{3,1},{4,6},{6,4},{5,7},{7,5},{8,10},{10,8},{9,1... | collective-permute-start | bytes 294920 | tf_op jit(solution)/shard_map/ppermute | solution.py:25
  74.6 10.3 %collective-permute-start.8 = (f32[3,64,128]{2,1,0:T(8,128)S(1)}, f32[3,64,128]{2,1,0:T(8,128)S(1)}, u32[]{:S(2)}, u32[]{:S(2)}) collective-permute-start(f32[3,64,128]{2,1,0:T(8,128)S(1)} %shard_map.79.refs_0_), channel_id=1, source_target_pairs={{0,2},{2,0},{1,3},{3,1},{4,6},{6,4},{5,7},{7,5},{8,10},{10,8},{9,1... | collective-permute-start | bytes 294920 | tf_op jit(solution)/shard_map/ppermute | solution.py:25
  85.3 2.0 %collective-permute-start.25 = (bf16[6,128,128]{2,1,0:T(8,128)(2,1)S(1)}, bf16[6,128,128]{2,1,0:T(8,128)(2,1)S(1)}, u32[]{:S(2)}, u32[]{:S(2)}) collective-permute-start(bf16[6,128,128]{2,1,0:T(8,128)(2,1)S(1)} %shard_map.97.refs_2_), channel_id=1, source_target_pairs={{0,1},{1,0},{2,3},{3,2},{4,5},{5,4},{6,7},{7,6},{8,9},{9,8},{10,11... | collective-permute-start | bytes 589832 | tf_op jit(solution)/shard_map/ppermute | solution.py:25
  85.8 1.6 %collective-permute-start.24 = (bf16[6,128,128]{2,1,0:T(8,128)(2,1)S(1)}, bf16[6,128,128]{2,1,0:T(8,128)(2,1)S(1)}, u32[]{:S(2)}, u32[]{:S(2)}) collective-permute-start(bf16[6,128,128]{2,1,0:T(8,128)(2,1)S(1)} %shard_map.96.refs_1_), channel_id=1, source_target_pairs={{0,1},{1,0},{2,3},{3,2},{4,5},{5,4},{6,7},{7,6},{8,9},{9,8},{10,11... | collective-permute-start | bytes 589832 | tf_op jit(solution)/shard_map/ppermute | solution.py:25
  86.7 1.5 %collective-permute-start.23 = (bf16[6,128,128]{2,1,0:T(8,128)(2,1)S(1)}, bf16[6,128,128]{2,1,0:T(8,128)(2,1)S(1)}, u32[]{:S(2)}, u32[]{:S(2)}) collective-permute-start(bf16[6,128,128]{2,1,0:T(8,128)(2,1)S(1)} %shard_map.95.refs_0_), channel_id=1, source_target_pairs={{0,1},{1,0},{2,3},{3,2},{4,5},{5,4},{6,7},{7,6},{8,9},{9,8},{10,11... | collective-permute-start | bytes 589832 | tf_op jit(solution)/shard_map/ppermute | solution.py:25
